TPU v7x, 32 devices: a whole 2x2x4 slice. The times are simulated.
32 devices in a mesh: row: 8 (over z, y), col: 4 (over x, core).
Axes of the slice: x: 2, y: 2, z: 4, core: 2. Of those that a mesh axis runs over, the one named last changes fastest.
Arguments:
- weights: float32 [192, 16, 64, 64], P('row', 'col'), may hold values from 9.765625e-05 to 0.0029296875
- block_cols: int32 [192, 16], P('row'), may hold values from 0 to 191, as said below
- counts: int32 [192], P('row'), may hold values from 1 to 16, as said below
- near_null: float32 [192, 64], P('row'), may hold values from 0.5 to 2
- prior_ridge: float32 [192, 64], P('row'), may hold values from 0.1 to 1
Outputs:
- coarse_band: float32 [192, 128], P(('row', 'col'))
Inputs may be any that keep to these rules, and one draw needn't show every extreme that they name: `block_cols`: row i holds i in slot 0; its other slots hold distinct aggregates j with (j - i) modulo 192 between -21 and 21 and not 0; some row holds a neighbour at +21 and some at -21. Slots at or beyond a row's count are unused. `counts`: both ends are reached in every draw; the mean over the 24 rows of one index of row differs from index to index.
All inputs are finite; a program needn't handle non-finite values.
Results may differ from a plain program's by a relative error of at most 0.0003.
Values sent between devices are 32-bit elements; how exact they have to be, the bound alone decides.
No kernel may reach another device: no remote copies, remote signals or barrier semaphores. Data moves between devices by JAX's collectives and lax.ppermute only.
A program may use at most 64 MiB of HBM per device.

v0:
```python
import jax
import jax.numpy as jnp
from jax import lax
from jax.sharding import PartitionSpec as P

H = 21
BAND = 128


epsilon = 1e-06
relax_weight = 2.0 / 3.0


def with_halo(block, sides, width):
    for axis, dim in sides:
        count = lax.axis_size(axis)
        forward = [(i, i + 1) for i in range(count - 1)]
        forward.append((count - 1, 0))
        backward = [(target, source) for source, target in forward]
        low = lax.ppermute(
            lax.slice_in_dim(block, block.shape[dim] - width, None, axis=dim), axis, forward
        )
        high = lax.ppermute(lax.slice_in_dim(block, 0, width, axis=dim), axis, backward)
        block = jnp.concatenate([low, block, high], axis=dim)
    return block


def shifted_2(array, axis, by):
    devices = lax.axis_size(axis)
    return lax.ppermute(array, axis, [(i, (i + by) % devices) for i in range(devices)])


def band_form(tiles, tile_offsets):
    one_hot = (
        tile_offsets[..., None] + BAND // 2 == jnp.arange(BAND, dtype=jnp.int32)[None, None, :]
    ).astype(jnp.float32)
    return jnp.einsum("nkx,nkq->nxq", tiles, one_hot, precision=lax.Precision.HIGHEST)


def shift_table(amounts):
    band_pos = jnp.arange(BAND, dtype=jnp.int32)
    source = (band_pos[None, None, :] - amounts[:, None, None]) % BAND
    return (band_pos[None, :, None] == source).astype(jnp.float32)


def on_device(weights, block_cols, counts, near_null, prior_ridge):
    highest = lax.Precision.HIGHEST
    block_rows = weights.shape[0]
    slot_count = weights.shape[1]
    all_slots = block_cols.shape[1]
    total_blocks = block_rows * lax.axis_size("row")
    first_block = lax.axis_index("row") * block_rows
    column = lax.axis_index("col")
    local_rows = jnp.arange(block_rows, dtype=jnp.int32)
    offsets = (block_cols - (first_block + local_rows)[:, None] + H) % total_blocks - H
    mask_all = (jnp.arange(all_slots, dtype=jnp.int32)[None, :] < counts[:, None]).astype(
        jnp.float32
    )
    slot_start = column * slot_count
    mask_own = lax.dynamic_slice_in_dim(mask_all, slot_start, slot_count, 1)
    own_offsets = lax.dynamic_slice_in_dim(offsets, slot_start, slot_count, 1)
    slot_ids = slot_start + jnp.arange(slot_count, dtype=jnp.int32)
    degree_part = jnp.einsum("ikxy,ik->ix", weights, mask_own, precision=highest)
    degree = lax.psum(degree_part, "col") + prior_ridge
    unit_null = near_null / jnp.sqrt(
        jnp.sum(near_null * near_null, axis=1, keepdims=True) + epsilon
    )
    null_ext = with_halo(unit_null, (("row", 0),), H)
    targets = local_rows[:, None] + H + own_offsets
    near_rows = null_ext[targets]
    applied = jnp.einsum("ikxy,iky->ikx", weights, near_rows, precision=highest)
    own_term = (
        jnp.where(slot_ids == 0, 1.0 - relax_weight, 0.0).astype(jnp.float32)[None, :, None]
        * unit_null[:, None, :]
    )
    prolong = mask_own[:, :, None] * (own_term + relax_weight * applied / degree[:, None, :])
    part_band = band_form(prolong, own_offsets)
    whole_band = lax.psum(part_band, "col")
    ext_band = with_halo(whole_band, (("row", 0),), H)
    pick_hot = (
        offsets[..., None] + BAND // 2 == jnp.arange(BAND, dtype=jnp.int32)[None, None, :]
    ).astype(jnp.float32)
    full_slots = jnp.einsum("ixq,ikq->ikx", whole_band, pick_hot, precision=highest)
    own_band = ext_band[H : H + block_rows]
    summed = jnp.zeros(own_band.shape, jnp.float32)
    for slot_index in range(slot_count):
        picked = ext_band[targets[:, slot_index]]
        mover = shift_table(own_offsets[:, slot_index])
        rolled = jnp.einsum("iyp,ipq->iyq", picked, mover, precision=highest)
        step_term = jnp.einsum("ixy,iyq->ixq", weights[:, slot_index], rolled, precision=highest)
        summed = summed + mask_own[:, slot_index][:, None, None] * step_term
    applied_p = jnp.where(column == 0, degree[:, :, None] * own_band, 0.0) - summed
    contrib = jnp.einsum("ikx,ixq->ikq", full_slots, applied_p, precision=highest)
    pieces = []
    for slot_index in range(all_slots):
        mover = shift_table(-offsets[:, slot_index])
        pieces.append(jnp.einsum("ip,ipq->iq", contrib[:, slot_index], mover, precision=highest))
    shifted = jnp.stack(pieces, axis=1)
    destination = (local_rows[:, None] + H + offsets).reshape(-1)
    one_hot = (
        destination[:, None] == jnp.arange(block_rows + 2 * H, dtype=jnp.int32)[None, :]
    ).astype(jnp.float32)
    collected = jnp.einsum("nt,nq->tq", one_hot, shifted.reshape(-1, BAND), precision=highest)
    from_prev = shifted_2(collected[block_rows + H :], "row", 1)
    from_next = shifted_2(collected[:H], "row", -1)
    own_coarse = collected[H : block_rows + H]
    own_coarse = own_coarse.at[:H].add(from_prev)
    own_coarse = own_coarse.at[block_rows - H :].add(from_next)
    return lax.psum_scatter(own_coarse, "col", scatter_dimension=0, tiled=True)


def solution(mesh):
    placed = (P("row", "col", None, None), P("row", None), P("row"), P("row", None), P("row", None))
    return jax.shard_map(
        on_device, mesh=mesh, in_specs=placed, out_specs=P(("row", "col"), None), check_vma=False
    )
```

profile of v0, /device:TPU:0, one launch (start us, length us, event | category | flops | bytes accessed | tf_op | source)
XLA Modules:
  0.0 173.8 jit_solution(2995312101073054942)
XLA Ops:
  6.5 0.8 multiply_reduce_fusion
  8.2 3.0 %collective-permute-start = (f32[21,64]{1,0:T(8,128)S(1)}, f32[21,64]{1,0:T(8,128)S(1)}, u32[]{:S(2)}, u32[]{:S(2)}) collective-permute-start(f32[21,64]{1,0:T(8,128)S(1)} %get-tuple-element.39), channel_id=1, source_target_pairs={{0,4},{4,8},{8,12},{12,16},{16,20},{20,24},{24,28},{28,0},{1,5},{5... | collective-permute-start | bytes 16136 | tf_op jit(solution)/shard_map/ppermute | solution.py:20
  11.2 3.1 %collective-permute-start.1 = (f32[21,64]{1,0:T(8,128)S(1)}, f32[21,64]{1,0:T(8,128)S(1)}, u32[]{:S(2)}, u32[]{:S(2)}) collective-permute-start(f32[21,64]{1,0:T(8,128)S(1)} %get-tuple-element.40), channel_id=1, source_target_pairs={{4,0},{8,4},{12,8},{16,12},{20,16},{24,20},{28,24},{0,28},{5,1},{9... | collective-permute-start | bytes 16136 | tf_op jit(solution)/shard_map/ppermute | solution.py:23
  21.9 2.9 %reduce_sum.19 = f32[24,4,64]{2,1,0:T(4,128)S(1)} reduce(f32[24,4,64,64]{3,2,1,0:T(8,128)} %param.9, f32[]{:T(128)} %constant.208.clone.1), dimensions={3}, to_apply=%region_1.2 | reduce | flops 387072 | bytes 1597444 | tf_op jit(solution)/shard_map/ikxy,ik->ix/reduce_sum | solution.py:63
  25.1 10.6 %psum.14 = f32[24,64]{1,0:T(8,128)S(1)} all-reduce(f32[24,64]{1,0:T(8,128)S(1)} %bitcast.240), channel_id=1, replica_groups=mesh['row'=8,'col'=4] {'col'}, use_global_device_ids=true, to_apply=%region_2.3 | all-reduce | flops 1536 | bytes 12288 | tf_op jit(solution)/shard_map/psum | solution.py:64
  36.4 5.0 %fusion.175 = f32[24,4,1,64]{3,2,1,0:T(1,128)S(1)} fusion(f32[24,4,64,1]{2,3,1,0:T(1,128)S(1)} %bitcast.239, f32[24,4,64,64]{3,2,1,0:T(8,128)S(1)} %copy-done), kind=kOutput, calls=%fused_computation.338 | convolution fusion | flops 4718592 | bytes 1622016 | tf_op jit(solution)/shard_map/ikxy,iky->ikx/dot_general | solution.py:71
  41.4 1.8 %fusion.57 = f32[24,64,128]{2,1,0:T(8,128)} fusion(f32[24,4,64]{2,1,0:T(4,128)S(1)} %bitcast.238, s32[24,4]{1,0:T(8,128)S(1)} %copy.19, f32[24,64]{1,0:T(8,128)S(1)} %add.346, f32[24,64]{1,0:T(8,128)S(1)} %broadcast_divide_fusion, f32[4]{0:T(128)S(1)} %copy-done.16, f32[24,4]{1,0:T(8,128)S(1)} %copy.17), kind=kOutput, calls=%fused_computation.90 | convolution fusion | flops 9480192 | bytes 824080 | tf_op jit(solution)/shard_map/nkx,nkq->nxq/dot_general | solution.py:37
  44.5 32.1 %all-reduce.3.cloned.1.call-done = f32[24,64,128]{2,1,0:T(8,128)} async-done(((f32[24,64,128]{2,1,0:T(8,128)}), f32[24,64,128]{2,1,0:T(8,128)}) %all-reduce.3.cloned.1.call-update) | async-done | bytes 786448 | tf_op jit(solution)/shard_map/psum | solution.py:78
  76.6 1.5 fusion.172
  78.1 1.5 collective-permute-start.2
  80.3 3.2 %collective-permute-start.3 = (f32[21,64,128]{2,1,0:T(8,128)S(1)}, f32[21,64,128]{2,1,0:T(8,128)S(1)}, u32[]{:S(2)}, u32[]{:S(2)}) collective-permute-start(f32[21,64,128]{2,1,0:T(8,128)S(1)} %get-tuple-element.35), channel_id=1, source_target_pairs={{4,0},{8,4},{12,8},{16,12},{20,16},{24,20},{28,24},{0,28},{5,1},{9... | collective-permute-start | bytes 2064392 | tf_op jit(solution)/shard_map/ppermute | solution.py:23
  84.9 23.1 %collective-permute-done.2 = f32[21,64,128]{2,1,0:T(8,128)S(1)} collective-permute-done((f32[21,64,128]{2,1,0:T(8,128)S(1)}, f32[21,64,128]{2,1,0:T(8,128)S(1)}, u32[]{:S(2)}, u32[]{:S(2)}) %collective-permute-start.2) | collective-permute-done | bytes 688160 | tf_op jit(solution)/shard_map/ppermute | solution.py:20
  107.9 0.9 constant_dynamic-update-slice_fusion.2
  108.8 1.0 constant_dynamic-update-slice_fusion.1
  109.8 1.0 collective-permute-done.3
  110.8 0.9 constant_dynamic-update-slice_fusion
  111.7 3.2 %gather_fusion.1 = f32[24,64,128]{2,1,0:T(8,128)} fusion(f32[66,64,128]{2,1,0:T(8,128)} %constant_dynamic-update-slice_fusion, s32[1024]{0:T(1024)} %pad_clamp_fusion.3), kind=kCustom, calls=%fused_computation.1 | custom fusion | bytes 1572960 | tf_op jit(solution)/shard_map/gather | solution.py:87
  114.9 3.2 %gather_fusion.2 = f32[24,64,128]{2,1,0:T(8,128)} fusion(f32[66,64,128]{2,1,0:T(8,128)} %constant_dynamic-update-slice_fusion, s32[1024]{0:T(1024)} %pad_clamp_fusion.2), kind=kCustom, calls=%fused_computation.2 | custom fusion | bytes 1572960 | tf_op jit(solution)/shard_map/gather | solution.py:87
  118.1 3.2 %gather_fusion.3 = f32[24,64,128]{2,1,0:T(8,128)} fusion(f32[66,64,128]{2,1,0:T(8,128)} %constant_dynamic-update-slice_fusion, s32[1024]{0:T(1024)} %pad_clamp_fusion.1), kind=kCustom, calls=%fused_computation.3 | custom fusion | bytes 1572960 | tf_op jit(solution)/shard_map/gather | solution.py:87
  121.4 3.2 %gather_fusion.4 = f32[24,64,128]{2,1,0:T(8,128)} fusion(f32[66,64,128]{2,1,0:T(8,128)} %constant_dynamic-update-slice_fusion, s32[1024]{0:T(1024)} %pad_clamp_fusion), kind=kCustom, calls=%fused_computation.4 | custom fusion | bytes 1572960 | tf_op jit(solution)/shard_map/gather | solution.py:87
  124.6 2.1 %fusion = f32[24,64,128]{2,1,0:T(8,128)S(1)} fusion(f32[24,64,128]{2,1,0:T(8,128)} %gather_fusion.1, s32[24,128]{1,0:T(8,128)S(1)} %add_select_fusion.19), kind=kOutput, calls=%fused_computation.25 | convolution fusion | flops 302383104 | bytes 1585152 | tf_op jit(solution)/shard_map/iyp,ipq->iyq/dot_general | solution.py:89
  126.7 0.9 convolution_multiply_fusion.3
  127.8 0.9 fusion.1
  128.7 0.9 fusion.2
  129.7 0.9 fusion.3
  130.6 0.9 fusion.24
  131.6 0.9 fusion.23
  132.7 1.0 fusion.22
  134.5 0.8 fusion.10
  135.3 0.8 fusion.11
  136.1 0.8 fusion.12
  136.9 1.0 fusion.13
  138.0 0.8 fusion.14
  138.8 0.8 fusion.15
  139.6 0.8 fusion.16
  140.4 0.8 fusion.17
  141.2 0.8 fusion.18
  142.1 0.8 fusion.19
  142.9 0.8 fusion.6
  143.7 0.8 fusion.7
  144.5 0.8 fusion.8
  145.3 0.8 fusion.9
  146.2 0.8 fusion.5
  147.0 0.8 fusion.4
  148.5 1.5 collective-permute-start.4
  151.3 3.3 %collective-permute-start.5 = (f32[21,128]{1,0:T(8,128)S(1)}, f32[21,128]{1,0:T(8,128)S(1)}, u32[]{:S(2)}, u32[]{:S(2)}) collective-permute-start(f32[21,128]{1,0:T(8,128)S(1)} %get-tuple-element.37), channel_id=1, source_target_pairs={{0,28},{4,0},{8,4},{12,8},{16,12},{20,16},{24,20},{28,24},{1,29},{... | collective-permute-start | bytes 32264 | tf_op jit(solution)/shard_map/ppermute | solution.py:30
  155.2 0.8 collective-permute-done.5
  156.2 10.1 %all-reduce = f32[24,128]{1,0:T(8,128)S(1)} all-reduce(f32[24,128]{1,0:T(8,128)S(1)} %scatter-add.9), channel_id=2, replica_groups=mesh['row'=8,'col'=4] {'col'}, use_global_device_ids=true, to_apply=%region_4.5.clone | all-reduce | flops 3072 | bytes 24576
  (104 shorter events, 16.6 us)
Async XLA Ops:
  6.5 70.1 %all-reduce.3.cloned.1.call-start = ((), (), s32[]{:S(2)}) async-start(), calls=%async_computation | async-start | bytes 1572864 | tf_op jit(solution)/shard_map/psum | solution.py:78
  8.2 27.5 %collective-permute-start = (f32[21,64]{1,0:T(8,128)S(1)}, f32[21,64]{1,0:T(8,128)S(1)}, u32[]{:S(2)}, u32[]{:S(2)}) collective-permute-start(f32[21,64]{1,0:T(8,128)S(1)} %get-tuple-element.39), channel_id=1, source_target_pairs={{0,4},{4,8},{8,12},{12,16},{16,20},{20,24},{24,28},{28,0},{1,5},{5... | collective-permute-start | bytes 16136 | tf_op jit(solution)/shard_map/ppermute | solution.py:20
  11.2 24.5 %collective-permute-start.1 = (f32[21,64]{1,0:T(8,128)S(1)}, f32[21,64]{1,0:T(8,128)S(1)}, u32[]{:S(2)}, u32[]{:S(2)}) collective-permute-start(f32[21,64]{1,0:T(8,128)S(1)} %get-tuple-element.40), channel_id=1, source_target_pairs={{4,0},{8,4},{12,8},{16,12},{20,16},{24,20},{28,24},{0,28},{5,1},{9... | collective-permute-start | bytes 16136 | tf_op jit(solution)/shard_map/ppermute | solution.py:23
  21.9 13.8 %copy-start.11 = (f32[24,64]{1,0:T(8,128)S(1)}, f32[24,64]{1,0:T(8,128)}, u32[]{:S(2)}) copy-start(f32[24,64]{1,0:T(8,128)} %param.13) | copy-start | bytes 18436
  21.9 14.4 %copy-start = (f32[24,4,64,64]{3,2,1,0:T(8,128)S(1)}, f32[24,4,64,64]{3,2,1,0:T(8,128)}, u32[]{:S(2)}) copy-start(f32[24,4,64,64]{3,2,1,0:T(8,128)} %param.9) | copy-start | bytes 4718596
  36.4 5.0 %copy-start.16 = (f32[4]{0:T(128)S(1)}, f32[4]{0:T(128)}, u32[]{:S(2)}) copy-start(f32[4]{0:T(128)} %compare_select_fusion.5) | copy-start | bytes 52
  76.6 7.5 %copy-start.1 = (f32[24,64,128]{2,1,0:T(8,128)S(1)}, f32[24,64,128]{2,1,0:T(8,128)}, u32[]{:S(2)}) copy-start(f32[24,64,128]{2,1,0:T(8,128)} %all-reduce.3.cloned.1.call-done) | copy-start | bytes 2359300
  78.1 29.9 %collective-permute-start.2 = (f32[21,64,128]{2,1,0:T(8,128)S(1)}, f32[21,64,128]{2,1,0:T(8,128)S(1)}, u32[]{:S(2)}, u32[]{:S(2)}) collective-permute-start(f32[21,64,128]{2,1,0:T(8,128)S(1)} %get-tuple-element.36), channel_id=1, source_target_pairs={{0,4},{4,8},{8,12},{12,16},{16,20},{20,24},{24,28},{28,0},{1,5},{5... | collective-permute-start | bytes 2064392 | tf_op jit(solution)/shard_map/ppermute | solution.py:20
  80.3 30.5 %collective-permute-start.3 = (f32[21,64,128]{2,1,0:T(8,128)S(1)}, f32[21,64,128]{2,1,0:T(8,128)S(1)}, u32[]{:S(2)}, u32[]{:S(2)}) collective-permute-start(f32[21,64,128]{2,1,0:T(8,128)S(1)} %get-tuple-element.35), channel_id=1, source_target_pairs={{4,0},{8,4},{12,8},{16,12},{20,16},{24,20},{28,24},{0,28},{5,1},{9... | collective-permute-start | bytes 2064392 | tf_op jit(solution)/shard_map/ppermute | solution.py:23
  121.4 5.3 %copy-start.13 = (f32[24]{0:T(128)S(1)}, f32[24]{0:T(128)}, u32[]{:S(2)}) copy-start(f32[24]{0:T(128)} %get-tuple-element.61) | copy-start | bytes 292
  126.7 1.1 copy-start.5
  126.7 2.1 %copy-start.4 = (f32[24,64,128]{2,1,0:T(8,128)S(1)}, f32[24,64,128]{2,1,0:T(8,128)}, u32[]{:S(2)}) copy-start(f32[24,64,128]{2,1,0:T(8,128)} %gather_fusion.3) | copy-start | bytes 2359300
  127.8 1.9 %copy-start.3 = (f32[24,64,128]{2,1,0:T(8,128)S(1)}, f32[24,64,128]{2,1,0:T(8,128)}, u32[]{:S(2)}) copy-start(f32[24,64,128]{2,1,0:T(8,128)} %gather_fusion.4) | copy-start | bytes 2359300
  128.7 1.9 %copy-start.15 = (f32[24]{0:T(128)S(1)}, f32[24]{0:T(128)}, u32[]{:S(2)}) copy-start(f32[24]{0:T(128)} %get-tuple-element.60) | copy-start | bytes 292
  130.6 0.9 copy-start.14
  131.5 1.1 copy-start.2
  131.6 1.1 copy-start.12
  138.8 4.9 %copy-start.6 = (s32[24,128]{1,0:T(8,128)S(1)}, s32[24,128]{1,0:T(8,128)}, u32[]{:S(2)}) copy-start(s32[24,128]{1,0:T(8,128)} %add_select_fusion.12) | copy-start | bytes 36868
  139.6 4.9 %copy-start.7 = (s32[24,128]{1,0:T(8,128)S(1)}, s32[24,128]{1,0:T(8,128)}, u32[]{:S(2)}) copy-start(s32[24,128]{1,0:T(8,128)} %add_select_fusion.11) | copy-start | bytes 36868
  140.4 4.9 %copy-start.8 = (s32[24,128]{1,0:T(8,128)S(1)}, s32[24,128]{1,0:T(8,128)}, u32[]{:S(2)}) copy-start(s32[24,128]{1,0:T(8,128)} %add_select_fusion.10) | copy-start | bytes 36868
  141.2 4.9 %copy-start.9 = (s32[24,128]{1,0:T(8,128)S(1)}, s32[24,128]{1,0:T(8,128)}, u32[]{:S(2)}) copy-start(s32[24,128]{1,0:T(8,128)} %add_select_fusion.14) | copy-start | bytes 36868
  142.1 4.9 %copy-start.10 = (s32[24,128]{1,0:T(8,128)S(1)}, s32[24,128]{1,0:T(8,128)}, u32[]{:S(2)}) copy-start(s32[24,128]{1,0:T(8,128)} %add_select_fusion.15) | copy-start | bytes 36868
  143.7 6.4 %copy-start.17 = (u32[32]{0:T(128)S(1)}, u32[32]{0:T(128)}, u32[]{:S(2)}) copy-start(u32[32]{0:T(128)} %constant.218) | copy-start | bytes 388
  148.5 6.4 %collective-permute-start.4 = (f32[21,128]{1,0:T(8,128)S(1)}, f32[21,128]{1,0:T(8,128)S(1)}, u32[]{:S(2)}, u32[]{:S(2)}) collective-permute-start(f32[21,128]{1,0:T(8,128)S(1)} %get-tuple-element.38), channel_id=1, source_target_pairs={{0,4},{4,8},{8,12},{12,16},{16,20},{20,24},{24,28},{28,0},{1,5},{5... | collective-permute-start | bytes 32264 | tf_op jit(solution)/shard_map/ppermute | solution.py:30
  151.3 4.7 %collective-permute-start.5 = (f32[21,128]{1,0:T(8,128)S(1)}, f32[21,128]{1,0:T(8,128)S(1)}, u32[]{:S(2)}, u32[]{:S(2)}) collective-permute-start(f32[21,128]{1,0:T(8,128)S(1)} %get-tuple-element.37), channel_id=1, source_target_pairs={{0,28},{4,0},{8,4},{12,8},{16,12},{20,16},{24,20},{28,24},{1,29},{... | collective-permute-start | bytes 32264 | tf_op jit(solution)/shard_map/ppermute | solution.py:30
Sparse Core Ops, SparseCore 0:
  43.3 33.2 all-reduce.2
where the time goes:
time: 174 us
  waiting for transfers between devices  57.4 us (33%)
  matrix products  30.7 us (18%)
  local copies, waits for them, and re-layouts  21.4 us (12%)
  blocking collectives  20.7 us (12%)
  starting transfers between devices  15.8 us (9%)
  between operations  14.4 us (8%)
  other arithmetic  13.5 us (8%)
    psum x1, waiting for transfers between devices, on_device(): whole_band = lax.psum(part_band, 'col')  32.1 us
    ppermute x2, waiting for transfers between devices, with_halo(): lax.ppermute(lax.slice_in_dim(block, block.shape[dim] - width, None, axis...  23.1 us
    dot_general x16, matrix products, on_device(): jnp.einsum('ip,ipq->iq', contrib[:, slot_index], mover, precision=highest)  13.2 us
    gather x4, local copies, waits for them, and re-layouts, on_device(): picked = ext_band[targets[:, slot_index]]  12.9 us
    psum x1, blocking collectives, on_device(): degree = lax.psum(degree_part, 'col') + prior_ridge  10.6 us
    unnamed x1, blocking collectives  10.1 us
    ppermute x2, starting transfers between devices, with_halo(): lax.ppermute(lax.slice_in_dim(block, 0, width, axis=dim), axis, backward)  6.35 us
    dot_general x1, matrix products, on_device(): applied = jnp.einsum('ikxy,iky->ikx', weights, near_rows, precision=highest)  4.97 us
  transfers between devices with their start and end apart: 7, of which 5 were waited for; matrix products, arithmetic and copies ran while one was open for 10% of the time, Pallas kernels for 0%

commit v1 on v0

v1 whole, which is shorter than its diff:
```python
import functools

import jax
import jax.numpy as jnp
from jax import lax
from jax.experimental import pallas as pl
from jax.experimental.pallas import tpu as pltpu
from jax.sharding import PartitionSpec as P

H = 21
BAND = 128
LANES = 128

epsilon = 1e-06
relax_weight = 2.0 / 3.0

NT = (((1,), (1,)), ((), ()))
NN = (((1,), (0,)), ((), ()))
TN = (((0,), (0,)), ((), ()))


def mxu(a, b, dims):
    return lax.dot_general(a, b, dims, preferred_element_type=jnp.float32)


def split(x):
    hi = x.astype(jnp.bfloat16)
    lo = (x - hi.astype(jnp.float32)).astype(jnp.bfloat16)
    return hi, lo


def lane_iota(shape):
    return lax.broadcasted_iota(jnp.int32, shape, len(shape) - 1)


def row_iota(shape):
    return lax.broadcasted_iota(jnp.int32, shape, 0)


def pack_kernel(scal, counts, w_ref, hi_ref, lo_ref):
    rows, slots, size, _ = w_ref.shape
    start = scal[0] * slots
    per = LANES // size
    for i in range(rows):
        for p in range(slots // per):
            tile = jnp.concatenate([w_ref[i, per * p + h] for h in range(per)], axis=1)
            slot = lane_iota((size, LANES)) // size + (start + per * p)
            tile = jnp.where(slot < counts[i], tile, 0.0)
            hi, lo = split(tile)
            hi_ref[i, :, p * LANES : (p + 1) * LANES] = hi
            lo_ref[i, :, p * LANES : (p + 1) * LANES] = lo


def unit_kernel(size, scal, offs, counts, prev_ref, own_ref, next_ref, ridge_ref, hi_ref, lo_ref,
                block_ref, unit_ref, acc_ref):
    rows = own_ref.shape[0]
    slots = hi_ref.shape[2] // size
    column = scal[0]
    lane = lane_iota((rows, LANES))
    for g, ref in enumerate((prev_ref, own_ref, next_ref)):
        x = jnp.where(lane < size, ref[...], 0.0)
        unit = x / jnp.sqrt(jnp.sum(x * x, axis=1, keepdims=True) + epsilon)
        unit_ref[g * rows : (g + 1) * rows, :] = unit + pltpu.roll(unit, size, 1)
    row8 = row_iota((8, LANES))
    half = lane_iota((8, LANES)) // size
    for i in range(rows):
        parts = []
        for p in range(slots // 2):
            tile = jnp.where(row8 == slots, 1.0, 0.0)
            for h in range(2):
                k = 2 * p + h
                t = rows + i + offs[i, column * slots + k]
                vec = jnp.broadcast_to(unit_ref[pl.ds(t, 1), :], (8, LANES))
                tile = jnp.where((row8 == k) & (half == h), vec, tile)
            parts.append(tile)
        lhs = jnp.concatenate(parts, axis=1)
        hi, lo = split(lhs)
        both = mxu(jnp.concatenate([hi, lo], axis=0), hi_ref[i], NT)
        low = mxu(hi, lo_ref[i], NT)
        acc_ref[8 * i : 8 * i + 8, :] = both[:8] + both[8:] + low
    plane = [acc_ref[pl.ds(k, rows, stride=8), :] for k in range(slots + 1)]
    for p in range(slots // 2):
        block_ref[p * rows : (p + 1) * rows, :] = jnp.concatenate(plane[2 * p : 2 * p + 2], axis=1)
    degree = plane[slots] + jnp.where(column == 0, ridge_ref[...], 0.0)
    block_ref[(slots // 2) * rows :, :] = jnp.concatenate([degree, jnp.zeros_like(degree)], axis=1)


def hot_kernel(size, slots, ncol, scal, prev_ref, own_ref, next_ref, hot_ref, tmp_ref):
    rows = own_ref.shape[0]
    column = scal[0]
    lane = lane_iota((rows, LANES))
    total = slots * ncol
    for g, ref in enumerate((prev_ref, own_ref, next_ref)):
        offsets = ref[...].astype(jnp.int32)
        bit = 1
        while bit < ncol:
            step = bit * slots
            swapped = jnp.where((lane // step) % 2 == 1, pltpu.roll(offsets, step, 1),
                                pltpu.roll(offsets, LANES - step, 1))
            offsets = jnp.where((column // bit) % 2 == 1, swapped, offsets)
            bit *= 2
        place = offsets + (row_iota((rows, LANES)) + (g + 1) * rows)
        for s in range(total):
            where = jnp.broadcast_to(place[:, size + s : size + s + 1], (rows, LANES))
            tmp_ref[pl.ds(g * rows * total + s, rows, stride=total), :] = jnp.where(
                where == lane, 1.0, 0.0)
    for j in range(3 * rows):
        hot_ref[j] = tmp_ref[j * total : (j + 1) * total, :].astype(jnp.bfloat16)


def coarse_kernel(size, ncol, scal, offs, *refs):
    blocks = refs[: 3 * ncol]
    unit_ref, hot_ref, hi_ref, lo_ref, out_ref, p_ref, ph_ref, pl_ref, r_ref, t_ref = refs[3 * ncol :]
    rows = hi_ref.shape[0]
    slots = hi_ref.shape[2] // size
    total = slots * ncol
    pairs = slots // 2
    column = scal[0]
    lane = lane_iota((rows, LANES))
    low_half = lane < size
    for g in range(3):
        degree = sum(blocks[g * ncol + d][pairs * rows :, :] for d in range(ncol))
        inverse = relax_weight / jnp.where(low_half, degree, 1.0)
        inverse = jnp.where(low_half, inverse, pltpu.roll(inverse, size, 1))
        own_term = jnp.where(low_half, (1.0 - relax_weight) * unit_ref[g * rows : (g + 1) * rows, :], 0.0)
        for d in range(ncol):
            for p in range(pairs):
                v = blocks[g * ncol + d][p * rows : (p + 1) * rows, :] * inverse
                if p == 0:
                    v = v + jnp.where(column == d, own_term, 0.0)
                w = pltpu.roll(v, size, 1)
                base = g * rows * total + d * slots + 2 * p
                p_ref[pl.ds(base, rows, stride=total), :] = jnp.where(low_half, v, w)
                p_ref[pl.ds(base + 1, rows, stride=total), :] = jnp.where(low_half, w, v)
    for j in range(3 * rows):
        hi, lo = split(p_ref[j * total : (j + 1) * total, :])
        ph_ref[j] = hi
        pl_ref[j] = lo
    tile_half = lane_iota((total, LANES)) // size
    zero = jnp.zeros((total, LANES), jnp.bfloat16)
    targets = [[rows + i + offs[i, column * slots + k] for k in range(slots)] for i in range(rows)]
    for i in range(rows):
        for p in range(pairs):
            his, los = [], []
            for h in range(2):
                t = targets[i][2 * p + h]
                his.append(jnp.where(tile_half == h, ph_ref[t], zero))
                los.append(jnp.where(tile_half == h, pl_ref[t], zero))
            lanes = slice(p * LANES, (p + 1) * LANES)
            high = jnp.concatenate(his, axis=0)
            both = mxu(jnp.concatenate([high] + los, axis=0), hi_ref[i, :, lanes], NT)
            rest = mxu(high, lo_ref[i, :, lanes], NT)
            r_ref[i, 2 * p * total : 2 * (p + 1) * total, :] = -(
                both[: 2 * total] + both[2 * total :] + rest)
    own_degree = blocks[ncol][pairs * rows :, :]
    for i in range(rows):
        j = rows + i
        diagonal = p_ref[j * total : (j + 1) * total, :size] * own_degree[i : i + 1, :size]
        r = jnp.concatenate([r_ref[i], diagonal], axis=0)
        hi, lo = split(jnp.concatenate([r, r], axis=1))
        rhs = jnp.concatenate([hi, lo], axis=1)
        first = jnp.where(tile_half == 0, ph_ref[j], pl_ref[j])
        second = jnp.where(tile_half == 0, ph_ref[j], zero)
        s = mxu(jnp.concatenate([first, second], axis=1), rhs, NT)
        hi, lo = split(s)
        hot = jnp.concatenate([hot_ref[t] for t in targets[i]] + [hot_ref[j]], axis=0)
        both = mxu(jnp.concatenate([hi, lo], axis=0), hot, NN)
        t_ref[i * total : (i + 1) * total, :] = both[:total] + both[total:]
    hi, lo = split(t_ref[...])
    own_hot = hot_ref[rows : 2 * rows].reshape(rows * total, LANES)
    absolute = mxu(own_hot, hi, TN) + mxu(own_hot, lo, TN)
    amount = (BAND // 2 - row_iota((LANES, LANES))) % LANES
    bit = 1
    while bit < LANES:
        absolute = jnp.where((amount // bit) % 2 == 1, pltpu.roll(absolute, bit, 1), absolute)
        bit *= 2
    out_ref[...] = absolute[rows : 4 * rows]


SMEM = pl.BlockSpec(memory_space=pltpu.SMEM)
VMEM = pl.BlockSpec(memory_space=pltpu.VMEM)


def on_device(weights, block_cols, counts, near_null, prior_ridge):
    rows, slots, size, _ = weights.shape
    total = block_cols.shape[1]
    nrow, ncol = lax.axis_size("row"), lax.axis_size("col")
    all_rows = rows * nrow
    first = lax.axis_index("row") * rows
    column = lax.axis_index("col")
    scal = column.reshape(1).astype(jnp.int32)
    local = jnp.arange(rows, dtype=jnp.int32)
    offsets = (block_cols - (first + local)[:, None] + H) % all_rows - H
    f32, bf16 = jnp.float32, jnp.bfloat16

    def to_row(x, by):
        return lax.ppermute(x, "row", [(r, (r + by) % nrow) for r in range(nrow)])

    def to_col(x, d):
        return lax.ppermute(x, "col", [(c, c ^ d) for c in range(ncol)])

    own = jnp.concatenate(
        [near_null, offsets.astype(f32), jnp.zeros((rows, LANES - size - total), f32)], axis=1)
    prev, nxt = to_row(own, 1), to_row(own, -1)
    w_hi, w_lo = pl.pallas_call(
        pack_kernel,
        out_shape=[jax.ShapeDtypeStruct((rows, size, slots * size), bf16)] * 2,
        in_specs=[SMEM, SMEM, VMEM], out_specs=[VMEM] * 2, name="pack",
    )(scal, counts, weights)
    planes = (slots // 2 + 1) * rows
    block, unit = pl.pallas_call(
        functools.partial(unit_kernel, size),
        out_shape=[jax.ShapeDtypeStruct((planes, LANES), f32),
                   jax.ShapeDtypeStruct((3 * rows, LANES), f32)],
        in_specs=[SMEM] * 3 + [VMEM] * 6, out_specs=[VMEM] * 2,
        scratch_shapes=[pltpu.VMEM((8 * rows, size), f32)], name="unit",
    )(scal, offsets, counts, prev, own, nxt, prior_ridge, w_hi, w_lo)
    hot = pl.pallas_call(
        functools.partial(hot_kernel, size, slots, ncol),
        out_shape=jax.ShapeDtypeStruct((3 * rows, total, LANES), bf16),
        in_specs=[SMEM] + [VMEM] * 3, out_specs=VMEM,
        scratch_shapes=[pltpu.VMEM((3 * rows * total, LANES), f32)], name="hot",
    )(scal, prev, own, nxt)
    halo = jnp.stack([to_row(block, 1), block, to_row(block, -1)])
    gathered = [halo] + [to_col(halo, d) for d in range(1, ncol)]
    blocks = [gathered[d][g] for g in range(3) for d in range(ncol)]
    parts = pl.pallas_call(
        functools.partial(coarse_kernel, size, ncol),
        out_shape=jax.ShapeDtypeStruct((3 * rows, LANES), f32),
        in_specs=[SMEM] * 2 + [VMEM] * (3 * ncol + 4), out_specs=VMEM,
        scratch_shapes=[
            pltpu.VMEM((3 * rows * total, LANES), f32),
            pltpu.VMEM((3 * rows, total, LANES), bf16),
            pltpu.VMEM((3 * rows, total, LANES), bf16),
            pltpu.VMEM((rows, slots * total, size), f32),
            pltpu.VMEM((rows * total, LANES), f32),
        ], name="coarse",
    )(scal, offsets, *blocks, unit, hot, w_hi, w_lo)
    own_rows = parts[rows : 2 * rows] + to_row(parts[2 * rows :], 1) + to_row(parts[:rows], -1)
    share = rows // ncol
    mine = lax.dynamic_slice_in_dim(own_rows, column * share, share, 0)
    for d in range(1, ncol):
        mine = mine + to_col(lax.dynamic_slice_in_dim(own_rows, (column ^ d) * share, share, 0), d)
    return mine


def solution(mesh):
    placed = (P("row", "col", None, None), P("row", None), P("row"), P("row", None), P("row", None))
    return jax.shard_map(
        on_device, mesh=mesh, in_specs=placed, out_specs=P(("row", "col"), None), check_vma=False
    )
```

time: 174 us -> 53.5 us (0.31)
  waiting for transfers between devices: 57.4 us -> 9.31 us
  matrix products: 30.7 us -> 0 us
  blocking collectives: 20.7 us -> 0 us
  local copies, waits for them, and re-layouts: 21.4 us -> 4.13 us
  Pallas kernels: 0 us -> 16.1 us
  between operations: 14.4 us -> 0.06 us
  other arithmetic: 13.5 us -> 3.58 us
  starting transfers between devices: 15.8 us -> 19.7 us
    psum x1 -> x0, waiting for transfers between devices: 32.1 us -> none  [on_device(): whole_band = lax.psum(part_band, 'col')]
    dot_general x30 -> x0, matrix products: 30.7 us -> none  [the longest x16 13.2 us: on_device(): jnp.einsum('ip,ipq->iq', contrib[:, slot_index], mover, precision=highest)]
    pallas_call x0 -> x4, Pallas kernels: none -> 16.1 us  [the longest x1 7.67 us: on_device(): pl.pallas_call(functools.partial(coarse_kernel, size, ncol), out_shape=ja...]
    ppermute x6 -> x12, waiting for transfers between devices: 25.3 us -> 9.31 us  [the longest x6 5.49 us: to_col(): return lax.ppermute(x, 'col', [(c, c ^ d) for c in range(ncol)])]
    gather x5 -> x0, local copies, waits for them, and re-layouts: 13.5 us -> none  [the longest x4 12.9 us: on_device(): picked = ext_band[targets[:, slot_index]]]
    psum x1 -> x0, blocking collectives: 10.6 us -> none  [on_device(): degree = lax.psum(degree_part, 'col') + prior_ridge]
    unnamed x1 -> x0, blocking collectives: 10.1 us -> none
    select_n x23 -> x0, other arithmetic: 5.07 us -> none  [the longest x20 4.55 us: shift_table(): source = (band_pos[None, None, :] - amounts[:, None, None]) % BAND]
  transfers between devices with their start and end apart: 7 -> 12, of which waited for: 5 -> 6; matrix products, arithmetic and copies ran while one was open for 10% -> 2% of each run, Pallas kernels for 0% -> 11%
where the time goes in v1:
time: 53.5 us; the launch traced here: 52.9 us
  starting transfers between devices  19.7 us (37%)
  Pallas kernels  16.1 us (30%)
  waiting for transfers between devices  9.31 us (17%)
  local copies, waits for them, and re-layouts  4.13 us (8%)
  other arithmetic  3.58 us (7%)
    ppermute x6, starting transfers between devices, to_row(): return lax.ppermute(x, 'row', [(r, (r + by) % nrow) for r in range(nrow)])  15.5 us
    pallas_call x1, Pallas kernels, on_device(): pl.pallas_call(functools.partial(coarse_kernel, size, ncol), out_shape=ja...  7.67 us
    ppermute x6, waiting for transfers between devices, to_col(): return lax.ppermute(x, 'col', [(c, c ^ d) for c in range(ncol)])  5.49 us
    ppermute x6, starting transfers between devices, to_col(): return lax.ppermute(x, 'col', [(c, c ^ d) for c in range(ncol)])  4.12 us
    ppermute x6, waiting for transfers between devices, to_row(): return lax.ppermute(x, 'row', [(r, (r + by) % nrow) for r in range(nrow)])  3.82 us
    pallas_call x1, Pallas kernels, on_device(): pl.pallas_call(pack_kernel, out_shape=[jax.ShapeDtypeStruct((rows, size,...  3.54 us
    pallas_call x1, Pallas kernels, on_device(): pl.pallas_call(functools.partial(unit_kernel, size), out_shape=[jax.Shape...  2.84 us
    pallas_call x1, Pallas kernels, on_device(): pl.pallas_call(functools.partial(hot_kernel, size, slots, ncol), out_shap...  2.09 us
  transfers between devices with their start and end apart: 12, of which 6 were waited for; matrix products, arithmetic and copies ran while one was open for 2% of the time, Pallas kernels for 11%

profile of v1, /device:TPU:0, one launch (start us, length us, event | category | flops | bytes accessed | tf_op | source)
XLA Modules:
  0.0 52.9 jit_solution(16951839185676209135)
XLA Ops:
  0.0 0.8 %copy.6 = s32[24,16]{1,0:T(8,128)S(1)} copy(s32[24,16]{0,1:T(8,128)} %param.6) | data formatting | bytes 3072 | tf_op args[1]
  0.8 0.7 %fusion.2 = (f32[24,16]{1,0:T(8,128)S(1)}, s32[24,16]{1,0:T(8,128)}) fusion(s32[24,16]{1,0:T(8,128)S(1)} %copy.6, s32[24]{0:T(128)S(1)} %iota_add_fusion), kind=kLoop, calls=%fused_computation.21 | loop fusion | flops 3840 | bytes 4704 | tf_op jit(solution)/shard_map/convert_element_type | solution.py:203
  1.5 0.1 pad.5.clone
  1.5 0.8 %maximum_maximum_fusion.own_ref = f32[24,128]{1,0:T(8,128)S(1)} fusion(f32[24,16]{1,0:T(8,128)S(1)} %get-tuple-element.13, f32[24,64]{1,0:T(8,128)} %param.8, f32[128]{0:T(128)S(1)} %pad.5.clone), kind=kLoop, calls=%fused_computation.14 | loop fusion | flops 6144 | bytes 20480 | tf_op jit(solution)/shard_map/concatenate | solution.py:202
  2.3 0.0 copy-start.2
  2.3 3.0 %collective-permute-start = (f32[24,128]{1,0:T(8,128)S(1)}, f32[24,128]{1,0:T(8,128)S(1)}, u32[]{:S(2)}, u32[]{:S(2)}) collective-permute-start(f32[24,128]{1,0:T(8,128)S(1)} %maximum_maximum_fusion.own_ref), channel_id=1, source_target_pairs={{0,4},{4,8},{8,12},{12,16},{16,20},{20,24},{24,28},{28,0},{1,5},{5... | collective-permute-start | bytes 36872 | tf_op jit(solution)/shard_map/ppermute | solution.py:197
  5.3 3.1 %collective-permute-start.1 = (f32[24,128]{1,0:T(8,128)S(1)}, f32[24,128]{1,0:T(8,128)S(1)}, u32[]{:S(2)}, u32[]{:S(2)}) collective-permute-start(f32[24,128]{1,0:T(8,128)S(1)} %maximum_maximum_fusion.own_ref), channel_id=1, source_target_pairs={{0,28},{4,0},{8,4},{12,8},{16,12},{20,16},{24,20},{28,24},{1,29},{... | collective-permute-start | bytes 36872 | tf_op jit(solution)/shard_map/ppermute | solution.py:197
  8.4 3.5 %pack.1 = (bf16[24,64,256]{2,1,0:T(8,128)(2,1)}, bf16[24,64,256]{2,1,0:T(8,128)(2,1)}) custom-call(s32[1]{0:T(128)} %bitcast.scal, s32[24]{0:T(128)} %counts.3, f32[24,4,64,64]{3,2,1,0:T(8,128)} %w_ref.1), custom_call_target="tpu_custom_call" | custom-call | tf_op jit(solution)/shard_map/pack/pallas_call | solution.py:205
  12.0 0.0 collective-permute-done.prev_ref
  12.0 0.0 copy-start.3
  12.0 0.0 collective-permute-done.1.next_ref
  12.0 0.0 copy-start.4
  12.0 0.0 copy-done.2
  12.0 0.6 %copy-done.3 = f32[24,128]{1,0:T(8,128)} copy-done((f32[24,128]{1,0:T(8,128)}, f32[24,128]{1,0:T(8,128)S(1)}, u32[]{:S(2)}) %copy-start.3) | copy-done | bytes 12312
  12.6 0.0 copy-done.4
  12.6 2.8 %unit.1 = (f32[72,128]{1,0:T(8,128)}, f32[72,128]{1,0:T(8,128)}) custom-call(s32[1]{0:T(128)} %bitcast.scal, s32[24,16]{1,0:T(8,128)} %get-tuple-element.14.offs, s32[24]{0:T(128)} %counts.3, f32[24,128]{1,0:T(8,128)} %copy-done.3, f32[24,128]{1,0:T(8,128)} %copy-done.2, f32[24,128]{1,0:T(8,128)} %copy-done.4, f32[24,64]{1,0:T(8,128)} %ridge_ref.1, ...), custom_call_target="tpu_custom_call" | custom-call | tf_op jit(solution)/shard_map/unit/pallas_call | solution.py:211
  15.4 0.0 collective-permute-start.2
  15.4 4.7 %collective-permute-start.3 = (f32[72,128]{1,0:T(8,128)}, f32[72,128]{1,0:T(8,128)S(1)}, u32[]{:S(2)}, u32[]{:S(2)}) collective-permute-start(f32[72,128]{1,0:T(8,128)} %get-tuple-element.11.refs_4_), channel_id=1, source_target_pairs={{0,28},{4,0},{8,4},{12,8},{16,12},{20,16},{24,20},{28,24},{1,29},{... | collective-permute-start | bytes 110600 | tf_op jit(solution)/shard_map/ppermute | solution.py:197
  20.1 2.1 %collective-permute-done.2.refs_0_ = f32[72,128]{1,0:T(8,128)S(1)} collective-permute-done((f32[72,128]{1,0:T(8,128)}, f32[72,128]{1,0:T(8,128)S(1)}, u32[]{:S(2)}, u32[]{:S(2)}) %collective-permute-start.2) | collective-permute-done | bytes 36896 | tf_op jit(solution)/shard_map/ppermute | solution.py:197
  22.3 0.0 copy-start
  22.3 0.0 collective-permute-done.3.refs_8_
  22.3 0.8 %pad_maximum_fusion = f32[3,72,128]{2,1,0:T(8,128)S(1)} fusion(f32[1,72,128]{2,1,0:T(8,128)S(1)} %bitcast.24, f32[1,72,128]{2,1,0:T(8,128)} %bitcast.22, f32[1,72,128]{2,1,0:T(8,128)S(1)} %bitcast.23), kind=kLoop, calls=%fused_computation | loop fusion | flops 55296 | bytes 221184 | tf_op jit(solution)/shard_map/stack | solution.py:224
  23.1 0.1 collective-permute-start.6
  23.2 2.1 %hot.1.refs_13_ = bf16[72,16,128]{2,1,0:T(8,128)(2,1)} custom-call(s32[1]{0:T(128)} %bitcast.scal, f32[24,128]{1,0:T(8,128)} %copy-done.3, f32[24,128]{1,0:T(8,128)} %copy-done.2, f32[24,128]{1,0:T(8,128)} %copy-done.4), custom_call_target="tpu_custom_call" | custom-call | tf_op jit(solution)/shard_map/hot/pallas_call | solution.py:218
  25.2 1.6 %collective-permute-start.5 = (f32[3,72,128]{2,1,0:T(8,128)S(1)}, f32[3,72,128]{2,1,0:T(8,128)S(1)}, u32[]{:S(2)}, u32[]{:S(2)}) collective-permute-start(f32[3,72,128]{2,1,0:T(8,128)S(1)} %pad_maximum_fusion), channel_id=1, source_target_pairs={{0,2},{1,3},{2,0},{3,1},{4,6},{5,7},{6,4},{7,5},{8,10},{9,11},{10,... | collective-permute-start | bytes 331784 | tf_op jit(solution)/shard_map/ppermute | solution.py:200
  26.8 0.3 collective-permute-start.4
  27.1 1.3 %collective-permute-done.6 = f32[3,72,128]{2,1,0:T(8,128)S(1)} collective-permute-done((f32[3,72,128]{2,1,0:T(8,128)S(1)}, f32[3,72,128]{2,1,0:T(8,128)S(1)}, u32[]{:S(2)}, u32[]{:S(2)}) %collective-permute-start.6) | collective-permute-done | bytes 110624 | tf_op jit(solution)/shard_map/ppermute | solution.py:200
  28.4 0.7 %slice_bitcast_fusion = (f32[72,128]{1,0:T(8,128)}, f32[72,128]{1,0:T(8,128)}, f32[72,128]{1,0:T(8,128)}) fusion(f32[3,72,128]{2,1,0:T(8,128)S(1)} %collective-permute-done.6), kind=kLoop, calls=%fused_computation.1 | loop fusion | bytes 221184 | tf_op jit(solution)/shard_map/squeeze | solution.py:226
  29.0 1.4 %collective-permute-done.5 = f32[3,72,128]{2,1,0:T(8,128)S(1)} collective-permute-done((f32[3,72,128]{2,1,0:T(8,128)S(1)}, f32[3,72,128]{2,1,0:T(8,128)S(1)}, u32[]{:S(2)}, u32[]{:S(2)}) %collective-permute-start.5) | collective-permute-done | bytes 110624 | tf_op jit(solution)/shard_map/ppermute | solution.py:200
  30.5 0.6 %slice_bitcast_fusion.1 = (f32[72,128]{1,0:T(8,128)}, f32[72,128]{1,0:T(8,128)}, f32[72,128]{1,0:T(8,128)}) fusion(f32[3,72,128]{2,1,0:T(8,128)S(1)} %collective-permute-done.5), kind=kLoop, calls=%fused_computation.2 | loop fusion | bytes 221184 | tf_op jit(solution)/shard_map/squeeze | solution.py:226
  31.1 0.0 collective-permute-done.4
  31.1 0.7 %slice_bitcast_fusion.2 = (f32[72,128]{1,0:T(8,128)}, f32[72,128]{1,0:T(8,128)}, f32[72,128]{1,0:T(8,128)}) fusion(f32[3,72,128]{2,1,0:T(8,128)S(1)} %collective-permute-done.4), kind=kLoop, calls=%fused_computation.3 | loop fusion | bytes 221184 | tf_op jit(solution)/shard_map/squeeze | solution.py:226
  31.8 0.0 copy-done
  31.8 0.0 copy-done.1
  31.8 7.7 %coarse.1 = f32[72,128]{1,0:T(8,128)} custom-call(s32[1]{0:T(128)} %bitcast.scal, s32[24,16]{1,0:T(8,128)} %get-tuple-element.14.offs, f32[72,128]{1,0:T(8,128)} %copy-done, f32[72,128]{1,0:T(8,128)} %get-tuple-element.23.refs_1_, f32[72,128]{1,0:T(8,128)} %get-tuple-element.20.refs_2_, f32[72,128]{1,0:T(8,128)} %get-tuple-element.17.refs_3_, ...), custom_call_target="tpu_custom_call" | custom-call | tf_op jit(solution)/shard_map/coarse/pallas_call | solution.py:227
  39.4 0.7 %fusion.4 = (f32[24,128]{1,0:T(8,128)S(1)}, f32[24,128]{1,0:T(8,128)S(1)}) fusion(f32[72,128]{1,0:T(8,128)} %coarse.1), kind=kLoop, calls=%fused_computation.22 | loop fusion | bytes 49152 | tf_op jit(solution)/shard_map/slice | solution.py:239
  40.2 0.0 collective-permute-start.7
  40.2 4.7 %collective-permute-start.8 = (f32[24,128]{1,0:T(8,128)S(1)}, f32[24,128]{1,0:T(8,128)S(1)}, u32[]{:S(2)}, u32[]{:S(2)}) collective-permute-start(f32[24,128]{1,0:T(8,128)S(1)} %get-tuple-element.25), channel_id=1, source_target_pairs={{0,28},{4,0},{8,4},{12,8},{16,12},{20,16},{24,20},{28,24},{1,29},{... | collective-permute-start | bytes 36872 | tf_op jit(solution)/shard_map/ppermute | solution.py:197
  44.9 1.7 %collective-permute-done.7 = f32[24,128]{1,0:T(8,128)S(1)} collective-permute-done((f32[24,128]{1,0:T(8,128)S(1)}, f32[24,128]{1,0:T(8,128)S(1)}, u32[]{:S(2)}, u32[]{:S(2)}) %collective-permute-start.7) | collective-permute-done | bytes 12320 | tf_op jit(solution)/shard_map/ppermute | solution.py:197
  46.6 0.0 collective-permute-done.8
  46.6 0.7 %fusion.1 = f32[24,128]{1,0:T(8,128)S(1)} fusion(f32[24,128]{1,0:T(8,128)S(1)} %collective-permute-done.8, f32[24,128]{1,0:T(8,128)S(1)} %collective-permute-done.7, f32[72,128]{1,0:T(8,128)} %coarse.1), kind=kLoop, calls=%fused_computation.13 | loop fusion | flops 6144 | bytes 49152 | tf_op jit(solution)/shard_map/add | solution.py:239
  47.3 1.9 %collective-permute-start.10 = (f32[6,128]{1,0:T(8,128)S(1)}, f32[6,128]{1,0:T(8,128)S(1)}, u32[]{:S(2)}, u32[]{:S(2)}) collective-permute-start(f32[6,128]{1,0:T(8,128)S(1)} %get-tuple-element.28), channel_id=1, source_target_pairs={{0,2},{1,3},{2,0},{3,1},{4,6},{5,7},{6,4},{7,5},{8,10},{9,11},{10,... | collective-permute-start | bytes 9224 | tf_op jit(solution)/shard_map/ppermute | solution.py:200
  49.2 0.0 collective-permute-start.11
  49.2 0.3 collective-permute-start.9
  49.5 1.5 %collective-permute-done.10 = f32[6,128]{1,0:T(8,128)S(1)} collective-permute-done((f32[6,128]{1,0:T(8,128)S(1)}, f32[6,128]{1,0:T(8,128)S(1)}, u32[]{:S(2)}, u32[]{:S(2)}) %collective-permute-start.10) | collective-permute-done | bytes 3104 | tf_op jit(solution)/shard_map/ppermute | solution.py:200
  51.0 1.3 %collective-permute-done.11 = f32[6,128]{1,0:T(8,128)S(1)} collective-permute-done((f32[6,128]{1,0:T(8,128)S(1)}, f32[6,128]{1,0:T(8,128)S(1)}, u32[]{:S(2)}, u32[]{:S(2)}) %collective-permute-start.11) | collective-permute-done | bytes 3104 | tf_op jit(solution)/shard_map/ppermute | solution.py:200
  52.3 0.0 collective-permute-done.9
  52.3 0.6 %add_add_fusion = f32[6,128]{1,0:T(8,128)} fusion(f32[6,128]{1,0:T(8,128)S(1)} %collective-permute-done.11, f32[6,128]{1,0:T(8,128)S(1)} %collective-permute-done.10, f32[6,128]{1,0:T(8,128)S(1)} %collective-permute-done.9, f32[24,128]{1,0:T(8,128)S(1)} %fusion.1, s32[]{:T(128)S(6)} %select_n.20), kind=kLoop, calls=%fused_computation.16 | loop fusion | flops 2304 | bytes 15364 | tf_op jit(solution)/shard_map/add | solution.py:243
  (4 shorter events, 0.0 us)
Async XLA Ops:
  2.3 9.7 %copy-start.2 = (f32[24,128]{1,0:T(8,128)}, f32[24,128]{1,0:T(8,128)S(1)}, u32[]{:S(2)}) copy-start(f32[24,128]{1,0:T(8,128)S(1)} %maximum_maximum_fusion.own_ref) | copy-start | bytes 36868
  2.3 9.6 %collective-permute-start = (f32[24,128]{1,0:T(8,128)S(1)}, f32[24,128]{1,0:T(8,128)S(1)}, u32[]{:S(2)}, u32[]{:S(2)}) collective-permute-start(f32[24,128]{1,0:T(8,128)S(1)} %maximum_maximum_fusion.own_ref), channel_id=1, source_target_pairs={{0,4},{4,8},{8,12},{12,16},{16,20},{20,24},{24,28},{28,0},{1,5},{5... | collective-permute-start | bytes 36872 | tf_op jit(solution)/shard_map/ppermute | solution.py:197
  5.3 6.6 %collective-permute-start.1 = (f32[24,128]{1,0:T(8,128)S(1)}, f32[24,128]{1,0:T(8,128)S(1)}, u32[]{:S(2)}, u32[]{:S(2)}) collective-permute-start(f32[24,128]{1,0:T(8,128)S(1)} %maximum_maximum_fusion.own_ref), channel_id=1, source_target_pairs={{0,28},{4,0},{8,4},{12,8},{16,12},{20,16},{24,20},{28,24},{1,29},{... | collective-permute-start | bytes 36872 | tf_op jit(solution)/shard_map/ppermute | solution.py:197
  12.0 0.6 %copy-start.3 = (f32[24,128]{1,0:T(8,128)}, f32[24,128]{1,0:T(8,128)S(1)}, u32[]{:S(2)}) copy-start(f32[24,128]{1,0:T(8,128)S(1)} %collective-permute-done.prev_ref) | copy-start | bytes 36868
  12.0 0.6 %copy-start.4 = (f32[24,128]{1,0:T(8,128)}, f32[24,128]{1,0:T(8,128)S(1)}, u32[]{:S(2)}) copy-start(f32[24,128]{1,0:T(8,128)S(1)} %collective-permute-done.1.next_ref) | copy-start | bytes 36868
  15.4 6.9 %collective-permute-start.2 = (f32[72,128]{1,0:T(8,128)}, f32[72,128]{1,0:T(8,128)S(1)}, u32[]{:S(2)}, u32[]{:S(2)}) collective-permute-start(f32[72,128]{1,0:T(8,128)} %get-tuple-element.11.refs_4_), channel_id=1, source_target_pairs={{0,4},{4,8},{8,12},{12,16},{16,20},{20,24},{24,28},{28,0},{1,5},{5... | collective-permute-start | bytes 110600 | tf_op jit(solution)/shard_map/ppermute | solution.py:197
  15.4 6.9 %collective-permute-start.3 = (f32[72,128]{1,0:T(8,128)}, f32[72,128]{1,0:T(8,128)S(1)}, u32[]{:S(2)}, u32[]{:S(2)}) collective-permute-start(f32[72,128]{1,0:T(8,128)} %get-tuple-element.11.refs_4_), channel_id=1, source_target_pairs={{0,28},{4,0},{8,4},{12,8},{16,12},{20,16},{24,20},{28,24},{1,29},{... | collective-permute-start | bytes 110600 | tf_op jit(solution)/shard_map/ppermute | solution.py:197
  22.3 9.5 %copy-start = (f32[72,128]{1,0:T(8,128)}, f32[72,128]{1,0:T(8,128)S(1)}, u32[]{:S(2)}) copy-start(f32[72,128]{1,0:T(8,128)S(1)} %collective-permute-done.2.refs_0_) | copy-start | bytes 110596
  22.3 9.5 %copy-start.1 = (f32[72,128]{1,0:T(8,128)}, f32[72,128]{1,0:T(8,128)S(1)}, u32[]{:S(2)}) copy-start(f32[72,128]{1,0:T(8,128)S(1)} %collective-permute-done.3.refs_8_) | copy-start | bytes 110596
  23.1 5.3 %collective-permute-start.6 = (f32[3,72,128]{2,1,0:T(8,128)S(1)}, f32[3,72,128]{2,1,0:T(8,128)S(1)}, u32[]{:S(2)}, u32[]{:S(2)}) collective-permute-start(f32[3,72,128]{2,1,0:T(8,128)S(1)} %pad_maximum_fusion), channel_id=1, source_target_pairs={{0,3},{1,2},{2,1},{3,0},{4,7},{5,6},{6,5},{7,4},{8,11},{9,10},{10,... | collective-permute-start | bytes 331784 | tf_op jit(solution)/shard_map/ppermute | solution.py:200
  25.2 5.2 %collective-permute-start.5 = (f32[3,72,128]{2,1,0:T(8,128)S(1)}, f32[3,72,128]{2,1,0:T(8,128)S(1)}, u32[]{:S(2)}, u32[]{:S(2)}) collective-permute-start(f32[3,72,128]{2,1,0:T(8,128)S(1)} %pad_maximum_fusion), channel_id=1, source_target_pairs={{0,2},{1,3},{2,0},{3,1},{4,6},{5,7},{6,4},{7,5},{8,10},{9,11},{10,... | collective-permute-start | bytes 331784 | tf_op jit(solution)/shard_map/ppermute | solution.py:200
  26.8 4.3 %collective-permute-start.4 = (f32[3,72,128]{2,1,0:T(8,128)S(1)}, f32[3,72,128]{2,1,0:T(8,128)S(1)}, u32[]{:S(2)}, u32[]{:S(2)}) collective-permute-start(f32[3,72,128]{2,1,0:T(8,128)S(1)} %pad_maximum_fusion), channel_id=1, source_target_pairs={{0,1},{1,0},{2,3},{3,2},{4,5},{5,4},{6,7},{7,6},{8,9},{9,8},{10,11... | collective-permute-start | bytes 331784 | tf_op jit(solution)/shard_map/ppermute | solution.py:200
  40.2 6.4 %collective-permute-start.7 = (f32[24,128]{1,0:T(8,128)S(1)}, f32[24,128]{1,0:T(8,128)S(1)}, u32[]{:S(2)}, u32[]{:S(2)}) collective-permute-start(f32[24,128]{1,0:T(8,128)S(1)} %get-tuple-element.24), channel_id=1, source_target_pairs={{0,4},{4,8},{8,12},{12,16},{16,20},{20,24},{24,28},{28,0},{1,5},{5... | collective-permute-start | bytes 36872 | tf_op jit(solution)/shard_map/ppermute | solution.py:197
  40.2 6.4 %collective-permute-start.8 = (f32[24,128]{1,0:T(8,128)S(1)}, f32[24,128]{1,0:T(8,128)S(1)}, u32[]{:S(2)}, u32[]{:S(2)}) collective-permute-start(f32[24,128]{1,0:T(8,128)S(1)} %get-tuple-element.25), channel_id=1, source_target_pairs={{0,28},{4,0},{8,4},{12,8},{16,12},{20,16},{24,20},{28,24},{1,29},{... | collective-permute-start | bytes 36872 | tf_op jit(solution)/shard_map/ppermute | solution.py:197
  47.3 3.7 %collective-permute-start.10 = (f32[6,128]{1,0:T(8,128)S(1)}, f32[6,128]{1,0:T(8,128)S(1)}, u32[]{:S(2)}, u32[]{:S(2)}) collective-permute-start(f32[6,128]{1,0:T(8,128)S(1)} %get-tuple-element.28), channel_id=1, source_target_pairs={{0,2},{1,3},{2,0},{3,1},{4,6},{5,7},{6,4},{7,5},{8,10},{9,11},{10,... | collective-permute-start | bytes 9224 | tf_op jit(solution)/shard_map/ppermute | solution.py:200
  49.2 3.0 %collective-permute-start.11 = (f32[6,128]{1,0:T(8,128)S(1)}, f32[6,128]{1,0:T(8,128)S(1)}, u32[]{:S(2)}, u32[]{:S(2)}) collective-permute-start(f32[6,128]{1,0:T(8,128)S(1)} %get-tuple-element.27), channel_id=1, source_target_pairs={{0,3},{1,2},{2,1},{3,0},{4,7},{5,6},{6,5},{7,4},{8,11},{9,10},{10,... | collective-permute-start | bytes 9224 | tf_op jit(solution)/shard_map/ppermute | solution.py:200
  49.2 3.0 %collective-permute-start.9 = (f32[6,128]{1,0:T(8,128)S(1)}, f32[6,128]{1,0:T(8,128)S(1)}, u32[]{:S(2)}, u32[]{:S(2)}) collective-permute-start(f32[6,128]{1,0:T(8,128)S(1)} %get-tuple-element.26), channel_id=1, source_target_pairs={{0,1},{1,0},{2,3},{3,2},{4,5},{5,4},{6,7},{7,6},{8,9},{9,8},{10,11... | collective-permute-start | bytes 9224 | tf_op jit(solution)/shard_map/ppermute | solution.py:200

commit v2 on v1

v2 whole, which is shorter than its diff:
```python
import functools

import jax
import jax.numpy as jnp
from jax import lax
from jax.experimental import pallas as pl
from jax.experimental.pallas import tpu as pltpu
from jax.sharding import PartitionSpec as P


H = 21
BAND = 128
LANES = 128

epsilon = 1e-06
relax_weight = 2.0 / 3.0

NT = (((1,), (1,)), ((), ()))
NN = (((1,), (0,)), ((), ()))
TN = (((0,), (0,)), ((), ()))


def mxu(a, b, dims):
    return lax.dot_general(a, b, dims, preferred_element_type=jnp.float32)


def split(x):
    hi = x.astype(jnp.bfloat16)
    lo = (x - hi.astype(jnp.float32)).astype(jnp.bfloat16)
    return hi, lo


def lane_iota(shape):
    return lax.broadcasted_iota(jnp.int32, shape, len(shape) - 1)


def row_iota(shape):
    return lax.broadcasted_iota(jnp.int32, shape, 0)


def pack_kernel(place, counts, w_ref, hi_ref, lo_ref):
    rows, slots, size, _ = w_ref.shape
    start = place[1] * slots
    per = LANES // size
    for i in range(rows):
        for p in range(slots // per):
            tile = jnp.concatenate([w_ref[i, per * p + h] for h in range(per)], axis=1)
            slot = lane_iota((size, LANES)) // size + (start + per * p)
            tile = jnp.where(slot < counts[i], tile, 0.0)
            hi, lo = split(tile)
            hi_ref[i, :, p * LANES : (p + 1) * LANES] = hi
            lo_ref[i, :, p * LANES : (p + 1) * LANES] = lo


def wrap(x, count):
    x = jnp.where(x < 0, x + count, x)
    return jnp.where(x >= count, x - count, x)


def tile_targets(place, cols, rows, slots, all_rows):
    first, start = place[0] * rows, place[1] * slots
    return [
        [rows + i - H + wrap(cols[i, start + k] - (first + i) + H, all_rows) for k in range(slots)]
        for i in range(rows)
    ]


def unit_kernel(size, all_rows, place, cols, mine_ref, other_ref, own_ref, ridge_ref, hi_ref, lo_ref,
                block_ref, unit_ref, acc_ref):
    rows = own_ref.shape[0]
    slots = hi_ref.shape[2] // size
    column = place[1]
    even = column % 2 == 0
    prev = jnp.where(even, mine_ref[...], other_ref[...])
    after = jnp.where(even, other_ref[...], mine_ref[...])
    for g, x in enumerate((prev, own_ref[...], after)):
        unit = x / jnp.sqrt(jnp.sum(x * x, axis=1, keepdims=True) + epsilon)
        unit_ref[g * rows : (g + 1) * rows, :] = jnp.concatenate([unit, unit], axis=1)
    row8 = row_iota((8, LANES))
    half = lane_iota((8, LANES)) // size
    targets = tile_targets(place, cols, rows, slots, all_rows)
    for i in range(rows):
        parts = []
        for p in range(slots // 2):
            tile = jnp.where(row8 == slots, 1.0, 0.0)
            for h in range(2):
                k = 2 * p + h
                vec = jnp.broadcast_to(unit_ref[pl.ds(targets[i][k], 1), :], (8, LANES))
                tile = jnp.where((row8 == k) & (half == h), vec, tile)
            parts.append(tile)
        lhs = jnp.concatenate(parts, axis=1)
        hi, lo = split(lhs)
        both = mxu(jnp.concatenate([hi, lo], axis=0), hi_ref[i], NT)
        low = mxu(hi, lo_ref[i], NT)
        acc_ref[8 * i : 8 * i + 8, :] = both[:8] + both[8:] + low
    plane = [acc_ref[pl.ds(k, rows, stride=8), :] for k in range(slots + 1)]
    for p in range(slots // 2):
        block_ref[p * rows : (p + 1) * rows, :] = jnp.concatenate(plane[2 * p : 2 * p + 2], axis=1)
    degree = plane[slots] + jnp.where(column == 0, ridge_ref[...], 0.0)
    block_ref[(slots // 2) * rows :, :] = jnp.concatenate([degree, jnp.zeros_like(degree)], axis=1)


def hot_kernel(slots, all_rows, place, mine_ref, other_ref, own_ref, hot_ref, tmp_ref):
    rows, total = own_ref.shape
    column = place[1]
    even = column % 2 == 0
    prev = jnp.where(even, mine_ref[...], other_ref[...])
    after = jnp.where(even, other_ref[...], mine_ref[...])
    lane = lane_iota((rows, LANES))
    for g, cols in enumerate((prev, own_ref[...], after)):
        local = row_iota((rows, LANES)) + (g - 1) * rows
        cols = jnp.concatenate([cols, jnp.zeros((rows, LANES - total), jnp.int32)], axis=1)
        where = wrap(wrap(cols - place[0] * rows - local + H, all_rows), all_rows) - H + local + 2 * rows
        bit = slots
        while bit < total:
            swapped = jnp.where((lane // bit) % 2 == 1, pltpu.roll(where, bit, 1),
                                pltpu.roll(where, LANES - bit, 1))
            where = jnp.where((column * slots // bit) % 2 == 1, swapped, where)
            bit *= 2
        for s in range(total):
            spread = jnp.broadcast_to(where[:, s : s + 1], (rows, LANES))
            tmp_ref[pl.ds(g * rows * total + s, rows, stride=total), :] = jnp.where(
                spread == lane, 1.0, 0.0)
    for j in range(3 * rows):
        hot_ref[j] = tmp_ref[j * total : (j + 1) * total, :].astype(jnp.bfloat16)


def coarse_kernel(size, ncol, nrow, place, cols, own_ref, straight_ref, diagonal_ref, far_ref, last_ref,
                  unit_ref, hot_ref, hi_ref, lo_ref, out_ref, p_ref, ph_ref, pl_ref, r_ref, t_ref):
    rows = hi_ref.shape[0]
    slots = hi_ref.shape[2] // size
    total = slots * ncol
    pairs = slots // 2
    column = place[1]
    low_half = lane_iota((rows, LANES)) < size
    even = column % 2 == 0
    planes = (pairs + 1) * rows
    blocks = [
        [(straight_ref, 0), (straight_ref, 1), (diagonal_ref, 0), (diagonal_ref, 1)],
        [(own_ref, 0), (own_ref, 1), (far_ref, 0), (last_ref, 4)],
        [(last_ref, 1), (last_ref, 0), (last_ref, 3), (last_ref, 2)],
    ]

    def plane(part, d, p):
        ref, index = blocks[part][d]
        return ref[index * planes + p * rows : index * planes + (p + 1) * rows, :]

    groups = (jnp.where(even, 0, 2), 1, jnp.where(even, 2, 0))
    for part, group in enumerate(groups):
        degree = sum(plane(part, d, pairs) for d in range(ncol))
        inverse = relax_weight / jnp.where(low_half, degree, 1.0)
        inverse = jnp.where(low_half, inverse, pltpu.roll(inverse, size, 1))
        unit = unit_ref[pl.ds(pl.multiple_of(group * rows, 8), rows), :]
        own_term = jnp.where(low_half, (1.0 - relax_weight) * unit, 0.0)
        for d in range(ncol):
            for p in range(pairs):
                v = plane(part, d, p) * inverse
                if p == 0:
                    v = v + jnp.where(column == d, own_term, 0.0)
                w = pltpu.roll(v, size, 1)
                base = group * (rows * total) + (d * slots + 2 * p)
                p_ref[pl.ds(base, rows, stride=total), :] = jnp.where(low_half, v, w)
                p_ref[pl.ds(base + 1, rows, stride=total), :] = jnp.where(low_half, w, v)
    for j in range(3 * rows):
        hi, lo = split(p_ref[j * total : (j + 1) * total, :])
        ph_ref[j] = hi
        pl_ref[j] = lo
    tile_half = lane_iota((total, LANES)) // size
    zero = jnp.zeros((total, LANES), jnp.bfloat16)
    targets = tile_targets(place, cols, rows, slots, rows * nrow)
    for i in range(rows):
        for p in range(pairs):
            his, los = [], []
            for h in range(2):
                t = targets[i][2 * p + h]
                his.append(jnp.where(tile_half == h, ph_ref[t], zero))
                los.append(jnp.where(tile_half == h, pl_ref[t], zero))
            lanes = slice(p * LANES, (p + 1) * LANES)
            high = jnp.concatenate(his, axis=0)
            both = mxu(jnp.concatenate([high] + los, axis=0), hi_ref[i, :, lanes], NT)
            rest = mxu(high, lo_ref[i, :, lanes], NT)
            r_ref[i, 2 * p * total : 2 * (p + 1) * total, :] = -(
                both[: 2 * total] + both[2 * total :] + rest)
    own_degree = plane(1, 0, pairs)
    for i in range(rows):
        j = rows + i
        diagonal = p_ref[j * total : (j + 1) * total, :size] * own_degree[i : i + 1, :size]
        r = jnp.concatenate([r_ref[i], diagonal], axis=0)
        hi, lo = split(jnp.concatenate([r, r], axis=1))
        rhs = jnp.concatenate([hi, lo], axis=1)
        first = jnp.where(tile_half == 0, ph_ref[j], pl_ref[j])
        second = jnp.where(tile_half == 0, ph_ref[j], zero)
        s = mxu(jnp.concatenate([first, second], axis=1), rhs, NT)
        hi, lo = split(s)
        hot = jnp.concatenate([hot_ref[t] for t in targets[i]] + [hot_ref[j]], axis=0)
        both = mxu(jnp.concatenate([hi, lo], axis=0), hot, NN)
        t_ref[i * total : (i + 1) * total, :] = both[:total] + both[total:]
    hi, lo = split(t_ref[...])
    own_hot = hot_ref[rows : 2 * rows].reshape(rows * total, LANES)
    absolute = mxu(own_hot, hi, TN) + mxu(own_hot, lo, TN)
    amount = (BAND // 2 - row_iota((LANES, LANES))) % LANES
    bit = 1
    while bit < LANES:
        absolute = jnp.where((amount // bit) % 2 == 1, pltpu.roll(absolute, bit, 1), absolute)
        bit *= 2
    share = rows // ncol
    out_ref[...] = jnp.zeros_like(out_ref)
    for g in range(3):
        row = wrap(place[0] + (g - 1), nrow)
        for c in range(ncol):
            at = (g + 1) * rows + c * share
            out_ref[row * ncol + c] = absolute[at : at + share]


def sum_kernel(ncol, nrow, place, got_ref, out_ref):
    total = None
    for g in range(3):
        row = wrap(place[0] + (g - 1), nrow)
        for c in range(ncol):
            part = got_ref[row * ncol + c]
            total = part if total is None else total + part
    out_ref[...] = total


SMEM = pl.BlockSpec(memory_space=pltpu.SMEM)
VMEM = pl.BlockSpec(memory_space=pltpu.VMEM)
VMEM_LIMIT = 20 * 1024 * 1024


def on_device(weights, block_cols, counts, near_null, prior_ridge):
    rows, slots, size, _ = weights.shape
    total = block_cols.shape[1]
    nrow, ncol = lax.axis_size("row"), lax.axis_size("col")
    all_rows = rows * nrow
    f32, bf16 = jnp.float32, jnp.bfloat16
    place = jnp.stack([lax.axis_index("row"), lax.axis_index("col")]).astype(jnp.int32)

    def call(kernel, out_shape, smem, vmem, scratch, *operands):
        return pl.pallas_call(
            kernel, out_shape=out_shape, in_specs=[SMEM] * smem + [VMEM] * vmem,
            out_specs=jax.tree.map(lambda _: VMEM, out_shape), scratch_shapes=scratch,
            compiler_params=pltpu.CompilerParams(vmem_limit_bytes=VMEM_LIMIT),
        )(*operands)

    def send(x, to):
        pairs = []
        for r in range(nrow):
            for c in range(ncol):
                nr, nc = to(r, c)
                pairs.append((r * ncol + c, (nr % nrow) * ncol + nc))
        return lax.ppermute(x, ("row", "col"), pairs)

    def partner(x):
        return send(x, lambda r, c: (r, c ^ 1))

    def across(x):
        return send(x, lambda r, c: (r, c ^ 2))

    def outward(x, d=0):
        return send(x, lambda r, c: (r + (1 if c % 2 == 0 else -1), c ^ d))

    null_mine = outward(near_null)
    cols_mine = outward(block_cols)
    w_hi, w_lo = call(
        pack_kernel, [jax.ShapeDtypeStruct((rows, size, slots * size), bf16)] * 2, 2, 1, [],
        place, counts, weights)
    null_other = partner(null_mine)
    cols_other = partner(cols_mine)
    planes = (slots // 2 + 1) * rows
    block, unit = call(
        functools.partial(unit_kernel, size, all_rows),
        [jax.ShapeDtypeStruct((planes, LANES), f32), jax.ShapeDtypeStruct((3 * rows, LANES), f32)],
        2, 6, [pltpu.VMEM((8 * rows, size), f32)],
        place, block_cols, null_mine, null_other, near_null, prior_ridge, w_hi, w_lo)
    hot = call(
        functools.partial(hot_kernel, slots, all_rows),
        jax.ShapeDtypeStruct((3 * rows, total, LANES), bf16), 1, 3,
        [pltpu.VMEM((3 * rows * total, LANES), f32)],
        place, cols_mine, cols_other, block_cols)
    pair = partner(block)
    far = across(block)
    own = jnp.concatenate([block, pair])
    diagonal = outward(own, 2)
    straight = outward(own)
    last = partner(jnp.concatenate([straight, diagonal, far]))
    parts = call(
        functools.partial(coarse_kernel, size, ncol, nrow),
        jax.ShapeDtypeStruct((nrow * ncol, rows // ncol, LANES), f32), 2, 9,
        [
            pltpu.VMEM((3 * rows * total, LANES), f32),
            pltpu.VMEM((3 * rows, total, LANES), bf16),
            pltpu.VMEM((3 * rows, total, LANES), bf16),
            pltpu.VMEM((rows, slots * total, size), f32),
            pltpu.VMEM((rows * total, LANES), f32),
        ],
        place, block_cols, own, straight, diagonal, far, last, unit, hot, w_hi, w_lo)
    got = lax.all_to_all(parts, ("row", "col"), 0, 0)
    return call(
        functools.partial(sum_kernel, ncol, nrow), jax.ShapeDtypeStruct((rows // ncol, LANES), f32),
        1, 1, [], place, got)


def solution(mesh):
    placed = (P("row", "col", None, None), P("row", None), P("row"), P("row", None), P("row", None))

    return jax.shard_map(
        on_device, mesh=mesh, in_specs=placed, out_specs=P(("row", "col"), None), check_vma=False
    )
```

time: 53.5 us -> 51 us (0.953)
  starting transfers between devices: 19.7 us -> 6.46 us
  blocking collectives: 0 us -> 10.3 us
  waiting for transfers between devices: 9.31 us -> 19.6 us
  Pallas kernels: 16.1 us -> 11 us
  other arithmetic: 3.58 us -> 0.09 us
  local copies, waits for them, and re-layouts: 4.13 us -> 3.33 us
    ppermute x12 -> x9, starting transfers between devices: 19.7 us -> 6.46 us  [send(): return lax.ppermute(x, ('row', 'col'), pairs)]
    all_to_all x0 -> x1, blocking collectives: none -> 10.3 us  [on_device(): got = lax.all_to_all(parts, ('row', 'col'), 0, 0)]
    ppermute x12 -> x9, waiting for transfers between devices: 9.31 us -> 19.6 us  [send(): return lax.ppermute(x, ('row', 'col'), pairs)]
    pallas_call x4 -> x5, Pallas kernels: 16.1 us -> 11 us  [call(): pl.pallas_call(kernel, out_shape=out_shape, in_specs=[SMEM] * smem + [VME...]
    unnamed x11 -> x10, local copies, waits for them, and re-layouts: 1.36 us -> 3.32 us
    squeeze x3 -> x0, local copies, waits for them, and re-layouts: 1.96 us -> none  [on_device(): blocks = [gathered[d][g] for g in range(3) for d in range(ncol)]]
    add x3 -> x0, other arithmetic: 1.32 us -> none  [the longest x1 0.71 us: on_device(): parts[rows:2 * rows] + to_row(parts[2 * rows:], 1)]
    concatenate x1, other arithmetic: 0.78 us -> 0.01 us  [on_device(): last = partner(jnp.concatenate([straight, diagonal, far]))]
  transfers between devices with their start and end apart: 12 -> 9, of which waited for: 6 -> 7; matrix products, arithmetic and copies ran while one was open for 2% -> 2% of each run, Pallas kernels for 11% -> 4%
where the time goes in v2:
time: 51 us; the launch traced here: 50.8 us
  waiting for transfers between devices  19.6 us (38%)
  Pallas kernels  11 us (22%)
  blocking collectives  10.3 us (20%)
  starting transfers between devices  6.46 us (13%)
  local copies, waits for them, and re-layouts  3.33 us (7%)
    ppermute x9, waiting for transfers between devices, send(): return lax.ppermute(x, ('row', 'col'), pairs)  19.6 us
    pallas_call x5, Pallas kernels, call(): pl.pallas_call(kernel, out_shape=out_shape, in_specs=[SMEM] * smem + [VME...  11 us
    all_to_all x1, blocking collectives, on_device(): got = lax.all_to_all(parts, ('row', 'col'), 0, 0)  10.3 us
    ppermute x9, starting transfers between devices, send(): return lax.ppermute(x, ('row', 'col'), pairs)  6.46 us
    unnamed x10, local copies, waits for them, and re-layouts  3.32 us
  transfers between devices with their start and end apart: 9, of which 7 were waited for; matrix products, arithmetic and copies ran while one was open for 2% of the time, Pallas kernels for 4%

profile of v2, /device:TPU:0, one launch (start us, length us, event | category | flops | bytes accessed | tf_op | source)
XLA Modules:
  0.0 50.8 jit_solution(7417775861167882201)
XLA Ops:
  0.0 0.0 copy-start.1
  0.0 0.0 copy-start.2
  0.0 3.0 %collective-permute-start = (f32[24,64]{1,0:T(8,128)}, f32[24,64]{1,0:T(8,128)S(1)}, u32[]{:S(2)}, u32[]{:S(2)}) collective-permute-start(f32[24,64]{1,0:T(8,128)} %own_ref.2), channel_id=1, source_target_pairs={{0,4},{1,29},{2,6},{3,31},{4,8},{5,1},{6,10},{7,3},{8,12},{9,5},{1... | collective-permute-start | bytes 18440 | tf_op jit(solution)/shard_map/ppermute | solution.py:251
  3.0 5.0 %collective-permute-done.mine_ref = f32[24,64]{1,0:T(8,128)S(1)} collective-permute-done((f32[24,64]{1,0:T(8,128)}, f32[24,64]{1,0:T(8,128)S(1)}, u32[]{:S(2)}, u32[]{:S(2)}) %collective-permute-start) | collective-permute-done | bytes 6176 | tf_op jit(solution)/shard_map/ppermute | solution.py:251
  8.0 0.0 collective-permute-start.1
  8.0 0.1 pad_add_fusion.place
  8.1 0.8 %copy.9.cols.own_ref = s32[24,16]{1,0:T(8,128)S(1)} copy(s32[24,16]{0,1:T(8,128)} %param.6) | data formatting | bytes 3072 | tf_op args[1]
  8.8 0.0 copy-start
  8.8 1.9 %copy-done = f32[24,4,64,64]{3,2,1,0:T(8,128)S(1)} copy-done((f32[24,4,64,64]{3,2,1,0:T(8,128)S(1)}, f32[24,4,64,64]{3,2,1,0:T(8,128)}, u32[]{:S(2)}) %copy-start) | copy-done | bytes 1572888
  10.7 0.0 copy-start.3
  10.7 0.7 %copy-done.3 = s32[24]{0:T(128)S(1)} copy-done((s32[24]{0:T(128)S(1)}, s32[24]{0:T(128)}, u32[]{:S(2)}) %copy-start.3) | copy-done | bytes 120
  11.4 1.0 %shard_map.55 = (bf16[24,64,256]{2,1,0:T(8,128)(2,1)S(1)}, bf16[24,64,256]{2,1,0:T(8,128)(2,1)S(1)}) custom-call(s32[2]{0:T(128)S(1)} %pad_add_fusion.place, s32[24]{0:T(128)S(1)} %copy-done.3, f32[24,4,64,64]{3,2,1,0:T(8,128)S(1)} %copy-done), custom_call_target="tpu_custom_call" | custom-call | tf_op jit(solution)/shard_map/pallas_call | solution.py:239
  12.4 0.0 collective-permute-done.1.other_ref
  12.4 0.0 copy-done.1
  12.4 0.0 copy-done.2
  12.4 1.5 %shard_map.56 = (f32[72,128]{1,0:T(8,128)S(1)}, f32[72,128]{1,0:T(8,128)S(1)}) custom-call(s32[2]{0:T(128)S(1)} %pad_add_fusion.place, s32[24,16]{1,0:T(8,128)S(1)} %copy.9.cols.own_ref, f32[24,64]{1,0:T(8,128)S(1)} %collective-permute-done.mine_ref, f32[24,64]{1,0:T(8,128)S(1)} %collective-permute-done.1.other_ref, f32[24,64]{1,0:T(8,128)S(1)} %copy-done.1, ...), custom_call_target="tpu_custom_call" | custom-call | tf_op jit(solution)/shard_map/pallas_call | solution.py:239
  13.9 0.5 %collective-permute-start.2 = (f32[72,128]{1,0:T(8,128)S(1)}, f32[72,128]{1,0:T(8,128)S(1)}, u32[]{:S(2)}, u32[]{:S(2)}) collective-permute-start(f32[72,128]{1,0:T(8,128)S(1)} %get-tuple-element.11), channel_id=1, source_target_pairs={{0,1},{1,0},{2,3},{3,2},{4,5},{5,4},{6,7},{7,6},{8,9},{9,8},{10,11... | collective-permute-start | bytes 110600 | tf_op jit(solution)/shard_map/ppermute | solution.py:251
  14.5 0.9 %collective-permute-done.2 = f32[72,128]{1,0:T(8,128)S(1)} collective-permute-done((f32[72,128]{1,0:T(8,128)S(1)}, f32[72,128]{1,0:T(8,128)S(1)}, u32[]{:S(2)}, u32[]{:S(2)}) %collective-permute-start.2) | collective-permute-done | bytes 36896 | tf_op jit(solution)/shard_map/ppermute | solution.py:251
  15.3 0.0 collective-permute-start.3
  15.3 2.3 %collective-permute-start.4 = (f32[144,128]{1,0:T(8,128)S(1)}, f32[144,128]{1,0:T(8,128)S(1)}, u32[]{:S(2)}, u32[]{:S(2)}) collective-permute-start(f32[144,128]{1,0:T(8,128)S(1)} %constant_dynamic-update-slice_fusion.own_ref), channel_id=1, source_target_pairs={{0,6},{1,31},{2,4},{3,29},{4,10},{5,3},{6,8},{7,1},{8,14},{9,7},{1... | collective-permute-start | bytes 221192 | tf_op jit(solution)/shard_map/ppermute | solution.py:251
  17.6 0.5 %collective-permute-start.5 = (f32[72,128]{1,0:T(8,128)S(1)}, f32[72,128]{1,0:T(8,128)S(1)}, u32[]{:S(2)}, u32[]{:S(2)}) collective-permute-start(f32[72,128]{1,0:T(8,128)S(1)} %get-tuple-element.11), channel_id=1, source_target_pairs={{0,2},{1,3},{2,0},{3,1},{4,6},{5,7},{6,4},{7,5},{8,10},{9,11},{10,... | collective-permute-start | bytes 110600 | tf_op jit(solution)/shard_map/ppermute | solution.py:251
  18.1 3.5 %collective-permute-done.5.far_ref = f32[72,128]{1,0:T(8,128)S(1)} collective-permute-done((f32[72,128]{1,0:T(8,128)S(1)}, f32[72,128]{1,0:T(8,128)S(1)}, u32[]{:S(2)}, u32[]{:S(2)}) %collective-permute-start.5) | collective-permute-done | bytes 36896 | tf_op jit(solution)/shard_map/ppermute | solution.py:251
  21.6 1.2 %collective-permute-done.3.straight_ref = f32[144,128]{1,0:T(8,128)S(1)} collective-permute-done((f32[144,128]{1,0:T(8,128)S(1)}, f32[144,128]{1,0:T(8,128)S(1)}, u32[]{:S(2)}, u32[]{:S(2)}) %collective-permute-start.3) | collective-permute-done | bytes 73760 | tf_op jit(solution)/shard_map/ppermute | solution.py:251
  22.9 1.4 %collective-permute-done.4.diagonal_ref = f32[144,128]{1,0:T(8,128)S(1)} collective-permute-done((f32[144,128]{1,0:T(8,128)S(1)}, f32[144,128]{1,0:T(8,128)S(1)}, u32[]{:S(2)}, u32[]{:S(2)}) %collective-permute-start.4) | collective-permute-done | bytes 73760 | tf_op jit(solution)/shard_map/ppermute | solution.py:251
  24.3 0.1 collective-permute-start.6
  24.4 0.1 collective-permute-start.7
  24.4 6.4 %collective-permute-done.7.mine_ref = s32[24,16]{1,0:T(8,128)S(1)} collective-permute-done((s32[24,16]{1,0:T(8,128)S(1)}, s32[24,16]{1,0:T(8,128)S(1)}, u32[]{:S(2)}, u32[]{:S(2)}) %collective-permute-start.7) | collective-permute-done | bytes 1568 | tf_op jit(solution)/shard_map/ppermute | solution.py:251
  30.8 0.0 collective-permute-start.8
  30.8 1.2 %collective-permute-done.8.other_ref = s32[24,16]{1,0:T(8,128)S(1)} collective-permute-done((s32[24,16]{1,0:T(8,128)S(1)}, s32[24,16]{1,0:T(8,128)S(1)}, u32[]{:S(2)}, u32[]{:S(2)}) %collective-permute-start.8) | collective-permute-done | bytes 1568 | tf_op jit(solution)/shard_map/ppermute | solution.py:251
  32.0 1.2 %shard_map.57.hot_ref = bf16[72,16,128]{2,1,0:T(8,128)(2,1)S(1)} custom-call(s32[2]{0:T(128)S(1)} %pad_add_fusion.place, s32[24,16]{1,0:T(8,128)S(1)} %collective-permute-done.7.mine_ref, s32[24,16]{1,0:T(8,128)S(1)} %collective-permute-done.8.other_ref, s32[24,16]{1,0:T(8,128)S(1)} %copy.9.cols.own_ref), custom_call_target="tpu_custom_call" | custom-call | tf_op jit(solution)/shard_map/pallas_call | solution.py:239
  33.2 0.0 collective-permute-done.6.last_ref
  33.2 6.1 %shard_map.58 = f32[32,6,128]{2,1,0:T(8,128)S(1)} custom-call(s32[2]{0:T(128)S(1)} %pad_add_fusion.place, s32[24,16]{1,0:T(8,128)S(1)} %copy.9.cols.own_ref, f32[144,128]{1,0:T(8,128)S(1)} %constant_dynamic-update-slice_fusion.own_ref, f32[144,128]{1,0:T(8,128)S(1)} %collective-permute-done.3.straight_ref, ...), custom_call_target="tpu_custom_call" | custom-call | tf_op jit(solution)/shard_map/pallas_call | solution.py:239
  39.3 10.3 %all_to_all.5.got_ref = f32[32,6,128]{2,1,0:T(8,128)S(1)} all-to-all(f32[32,6,128]{2,1,0:T(8,128)S(1)} %shard_map.58), channel_id=1, replica_groups=mesh['row'=8,'col'=4] {'row','col'}, dimensions={0} | all-to-all | bytes 196608 | tf_op jit(solution)/shard_map/all_to_all | solution.py:297
  49.6 1.2 %shard_map.59 = f32[6,128]{1,0:T(8,128)} custom-call(s32[2]{0:T(128)S(1)} %pad_add_fusion.place, f32[32,6,128]{2,1,0:T(8,128)S(1)} %all_to_all.5.got_ref), custom_call_target="tpu_custom_call" | custom-call | tf_op jit(solution)/shard_map/pallas_call | solution.py:239
  (3 shorter events, 0.0 us)
Async XLA Ops:
  0.0 12.4 %copy-start.1 = (f32[24,64]{1,0:T(8,128)S(1)}, f32[24,64]{1,0:T(8,128)}, u32[]{:S(2)}) copy-start(f32[24,64]{1,0:T(8,128)} %own_ref.2) | copy-start | bytes 18436
  0.0 12.4 %copy-start.2 = (f32[24,64]{1,0:T(8,128)S(1)}, f32[24,64]{1,0:T(8,128)}, u32[]{:S(2)}) copy-start(f32[24,64]{1,0:T(8,128)} %ridge_ref.1) | copy-start | bytes 18436
  0.0 8.0 %collective-permute-start = (f32[24,64]{1,0:T(8,128)}, f32[24,64]{1,0:T(8,128)S(1)}, u32[]{:S(2)}, u32[]{:S(2)}) collective-permute-start(f32[24,64]{1,0:T(8,128)} %own_ref.2), channel_id=1, source_target_pairs={{0,4},{1,29},{2,6},{3,31},{4,8},{5,1},{6,10},{7,3},{8,12},{9,5},{1... | collective-permute-start | bytes 18440 | tf_op jit(solution)/shard_map/ppermute | solution.py:251
  8.0 4.4 %collective-permute-start.1 = (f32[24,64]{1,0:T(8,128)S(1)}, f32[24,64]{1,0:T(8,128)S(1)}, u32[]{:S(2)}, u32[]{:S(2)}) collective-permute-start(f32[24,64]{1,0:T(8,128)S(1)} %collective-permute-done.mine_ref), channel_id=1, source_target_pairs={{0,1},{1,0},{2,3},{3,2},{4,5},{5,4},{6,7},{7,6},{8,9},{9,8},{10,11... | collective-permute-start | bytes 18440 | tf_op jit(solution)/shard_map/ppermute | solution.py:251
  8.8 1.9 %copy-start = (f32[24,4,64,64]{3,2,1,0:T(8,128)S(1)}, f32[24,4,64,64]{3,2,1,0:T(8,128)}, u32[]{:S(2)}) copy-start(f32[24,4,64,64]{3,2,1,0:T(8,128)} %w_ref.1) | copy-start | bytes 4718596
  10.7 0.7 %copy-start.3 = (s32[24]{0:T(128)S(1)}, s32[24]{0:T(128)}, u32[]{:S(2)}) copy-start(s32[24]{0:T(128)} %counts.1) | copy-start | bytes 292
  13.9 1.4 %collective-permute-start.2 = (f32[72,128]{1,0:T(8,128)S(1)}, f32[72,128]{1,0:T(8,128)S(1)}, u32[]{:S(2)}, u32[]{:S(2)}) collective-permute-start(f32[72,128]{1,0:T(8,128)S(1)} %get-tuple-element.11), channel_id=1, source_target_pairs={{0,1},{1,0},{2,3},{3,2},{4,5},{5,4},{6,7},{7,6},{8,9},{9,8},{10,11... | collective-permute-start | bytes 110600 | tf_op jit(solution)/shard_map/ppermute | solution.py:251
  15.3 7.5 %collective-permute-start.3 = (f32[144,128]{1,0:T(8,128)S(1)}, f32[144,128]{1,0:T(8,128)S(1)}, u32[]{:S(2)}, u32[]{:S(2)}) collective-permute-start(f32[144,128]{1,0:T(8,128)S(1)} %constant_dynamic-update-slice_fusion.own_ref), channel_id=1, source_target_pairs={{0,4},{1,29},{2,6},{3,31},{4,8},{5,1},{6,10},{7,3},{8,12},{9,5},{1... | collective-permute-start | bytes 221192 | tf_op jit(solution)/shard_map/ppermute | solution.py:251
  15.3 8.9 %collective-permute-start.4 = (f32[144,128]{1,0:T(8,128)S(1)}, f32[144,128]{1,0:T(8,128)S(1)}, u32[]{:S(2)}, u32[]{:S(2)}) collective-permute-start(f32[144,128]{1,0:T(8,128)S(1)} %constant_dynamic-update-slice_fusion.own_ref), channel_id=1, source_target_pairs={{0,6},{1,31},{2,4},{3,29},{4,10},{5,3},{6,8},{7,1},{8,14},{9,7},{1... | collective-permute-start | bytes 221192 | tf_op jit(solution)/shard_map/ppermute | solution.py:251
  17.6 4.0 %collective-permute-start.5 = (f32[72,128]{1,0:T(8,128)S(1)}, f32[72,128]{1,0:T(8,128)S(1)}, u32[]{:S(2)}, u32[]{:S(2)}) collective-permute-start(f32[72,128]{1,0:T(8,128)S(1)} %get-tuple-element.11), channel_id=1, source_target_pairs={{0,2},{1,3},{2,0},{3,1},{4,6},{5,7},{6,4},{7,5},{8,10},{9,11},{10,... | collective-permute-start | bytes 110600 | tf_op jit(solution)/shard_map/ppermute | solution.py:251
  24.3 8.9 %collective-permute-start.6 = (f32[360,128]{1,0:T(8,128)S(1)}, f32[360,128]{1,0:T(8,128)S(1)}, u32[]{:S(2)}, u32[]{:S(2)}) collective-permute-start(f32[360,128]{1,0:T(8,128)S(1)} %pad_maximum_fusion), channel_id=1, source_target_pairs={{0,1},{1,0},{2,3},{3,2},{4,5},{5,4},{6,7},{7,6},{8,9},{9,8},{10,11... | collective-permute-start | bytes 552968 | tf_op jit(solution)/shard_map/ppermute | solution.py:251
  24.4 6.4 %collective-permute-start.7 = (s32[24,16]{1,0:T(8,128)S(1)}, s32[24,16]{1,0:T(8,128)S(1)}, u32[]{:S(2)}, u32[]{:S(2)}) collective-permute-start(s32[24,16]{1,0:T(8,128)S(1)} %copy.9.cols.own_ref), channel_id=1, source_target_pairs={{0,4},{1,29},{2,6},{3,31},{4,8},{5,1},{6,10},{7,3},{8,12},{9,5},{1... | collective-permute-start | bytes 4616 | tf_op jit(solution)/shard_map/ppermute | solution.py:251
  30.8 1.2 %collective-permute-start.8 = (s32[24,16]{1,0:T(8,128)S(1)}, s32[24,16]{1,0:T(8,128)S(1)}, u32[]{:S(2)}, u32[]{:S(2)}) collective-permute-start(s32[24,16]{1,0:T(8,128)S(1)} %collective-permute-done.7.mine_ref), channel_id=1, source_target_pairs={{0,1},{1,0},{2,3},{3,2},{4,5},{5,4},{6,7},{7,6},{8,9},{9,8},{10,11... | collective-permute-start | bytes 4616 | tf_op jit(solution)/shard_map/ppermute | solution.py:251

commit v3 on v2

v3 whole, which is shorter than its diff:
```python
import functools

import jax
import jax.numpy as jnp
from jax import lax
from jax.experimental import pallas as pl
from jax.experimental.pallas import tpu as pltpu
from jax.sharding import PartitionSpec as P


H = 21
BAND = 128
LANES = 128

epsilon = 1e-06
relax_weight = 2.0 / 3.0

NT = (((1,), (1,)), ((), ()))
NN = (((1,), (0,)), ((), ()))


def mxu(a, b, dims):
    return lax.dot_general(a, b, dims, preferred_element_type=jnp.float32)


def split(x):
    hi = x.astype(jnp.bfloat16)
    lo = (x - hi.astype(jnp.float32)).astype(jnp.bfloat16)
    return hi, lo


def lane_iota(shape):
    return lax.broadcasted_iota(jnp.int32, shape, len(shape) - 1)


def row_iota(shape):
    return lax.broadcasted_iota(jnp.int32, shape, 0)


def wrap(x, count):
    x = jnp.where(x < 0, x + count, x)
    return jnp.where(x >= count, x - count, x)


def roll(x, by):
    return pltpu.roll(x, by % LANES, 1)


def pack_kernel(all_rows, counts_hbm, w_hbm, cols_hbm, hi_ref, lo_ref, target_ref, counts, cols_ref,
                w_ref, sems):
    rows, slots, size, _ = w_ref.shape
    start = lax.axis_index("col") * slots
    per = LANES // size
    chunks = sems.shape[0] - 2
    step = rows // chunks
    small = [
        pltpu.make_async_copy(counts_hbm, counts, sems.at[chunks]),
        pltpu.make_async_copy(cols_hbm, cols_ref, sems.at[chunks + 1]),
    ]
    copies = [
        pltpu.make_async_copy(w_hbm.at[pl.ds(n * step, step)], w_ref.at[pl.ds(n * step, step)], sems.at[n])
        for n in range(chunks)
    ]
    for copy in small + copies:
        copy.start()
    for copy in small:
        copy.wait()
    cols = cols_ref[...]
    local = lane_iota(cols.shape)
    first = lax.axis_index("row") * rows
    target_ref[...] = wrap(cols - (first + local) + H, all_rows) + (rows - H) + local
    for i in range(rows):
        if i % step == 0:
            copies[i // step].wait()
        for p in range(slots // per):
            tile = jnp.concatenate([w_ref[i, per * p + h] for h in range(per)], axis=1)
            slot = lane_iota((size, LANES)) // size + (start + per * p)
            tile = jnp.where(slot < counts[i], tile, 0.0)
            hi, lo = split(tile)
            hi_ref[i, :, p * LANES : (p + 1) * LANES] = hi
            lo_ref[i, :, p * LANES : (p + 1) * LANES] = lo


def unit_kernel(size, targets, mine_ref, other_ref, own_ref, ridge_ref, hi_ref, lo_ref,
                block_ref, unit_ref, acc_ref):
    rows = own_ref.shape[0]
    slots = hi_ref.shape[2] // size
    column = lax.axis_index("col")
    even = column % 2 == 0
    prev = jnp.where(even, mine_ref[...], other_ref[...])
    after = jnp.where(even, other_ref[...], mine_ref[...])
    for g, x in enumerate((prev, own_ref[...], after)):
        unit = x / jnp.sqrt(jnp.sum(x * x, axis=1, keepdims=True) + epsilon)
        unit_ref[g * rows : (g + 1) * rows, :] = jnp.concatenate([unit, unit], axis=1)
    row8 = row_iota((8, LANES))
    half = lane_iota((8, LANES)) // size
    for i in range(rows):
        parts = []
        for p in range(slots // 2):
            tile = jnp.where(row8 == slots, 1.0, 0.0)
            for h in range(2):
                k = 2 * p + h
                vec = jnp.broadcast_to(unit_ref[pl.ds(targets[column * slots + k, i], 1), :], (8, LANES))
                tile = jnp.where((row8 == k) & (half == h), vec, tile)
            parts.append(tile)
        lhs = jnp.concatenate(parts, axis=1)
        hi, lo = split(lhs)
        both = mxu(jnp.concatenate([hi, lo], axis=0), hi_ref[i], NT)
        low = mxu(hi, lo_ref[i], NT)
        acc_ref[8 * i : 8 * i + 8, :] = both[:8] + both[8:] + low
    plane = [acc_ref[pl.ds(k, rows, stride=8), :] for k in range(slots + 1)]
    for p in range(slots // 2):
        block_ref[p * rows : (p + 1) * rows, :] = jnp.concatenate(plane[2 * p : 2 * p + 2], axis=1)
    degree = plane[slots] + jnp.where(column == 0, ridge_ref[...], 0.0)
    block_ref[(slots // 2) * rows :, :] = jnp.concatenate([degree, jnp.zeros_like(degree)], axis=1)


def hot_kernel(slots, all_rows, mine_ref, other_ref, own_ref, even_ref, odd_ref, turned_ref,
               even_tmp, odd_tmp):
    total, rows = own_ref.shape
    column = lax.axis_index("col")
    even = column % 2 == 0
    prev = jnp.where(even, mine_ref[...], other_ref[...])
    after = jnp.where(even, other_ref[...], mine_ref[...])
    lane = lane_iota((rows, LANES))
    pairs = total // 2
    for g, cols in enumerate((prev, own_ref[...], after)):
        local = row_iota((rows, LANES)) + (g - 1) * rows
        cols = jnp.concatenate([cols, jnp.zeros((total, LANES - rows), jnp.int32)], axis=1)
        cols = jnp.concatenate([cols, jnp.zeros((LANES - total, LANES), jnp.int32)], axis=0)
        cols = cols.T[:rows]
        base = lax.axis_index("row") * rows + local
        where = wrap(wrap(cols - base + H, all_rows), all_rows) - H + local + 2 * rows
        bit = slots
        while bit < total:
            swapped = jnp.where((lane // bit) % 2 == 1, roll(where, bit), roll(where, -bit))
            where = jnp.where((column * slots // bit) % 2 == 1, swapped, where)
            bit *= 2
        for s in range(total):
            spread = jnp.broadcast_to(where[:, s : s + 1], (rows, LANES))
            hot = jnp.where(spread == lane, 1.0, 0.0)
            at, other = s // 2 + (s % 2) * pairs, s // 2 + (1 - s % 2) * pairs
            even_tmp[pl.ds(g * rows * total + at, rows, stride=total), :] = hot
            odd_tmp[pl.ds(g * rows * total + other, rows, stride=total), :] = hot
    for j in range(3 * rows):
        even_ref[j] = even_tmp[j * total : (j + 1) * total, :].astype(jnp.bfloat16)
        odd_ref[j] = odd_tmp[j * total : (j + 1) * total, :].astype(jnp.bfloat16)
    for n in range(rows * total // LANES):
        at = rows * total + n * LANES
        turned = even_tmp[at : at + LANES, :].T
        turned_ref[:, n * LANES : (n + 1) * LANES] = turned[rows : 4 * rows].astype(jnp.bfloat16)


def coarse_kernel(size, ncol, nrow, targets, own_ref, straight_ref, diagonal_ref, far_ref, last_ref,
                  unit_ref, even_ref, odd_ref, turned_ref, hi_ref, lo_ref, out_ref,
                  p_ref, q_ref, qh_ref, ql_ref, rh_ref, rl_ref, s_ref, th_ref, tl_ref):
    rows = hi_ref.shape[0]
    slots = hi_ref.shape[2] // size
    total = slots * ncol
    pairs = slots // 2
    half = total // 2
    column = lax.axis_index("col")
    low_half = lane_iota((rows, LANES)) < size
    even = column % 2 == 0
    planes = (pairs + 1) * rows
    blocks = [
        [(straight_ref, 0), (straight_ref, 1), (diagonal_ref, 0), (diagonal_ref, 1)],
        [(own_ref, 0), (own_ref, 1), (far_ref, 0), (last_ref, 4)],
        [(last_ref, 1), (last_ref, 0), (last_ref, 3), (last_ref, 2)],
    ]

    def plane(part, d, p):
        ref, index = blocks[part][d]
        return ref[index * planes + p * rows : index * planes + (p + 1) * rows, :]

    for part, group in enumerate((jnp.where(even, 0, 2), 1, jnp.where(even, 2, 0))):
        degree = sum(plane(part, d, pairs) for d in range(ncol))
        inverse = relax_weight / jnp.where(low_half, degree, 1.0)
        inverse = jnp.where(low_half, inverse, roll(inverse, size))
        unit = unit_ref[pl.ds(pl.multiple_of(group * rows, 8), rows), :]
        own_term = jnp.where(low_half, (1.0 - relax_weight) * unit, 0.0)
        for d in range(ncol):
            for p in range(pairs):
                v = plane(part, d, p) * inverse
                if p == 0:
                    v = v + jnp.where(column == d, own_term, 0.0)
                p_ref[pl.ds(group * (rows * half) + (d * pairs + p), rows, stride=half), :] = v
    for j in range(3 * rows):
        v = p_ref[j * half : (j + 1) * half, :]
        q = jnp.concatenate([v, roll(v, size)], axis=0)
        if rows <= j < 2 * rows:
            q_ref[j - rows] = q
        qh_ref[j], ql_ref[j] = split(q)
    tile_half = lane_iota((total, LANES)) // size
    zero = jnp.zeros((total, LANES), jnp.bfloat16)
    tiles = [[targets[column * slots + k, i] for k in range(slots)] for i in range(rows)]
    for i in range(rows):
        for p in range(pairs):
            his, los = [], []
            for h in range(2):
                t = tiles[i][2 * p + h]
                his.append(jnp.where(tile_half == h, qh_ref[t], zero))
                los.append(jnp.where(tile_half == h, ql_ref[t], zero))
            lanes = slice(p * LANES, (p + 1) * LANES)
            high = jnp.concatenate(his, axis=0)
            both = mxu(jnp.concatenate([high] + los, axis=0), hi_ref[i, :, lanes], NT)
            rest = mxu(high, lo_ref[i, :, lanes], NT)
            at = slice(2 * p * total, 2 * (p + 1) * total)
            rh_ref[i, at, :], rl_ref[i, at, :] = split(both[: 2 * total] + both[2 * total :] + rest)
    own_degree = plane(1, 0, pairs)
    for i in range(rows):
        diagonal = q_ref[i, :, :size] * own_degree[i : i + 1, :size]
        rh_ref[i, slots * total :, :], rl_ref[i, slots * total :, :] = split(diagonal)
    sign = jnp.where(lane_iota((total, (slots + 1) * total)) < slots * total, -1.0, 1.0)
    for i in range(rows):
        j = rows + i
        left = qh_ref[j, :, :size]
        both = mxu(jnp.concatenate([left, ql_ref[j, :, :size]], axis=0), rh_ref[i], NT)
        s = (both[:total] + both[total:] + mxu(left, rl_ref[i], NT)) * sign
        s_ref[i, :total, :], s_ref[i, total:, :] = split(s)
    for i in range(rows):
        hot = [(even_ref if k % 2 == 0 else odd_ref)[tiles[i][k]] for k in range(slots)]
        both = mxu(s_ref[i], jnp.concatenate(hot + [even_ref[rows + i]], axis=0), NN)
        at = slice(i * total, (i + 1) * total)
        th_ref[at, :], tl_ref[at, :] = split(both[:total] + both[total:])
    turned = turned_ref[...]
    absolute = mxu(turned, th_ref[...], NN) + mxu(turned, tl_ref[...], NN)
    share = rows // ncol
    out_ref[...] = jnp.zeros_like(out_ref)
    for g in range(3):
        row = wrap(lax.axis_index("row") + (g - 1), nrow)
        part = roll(absolute[g * rows : (g + 1) * rows], (1 - g) * rows)
        for c in range(ncol):
            out_ref[row * ncol + c] = part[c * share : (c + 1) * share]


def sum_kernel(ncol, nrow, got_ref, out_ref):
    share = out_ref.shape[0]
    total = None
    for g in range(3):
        row = wrap(lax.axis_index("row") + (g - 1), nrow)
        for c in range(ncol):
            part = got_ref[row * ncol + c]
            total = part if total is None else total + part
    local = row_iota(total.shape) + lax.axis_index("col") * share
    amount = (BAND // 2 - 2 * share * ncol - local) % LANES
    bit = 1
    while bit < LANES:
        total = jnp.where((amount // bit) % 2 == 1, roll(total, bit), total)
        bit *= 2
    out_ref[...] = total


HBM = pl.BlockSpec(memory_space=pltpu.HBM)
SMEM = pl.BlockSpec(memory_space=pltpu.SMEM)
VMEM = pl.BlockSpec(memory_space=pltpu.VMEM)
VMEM_LIMIT = 20 * 1024 * 1024
PACK_LIMIT = 51 * 1024 * 1024
CHUNKS = 6


def on_device(weights, block_cols, counts, near_null, prior_ridge):
    rows, slots, size, _ = weights.shape
    total = block_cols.shape[1]
    nrow, ncol = lax.axis_size("row"), lax.axis_size("col")
    all_rows = rows * nrow
    f32, bf16, i32 = jnp.float32, jnp.bfloat16, jnp.int32
    array = jax.ShapeDtypeStruct
    scratch = pltpu.VMEM

    def call(kernel, out_shape, specs, scratches, *operands, limit=VMEM_LIMIT):
        return pl.pallas_call(
            kernel, out_shape=out_shape, in_specs=specs,
            out_specs=jax.tree.map(lambda _: VMEM, out_shape), scratch_shapes=scratches,
            compiler_params=pltpu.CompilerParams(vmem_limit_bytes=limit),
        )(*operands)

    def send(x, to):
        pairs = []
        for r in range(nrow):
            for c in range(ncol):
                nr, nc = to(r, c)
                pairs.append((r * ncol + c, (nr % nrow) * ncol + nc))
        return lax.ppermute(x, ("row", "col"), pairs)

    def partner(x):
        return send(x, lambda r, c: (r, c ^ 1))

    def across(x):
        return send(x, lambda r, c: (r, c ^ 2))

    def outward(x, d=0):
        return send(x, lambda r, c: (r + (1 if c % 2 == 0 else -1), c ^ d))

    cols = block_cols.T
    null_mine = outward(near_null)
    cols_mine = outward(cols)
    w_hi, w_lo, targets = call(
        functools.partial(pack_kernel, all_rows),
        [array((rows, size, slots * size), bf16)] * 2 + [array((total, rows), i32)],
        [HBM] * 3,
        [
            pltpu.SMEM((rows,), i32), scratch((total, rows), i32), scratch(weights.shape, f32),
            pltpu.SemaphoreType.DMA((2 + (CHUNKS if rows % CHUNKS == 0 else 1),)),
        ],
        counts, weights, cols, limit=PACK_LIMIT)
    null_other = partner(null_mine)
    cols_other = partner(cols_mine)
    planes = (slots // 2 + 1) * rows
    block, unit = call(
        functools.partial(unit_kernel, size),
        [array((planes, LANES), f32), array((3 * rows, LANES), f32)],
        [SMEM] + [VMEM] * 6, [scratch((8 * rows, size), f32)],
        targets, null_mine, null_other, near_null, prior_ridge, w_hi, w_lo)
    hots = call(
        functools.partial(hot_kernel, slots, all_rows),
        [array((3 * rows, total, LANES), bf16)] * 2 + [array((3 * rows, rows * total), bf16)],
        [VMEM] * 3, [scratch((3 * rows * total, LANES), f32)] * 2,
        cols_mine, cols_other, cols)
    own = jnp.concatenate([block, partner(block)])
    diagonal = outward(own, 2)
    straight = outward(own)
    far = across(block)
    last = partner(jnp.concatenate([straight, diagonal, far]))
    parts = call(
        functools.partial(coarse_kernel, size, ncol, nrow),
        array((nrow * ncol, rows // ncol, LANES), f32), [SMEM] + [VMEM] * 11,
        [
            scratch((3 * rows * total // 2, LANES), f32),
            scratch((rows, total, LANES), f32),
            scratch((3 * rows, total, LANES), bf16),
            scratch((3 * rows, total, LANES), bf16),
            scratch((rows, (slots + 1) * total, size), bf16),
            scratch((rows, (slots + 1) * total, size), bf16),
            scratch((rows, 2 * total, (slots + 1) * total), bf16),
            scratch((rows * total, LANES), bf16),
            scratch((rows * total, LANES), bf16),
        ],
        targets, own, straight, diagonal, far, last, unit, *hots, w_hi, w_lo)
    got = lax.all_to_all(parts, ("row", "col"), 0, 0)
    return call(
        functools.partial(sum_kernel, ncol, nrow), array((rows // ncol, LANES), f32), [VMEM], [], got)


def solution(mesh):
    placed = (P("row", "col", None, None), P("row", None), P("row"), P("row", None), P("row", None))

    return jax.shard_map(
        on_device, mesh=mesh, in_specs=placed, out_specs=P(("row", "col"), None), check_vma=False
    )
```

time: 51 us -> 46.2 us (0.906)
  Pallas kernels: 11 us -> 8.23 us
  local copies, waits for them, and re-layouts: 3.33 us -> 1.37 us
    pallas_call x5, Pallas kernels: 11 us -> 8.23 us  [call(): pl.pallas_call(kernel, out_shape=out_shape, in_specs=specs, out_specs=jax...]
    unnamed x10 -> x9, local copies, waits for them, and re-layouts: 3.32 us -> 1.36 us
  transfers between devices with their start and end apart: 9 -> 9, of which waited for: 7 -> 7; matrix products, arithmetic and copies ran while one was open for 2% -> 0% of each run, Pallas kernels for 4% -> 6%
where the time goes in v3:
time: 46.2 us; the launch traced here: 46 us
  waiting for transfers between devices  19.4 us (42%)
  blocking collectives  10.3 us (22%)
  Pallas kernels  8.23 us (18%)
  starting transfers between devices  6.52 us (14%)
  local copies, waits for them, and re-layouts  1.37 us (3%)
    ppermute x9, waiting for transfers between devices, send(): return lax.ppermute(x, ('row', 'col'), pairs)  19.4 us
    all_to_all x1, blocking collectives, on_device(): got = lax.all_to_all(parts, ('row', 'col'), 0, 0)  10.3 us
    pallas_call x5, Pallas kernels, call(): pl.pallas_call(kernel, out_shape=out_shape, in_specs=specs, out_specs=jax...  8.23 us
    ppermute x9, starting transfers between devices, send(): return lax.ppermute(x, ('row', 'col'), pairs)  6.52 us
    unnamed x9, local copies, waits for them, and re-layouts  1.36 us
  transfers between devices with their start and end apart: 9, of which 7 were waited for; matrix products, arithmetic and copies ran while one was open for 0% of the time, Pallas kernels for 6%

profile of v3, /device:TPU:0, one launch (start us, length us, event | category | flops | bytes accessed | tf_op | source)
XLA Modules:
  0.0 46.0 jit_solution(11851311022589986334)
XLA Ops:
  0.0 3.0 %collective-permute-start = (f32[24,64]{1,0:T(8,128)}, f32[24,64]{1,0:T(8,128)S(1)}, u32[]{:S(2)}, u32[]{:S(2)}) collective-permute-start(f32[24,64]{1,0:T(8,128)} %own_ref.1), channel_id=1, source_target_pairs={{0,4},{1,29},{2,6},{3,31},{4,8},{5,1},{6,10},{7,3},{8,12},{9,5},{1... | collective-permute-start | bytes 18440 | tf_op jit(solution)/shard_map/ppermute | solution.py:284
  3.0 4.9 %collective-permute-done.mine_ref = f32[24,64]{1,0:T(8,128)S(1)} collective-permute-done((f32[24,64]{1,0:T(8,128)}, f32[24,64]{1,0:T(8,128)S(1)}, u32[]{:S(2)}, u32[]{:S(2)}) %collective-permute-start) | collective-permute-done | bytes 6176 | tf_op jit(solution)/shard_map/ppermute | solution.py:284
  7.9 0.0 collective-permute-start.1
  7.9 0.0 copy-start
  7.9 0.7 %copy-done = s32[24,16]{0,1:T(8,128)S(1)} copy-done((s32[24,16]{0,1:T(8,128)S(1)}, s32[24,16]{0,1:T(8,128)}, u32[]{:S(2)}) %copy-start) | copy-done | bytes 1560
  8.6 0.0 copy-start.3
  8.6 0.7 %copy-done.3 = s32[24]{0:T(128)S(1)} copy-done((s32[24]{0:T(128)S(1)}, s32[24]{0:T(128)}, u32[]{:S(2)}) %copy-start.3) | copy-done | bytes 120
  9.3 0.0 copy-start.1
  9.3 0.0 copy-start.2
  9.3 2.1 %shard_map.55 = (bf16[24,64,256]{2,1,0:T(8,128)(2,1)S(1)}, bf16[24,64,256]{2,1,0:T(8,128)(2,1)S(1)}, s32[16,24]{1,0:T(8,128)S(1)}) custom-call(s32[24]{0:T(128)S(1)} %copy-done.3, f32[24,4,64,64]{3,2,1,0:T(8,128)} %w_hbm.1, s32[16,24]{1,0:T(8,128)S(1)} %bitcast.1), custom_call_target="tpu_custom_call" | custom-call | tf_op jit(solution)/shard_map/pallas_call | solution.py:272
  11.4 0.0 collective-permute-done.1.other_ref
  11.4 0.0 copy-done.1
  11.4 0.0 copy-done.2
  11.4 1.5 %shard_map.56 = (f32[72,128]{1,0:T(8,128)S(1)}, f32[72,128]{1,0:T(8,128)S(1)}) custom-call(s32[16,24]{1,0:T(8,128)S(1)} %get-tuple-element.13.targets, f32[24,64]{1,0:T(8,128)S(1)} %collective-permute-done.mine_ref, f32[24,64]{1,0:T(8,128)S(1)} %collective-permute-done.1.other_ref, f32[24,64]{1,0:T(8,128)S(1)} %copy-done.1, f32[24,64]{1,0:T(8,128)S(1)} %copy-done.2, ...), custom_call_target="tpu_custom_call" | custom-call | tf_op jit(solution)/shard_map/pallas_call | solution.py:272
  12.8 0.5 %collective-permute-start.2 = (f32[72,128]{1,0:T(8,128)S(1)}, f32[72,128]{1,0:T(8,128)S(1)}, u32[]{:S(2)}, u32[]{:S(2)}) collective-permute-start(f32[72,128]{1,0:T(8,128)S(1)} %get-tuple-element.16), channel_id=1, source_target_pairs={{0,1},{1,0},{2,3},{3,2},{4,5},{5,4},{6,7},{7,6},{8,9},{9,8},{10,11... | collective-permute-start | bytes 110600 | tf_op jit(solution)/shard_map/ppermute | solution.py:284
  13.4 0.9 %collective-permute-done.2 = f32[72,128]{1,0:T(8,128)S(1)} collective-permute-done((f32[72,128]{1,0:T(8,128)S(1)}, f32[72,128]{1,0:T(8,128)S(1)}, u32[]{:S(2)}, u32[]{:S(2)}) %collective-permute-start.2) | collective-permute-done | bytes 36896 | tf_op jit(solution)/shard_map/ppermute | solution.py:284
  14.2 0.0 collective-permute-start.3
  14.2 2.3 %collective-permute-start.4 = (f32[144,128]{1,0:T(8,128)S(1)}, f32[144,128]{1,0:T(8,128)S(1)}, u32[]{:S(2)}, u32[]{:S(2)}) collective-permute-start(f32[144,128]{1,0:T(8,128)S(1)} %constant_dynamic-update-slice_fusion.own_ref), channel_id=1, source_target_pairs={{0,6},{1,31},{2,4},{3,29},{4,10},{5,3},{6,8},{7,1},{8,14},{9,7},{1... | collective-permute-start | bytes 221192 | tf_op jit(solution)/shard_map/ppermute | solution.py:284
  16.6 0.5 %collective-permute-start.5 = (f32[72,128]{1,0:T(8,128)S(1)}, f32[72,128]{1,0:T(8,128)S(1)}, u32[]{:S(2)}, u32[]{:S(2)}) collective-permute-start(f32[72,128]{1,0:T(8,128)S(1)} %get-tuple-element.16), channel_id=1, source_target_pairs={{0,2},{1,3},{2,0},{3,1},{4,6},{5,7},{6,4},{7,5},{8,10},{9,11},{10,... | collective-permute-start | bytes 110600 | tf_op jit(solution)/shard_map/ppermute | solution.py:284
  17.1 3.5 %collective-permute-done.5.far_ref = f32[72,128]{1,0:T(8,128)S(1)} collective-permute-done((f32[72,128]{1,0:T(8,128)S(1)}, f32[72,128]{1,0:T(8,128)S(1)}, u32[]{:S(2)}, u32[]{:S(2)}) %collective-permute-start.5) | collective-permute-done | bytes 36896 | tf_op jit(solution)/shard_map/ppermute | solution.py:284
  20.6 1.1 %collective-permute-done.3.straight_ref = f32[144,128]{1,0:T(8,128)S(1)} collective-permute-done((f32[144,128]{1,0:T(8,128)S(1)}, f32[144,128]{1,0:T(8,128)S(1)}, u32[]{:S(2)}, u32[]{:S(2)}) %collective-permute-start.3) | collective-permute-done | bytes 73760 | tf_op jit(solution)/shard_map/ppermute | solution.py:284
  21.7 1.5 %collective-permute-done.4.diagonal_ref = f32[144,128]{1,0:T(8,128)S(1)} collective-permute-done((f32[144,128]{1,0:T(8,128)S(1)}, f32[144,128]{1,0:T(8,128)S(1)}, u32[]{:S(2)}, u32[]{:S(2)}) %collective-permute-start.4) | collective-permute-done | bytes 73760 | tf_op jit(solution)/shard_map/ppermute | solution.py:284
  23.3 0.1 collective-permute-start.6
  23.3 0.1 collective-permute-start.7
  23.4 6.3 %collective-permute-done.7.mine_ref = s32[16,24]{1,0:T(8,128)S(1)} collective-permute-done((s32[16,24]{1,0:T(8,128)S(1)}, s32[16,24]{1,0:T(8,128)S(1)}, u32[]{:S(2)}, u32[]{:S(2)}) %collective-permute-start.7) | collective-permute-done | bytes 1568 | tf_op jit(solution)/shard_map/ppermute | solution.py:284
  29.8 0.0 collective-permute-start.8
  29.8 1.2 %collective-permute-done.8.other_ref = s32[16,24]{1,0:T(8,128)S(1)} collective-permute-done((s32[16,24]{1,0:T(8,128)S(1)}, s32[16,24]{1,0:T(8,128)S(1)}, u32[]{:S(2)}, u32[]{:S(2)}) %collective-permute-start.8) | collective-permute-done | bytes 1568 | tf_op jit(solution)/shard_map/ppermute | solution.py:284
  30.9 0.8 %shard_map.57 = (bf16[72,16,128]{2,1,0:T(8,128)(2,1)S(1)}, bf16[72,16,128]{2,1,0:T(8,128)(2,1)S(1)}, bf16[72,384]{1,0:T(8,128)(2,1)S(1)}) custom-call(s32[16,24]{1,0:T(8,128)S(1)} %collective-permute-done.7.mine_ref, s32[16,24]{1,0:T(8,128)S(1)} %collective-permute-done.8.other_ref, s32[16,24]{1,0:T(8,128)S(1)} %bitcast.3), custom_call_target="tpu_custom_call" | custom-call | tf_op jit(solution)/shard_map/pallas_call | solution.py:272
  31.8 0.0 collective-permute-done.6.last_ref
  31.8 2.8 %shard_map.58 = f32[32,6,128]{2,1,0:T(8,128)S(1)} custom-call(s32[16,24]{1,0:T(8,128)S(1)} %get-tuple-element.13.targets, f32[144,128]{1,0:T(8,128)S(1)} %constant_dynamic-update-slice_fusion.own_ref, f32[144,128]{1,0:T(8,128)S(1)} %collective-permute-done.3.straight_ref, f32[144,128]{1,0:T(8,128)S(1)} %collective-permute-done.4.diagonal_ref, ...), custom_call_target="tpu_custom_call" | custom-call | tf_op jit(solution)/shard_map/pallas_call | solution.py:272
  34.6 10.3 %all_to_all.5.got_ref = f32[32,6,128]{2,1,0:T(8,128)S(1)} all-to-all(f32[32,6,128]{2,1,0:T(8,128)S(1)} %shard_map.58), channel_id=1, replica_groups=mesh['row'=8,'col'=4] {'row','col'}, dimensions={0} | all-to-all | bytes 196608 | tf_op jit(solution)/shard_map/all_to_all | solution.py:340
  44.9 1.1 %shard_map.59 = f32[6,128]{1,0:T(8,128)} custom-call(f32[32,6,128]{2,1,0:T(8,128)S(1)} %all_to_all.5.got_ref), custom_call_target="tpu_custom_call" | custom-call | tf_op jit(solution)/shard_map/pallas_call | solution.py:272
  (3 shorter events, 0.0 us)
Async XLA Ops:
  0.0 7.9 %collective-permute-start = (f32[24,64]{1,0:T(8,128)}, f32[24,64]{1,0:T(8,128)S(1)}, u32[]{:S(2)}, u32[]{:S(2)}) collective-permute-start(f32[24,64]{1,0:T(8,128)} %own_ref.1), channel_id=1, source_target_pairs={{0,4},{1,29},{2,6},{3,31},{4,8},{5,1},{6,10},{7,3},{8,12},{9,5},{1... | collective-permute-start | bytes 18440 | tf_op jit(solution)/shard_map/ppermute | solution.py:284
  7.9 3.4 %collective-permute-start.1 = (f32[24,64]{1,0:T(8,128)S(1)}, f32[24,64]{1,0:T(8,128)S(1)}, u32[]{:S(2)}, u32[]{:S(2)}) collective-permute-start(f32[24,64]{1,0:T(8,128)S(1)} %collective-permute-done.mine_ref), channel_id=1, source_target_pairs={{0,1},{1,0},{2,3},{3,2},{4,5},{5,4},{6,7},{7,6},{8,9},{9,8},{10,11... | collective-permute-start | bytes 18440 | tf_op jit(solution)/shard_map/ppermute | solution.py:284
  7.9 0.7 %copy-start = (s32[24,16]{0,1:T(8,128)S(1)}, s32[24,16]{0,1:T(8,128)}, u32[]{:S(2)}) copy-start(s32[24,16]{0,1:T(8,128)} %param.6) | copy-start | bytes 4612
  8.6 0.7 %copy-start.3 = (s32[24]{0:T(128)S(1)}, s32[24]{0:T(128)}, u32[]{:S(2)}) copy-start(s32[24]{0:T(128)} %counts_hbm.1) | copy-start | bytes 292
  9.3 2.1 %copy-start.1 = (f32[24,64]{1,0:T(8,128)S(1)}, f32[24,64]{1,0:T(8,128)}, u32[]{:S(2)}) copy-start(f32[24,64]{1,0:T(8,128)} %own_ref.1) | copy-start | bytes 18436
  9.3 2.1 %copy-start.2 = (f32[24,64]{1,0:T(8,128)S(1)}, f32[24,64]{1,0:T(8,128)}, u32[]{:S(2)}) copy-start(f32[24,64]{1,0:T(8,128)} %ridge_ref.1) | copy-start | bytes 18436
  12.8 1.4 %collective-permute-start.2 = (f32[72,128]{1,0:T(8,128)S(1)}, f32[72,128]{1,0:T(8,128)S(1)}, u32[]{:S(2)}, u32[]{:S(2)}) collective-permute-start(f32[72,128]{1,0:T(8,128)S(1)} %get-tuple-element.16), channel_id=1, source_target_pairs={{0,1},{1,0},{2,3},{3,2},{4,5},{5,4},{6,7},{7,6},{8,9},{9,8},{10,11... | collective-permute-start | bytes 110600 | tf_op jit(solution)/shard_map/ppermute | solution.py:284
  14.2 7.5 %collective-permute-start.3 = (f32[144,128]{1,0:T(8,128)S(1)}, f32[144,128]{1,0:T(8,128)S(1)}, u32[]{:S(2)}, u32[]{:S(2)}) collective-permute-start(f32[144,128]{1,0:T(8,128)S(1)} %constant_dynamic-update-slice_fusion.own_ref), channel_id=1, source_target_pairs={{0,4},{1,29},{2,6},{3,31},{4,8},{5,1},{6,10},{7,3},{8,12},{9,5},{1... | collective-permute-start | bytes 221192 | tf_op jit(solution)/shard_map/ppermute | solution.py:284
  14.2 9.0 %collective-permute-start.4 = (f32[144,128]{1,0:T(8,128)S(1)}, f32[144,128]{1,0:T(8,128)S(1)}, u32[]{:S(2)}, u32[]{:S(2)}) collective-permute-start(f32[144,128]{1,0:T(8,128)S(1)} %constant_dynamic-update-slice_fusion.own_ref), channel_id=1, source_target_pairs={{0,6},{1,31},{2,4},{3,29},{4,10},{5,3},{6,8},{7,1},{8,14},{9,7},{1... | collective-permute-start | bytes 221192 | tf_op jit(solution)/shard_map/ppermute | solution.py:284
  16.6 4.0 %collective-permute-start.5 = (f32[72,128]{1,0:T(8,128)S(1)}, f32[72,128]{1,0:T(8,128)S(1)}, u32[]{:S(2)}, u32[]{:S(2)}) collective-permute-start(f32[72,128]{1,0:T(8,128)S(1)} %get-tuple-element.16), channel_id=1, source_target_pairs={{0,2},{1,3},{2,0},{3,1},{4,6},{5,7},{6,4},{7,5},{8,10},{9,11},{10,... | collective-permute-start | bytes 110600 | tf_op jit(solution)/shard_map/ppermute | solution.py:284
  23.3 8.5 %collective-permute-start.6 = (f32[360,128]{1,0:T(8,128)S(1)}, f32[360,128]{1,0:T(8,128)S(1)}, u32[]{:S(2)}, u32[]{:S(2)}) collective-permute-start(f32[360,128]{1,0:T(8,128)S(1)} %pad_maximum_fusion), channel_id=1, source_target_pairs={{0,1},{1,0},{2,3},{3,2},{4,5},{5,4},{6,7},{7,6},{8,9},{9,8},{10,11... | collective-permute-start | bytes 552968 | tf_op jit(solution)/shard_map/ppermute | solution.py:284
  23.3 6.4 %collective-permute-start.7 = (s32[16,24]{1,0:T(8,128)S(1)}, s32[16,24]{1,0:T(8,128)S(1)}, u32[]{:S(2)}, u32[]{:S(2)}) collective-permute-start(s32[16,24]{1,0:T(8,128)S(1)} %bitcast.2), channel_id=1, source_target_pairs={{0,4},{1,29},{2,6},{3,31},{4,8},{5,1},{6,10},{7,3},{8,12},{9,5},{1... | collective-permute-start | bytes 4616 | tf_op jit(solution)/shard_map/ppermute | solution.py:284
  29.8 1.2 %collective-permute-start.8 = (s32[16,24]{1,0:T(8,128)S(1)}, s32[16,24]{1,0:T(8,128)S(1)}, u32[]{:S(2)}, u32[]{:S(2)}) collective-permute-start(s32[16,24]{1,0:T(8,128)S(1)} %collective-permute-done.7.mine_ref), channel_id=1, source_target_pairs={{0,1},{1,0},{2,3},{3,2},{4,5},{5,4},{6,7},{7,6},{8,9},{9,8},{10,11... | collective-permute-start | bytes 4616 | tf_op jit(solution)/shard_map/ppermute | solution.py:284

commit v4 on v3

v4 whole, which is shorter than its diff:
```python
import functools

import jax
import jax.numpy as jnp
from jax import lax
from jax.experimental import pallas as pl
from jax.experimental.pallas import tpu as pltpu
from jax.sharding import PartitionSpec as P


H = 21
BAND = 128
LANES = 128

epsilon = 1e-06
relax_weight = 2.0 / 3.0

NT = (((1,), (1,)), ((), ()))
NN = (((1,), (0,)), ((), ()))


def mxu(a, b, dims):
    return lax.dot_general(a, b, dims, preferred_element_type=jnp.float32)


def split(x):
    hi = x.astype(jnp.bfloat16)
    lo = (x - hi.astype(jnp.float32)).astype(jnp.bfloat16)
    return hi, lo


def lane_iota(shape):
    return lax.broadcasted_iota(jnp.int32, shape, len(shape) - 1)


def row_iota(shape):
    return lax.broadcasted_iota(jnp.int32, shape, 0)


def wrap(x, count):
    x = jnp.where(x < 0, x + count, x)
    return jnp.where(x >= count, x - count, x)


def roll(x, by):
    return pltpu.roll(x, by % LANES, 1)


def pack_kernel(w_hbm, pack_ref, w_ref, sems):
    rows, slots, size, _ = w_ref.shape
    per = LANES // size
    chunks = sems.shape[0]
    step = rows // chunks
    copies = [
        pltpu.make_async_copy(w_hbm.at[pl.ds(n * step, step)], w_ref.at[pl.ds(n * step, step)], sems.at[n])
        for n in range(chunks)
    ]
    for copy in copies:
        copy.start()
    for i in range(rows):
        if i % step == 0:
            copies[i // step].wait()
        for p in range(slots // per):
            tile = jnp.concatenate([w_ref[i, per * p + h] for h in range(per)], axis=1)
            hi, lo = split(tile)
            pack_ref[i, :, 2 * p * LANES : (2 * p + 1) * LANES] = hi
            pack_ref[i, :, (2 * p + 1) * LANES : 2 * (p + 1) * LANES] = lo


def two_part(hi, lo):
    top = jnp.concatenate([hi, hi], axis=1)
    return jnp.concatenate([top, jnp.concatenate([lo, jnp.zeros_like(lo)], axis=1)], axis=0)


def aim_kernel(all_rows, counts_ref, cols_ref, target_ref):
    total, rows = cols_ref.shape
    local = lane_iota((total, rows))
    first = lax.axis_index("row") * rows
    at = wrap(cols_ref[...] - (first + local) + H, all_rows) + (rows - H) + local
    mirror = jnp.where(at < rows, at + 2 * rows, jnp.where(at >= 2 * rows, at - 2 * rows, at))
    at = jnp.where(lax.axis_index("col") % 2 == 0, at, mirror)
    target_ref[...] = jnp.where(row_iota((total, rows)) < counts_ref[...], at, 3 * rows)


def unit_kernel(size, targets, mine_ref, other_ref, own_ref, ridge_ref, pack_ref,
                block_ref, unit_ref, acc_ref):
    rows = own_ref.shape[0]
    slots = pack_ref.shape[2] // (2 * size)
    column = lax.axis_index("col")
    for g, ref in enumerate((mine_ref, own_ref, other_ref)):
        x = ref[...]
        unit = x / jnp.sqrt(jnp.sum(x * x, axis=1, keepdims=True) + epsilon)
        unit_ref[g * rows : (g + 1) * rows, :] = jnp.concatenate([unit, unit], axis=1)
    unit_ref[3 * rows :, :] = jnp.zeros((8, LANES), jnp.float32)
    row8 = row_iota((8, LANES))
    half = lane_iota((8, LANES)) // size
    for i in range(rows):
        both = None
        for p in range(slots // 2):
            tile = jnp.zeros((8, LANES), jnp.float32)
            for h in range(2):
                k = 2 * p + h
                t = targets[column * slots + k, i]
                vec = jnp.broadcast_to(unit_ref[pl.ds(t, 1), :], (8, LANES))
                one = jnp.where(t < 3 * rows, 1.0, 0.0)
                tile = jnp.where((row8 == k) & (half == h), vec, tile)
                tile = jnp.where((row8 == slots) & (half == h), one, tile)
            term = mxu(two_part(*split(tile)), pack_ref[i, :, 2 * p * LANES : 2 * (p + 1) * LANES], NT)
            both = term if both is None else both + term
        acc_ref[8 * i : 8 * i + 8, :] = both[:8] + both[8:]
    plane = [acc_ref[pl.ds(k, rows, stride=8), :] for k in range(slots + 1)]
    for p in range(slots // 2):
        block_ref[p * rows : (p + 1) * rows, :] = jnp.concatenate(plane[2 * p : 2 * p + 2], axis=1)
    degree = plane[slots] + jnp.where(column == 0, ridge_ref[...], 0.0)
    keep = block_ref.shape[0] - (slots // 2) * rows
    rest = jnp.concatenate([degree[keep:], jnp.zeros((2 * keep - rows, size), jnp.float32)], axis=0)
    block_ref[(slots // 2) * rows :, :] = jnp.concatenate([degree[:keep], rest], axis=1)


def hot_kernel(slots, all_rows, mine_ref, other_ref, own_ref, even_ref, odd_ref, turned_ref,
               even_tmp, odd_tmp, turn_tmp):
    total, rows = own_ref.shape
    column = lax.axis_index("col")
    reach = jnp.where(column % 2 == 0, rows, -rows)
    lane = lane_iota((rows, LANES))
    pairs = total // 2
    for g, ref in enumerate((mine_ref, own_ref, other_ref)):
        cols = ref[...]
        local = row_iota((rows, LANES)) + (g - 1) * reach
        cols = jnp.concatenate([cols, jnp.zeros((total, LANES - rows), jnp.int32)], axis=1)
        cols = jnp.concatenate([cols, jnp.zeros((LANES - total, LANES), jnp.int32)], axis=0)
        cols = cols.T[:rows]
        base = lax.axis_index("row") * rows + local
        where = wrap(wrap(cols - base + H, all_rows), all_rows) - H + local + 2 * rows
        bit = slots
        while bit < total:
            swapped = jnp.where((lane // bit) % 2 == 1, roll(where, bit), roll(where, -bit))
            where = jnp.where((column * slots // bit) % 2 == 1, swapped, where)
            bit *= 2
        for s in range(total):
            spread = jnp.broadcast_to(where[:, s : s + 1], (rows, LANES))
            hot = jnp.where(spread == lane, 1.0, 0.0)
            at, other = s // 2 + (s % 2) * pairs, s // 2 + (1 - s % 2) * pairs
            even_tmp[pl.ds(g * rows * total + at, rows, stride=total), :] = hot
            odd_tmp[pl.ds(g * rows * total + other, rows, stride=total), :] = hot
            if g == 1:
                turn_tmp[pl.ds(at, rows, stride=total), :] = jnp.where(
                    spread == LANES - 1 - lane, 1.0, 0.0)
    for j in range(3 * rows):
        even_ref[j] = even_tmp[j * total : (j + 1) * total, :].astype(jnp.bfloat16)
        odd_ref[j] = odd_tmp[j * total : (j + 1) * total, :].astype(jnp.bfloat16)
    even_ref[3 * rows] = jnp.zeros((total, LANES), jnp.bfloat16)
    odd_ref[3 * rows] = jnp.zeros((total, LANES), jnp.bfloat16)
    for n in range(rows * total // LANES):
        lanes = slice(n * LANES, (n + 1) * LANES)
        turned = turn_tmp[lanes, :].T
        turned_ref[:, lanes] = turned[LANES - 4 * rows : LANES - rows].astype(jnp.bfloat16)


def prolong_rows(planes, unit, column, slots, size, p_ref, first, store):
    rows, ncol = unit.shape[0], len(planes)
    pairs = slots // 2
    half = pairs * ncol
    low_half = lane_iota((rows, LANES)) < size
    degree = sum(block(pairs * rows, None) for block in planes)
    keep = degree.shape[0]
    degree = jnp.concatenate([degree, roll(degree, size)[: rows - keep]], axis=0)
    inverse = relax_weight / jnp.where(low_half, degree, 1.0)
    inverse = jnp.where(low_half, inverse, roll(inverse, size))
    own_term = jnp.where(low_half, (1.0 - relax_weight) * unit, 0.0)
    for d in range(ncol):
        for p in range(pairs):
            v = planes[d](p * rows, (p + 1) * rows) * inverse
            if p == 0:
                v = v + jnp.where(column == d, own_term, 0.0)
            p_ref[pl.ds(first * half + d * pairs + p, rows, stride=half), :] = v
    for j in range(first, first + rows):
        v = p_ref[j * half : (j + 1) * half, :]
        store(j, jnp.concatenate([v, roll(v, size)], axis=0))


def block_of(ref, index, size):
    def rows_of(start, stop):
        return ref[index * size + start : index * size + (size if stop is None else stop), :]

    return rows_of


def ready_kernel(size, slots, straight_ref, diagonal_ref, own_ref, far_ref, far_partner_ref, unit_ref,
                 qh_ref, ql_ref, left_ref, diagonal_term_ref, p_ref):
    count = far_ref.shape[0]
    rows, total, _ = diagonal_term_ref.shape
    column = lax.axis_index("col")
    degree = own_ref[(slots // 2) * rows : count, :]
    degree = jnp.concatenate([degree, roll(degree, size)[: rows - degree.shape[0]]], axis=0)
    low_half = lane_iota((total, LANES)) < size
    groups = (
        [(straight_ref, 0), (straight_ref, 1), (diagonal_ref, 0), (diagonal_ref, 1)],
        [(own_ref, 0), (own_ref, 1), (far_ref, 0), (far_partner_ref, 0)],
    )

    def store(j, q):
        qh_ref[j], ql_ref[j] = split(q)
        if j >= rows:
            i = j - rows
            hi, lo = split(jnp.where(low_half, q, roll(q, size)))
            left_ref[i, :total, :] = hi
            left_ref[i, total:, :] = jnp.where(low_half, lo, jnp.zeros_like(lo))
            term = q[:, :size] * degree[i : i + 1, :size]
            diagonal_term_ref[i] = jnp.concatenate(split(term), axis=1)

    for g, group in enumerate(groups):
        blocks = [block_of(ref, index, count) for ref, index in group]
        unit = unit_ref[g * rows : (g + 1) * rows, :]
        prolong_rows(blocks, unit, column, slots, size, p_ref, g * rows, store)


def coarse_kernel(size, ncol, nrow, targets, last_ref, unit_ref, ready_h_ref, ready_l_ref, left_ref,
                  diagonal_term_ref, even_ref, odd_ref, turned_ref, pack_ref, out_ref,
                  p_ref, qh_ref, ql_ref, r_ref, s_ref, t_ref):
    rows = pack_ref.shape[0]
    slots = pack_ref.shape[2] // (2 * size)
    total = slots * ncol
    pairs = slots // 2
    column = lax.axis_index("col")
    count = last_ref.shape[0] // ncol

    def store(j, q):
        qh_ref[2 * rows + j], ql_ref[2 * rows + j] = split(q)

    blocks = [block_of(last_ref, d ^ 1, count) for d in range(ncol)]
    prolong_rows(blocks, unit_ref[2 * rows : 3 * rows, :], column, slots, size, p_ref, 0, store)
    for table, ready in ((qh_ref, ready_h_ref), (ql_ref, ready_l_ref)):
        table[: 2 * rows] = ready[...]
        table[3 * rows] = jnp.zeros((total, LANES), jnp.bfloat16)
    tile_half = lane_iota((total, LANES)) // size
    zero = jnp.zeros((total, LANES), jnp.bfloat16)
    tiles = [[targets[column * slots + k, i] for k in range(slots)] for i in range(rows)]
    for i in range(rows):
        for p in range(pairs):
            his, los = [], []
            for h in range(2):
                t = tiles[i][2 * p + h]
                his.append(jnp.where(tile_half == h, qh_ref[t], zero))
                los.append(jnp.where(tile_half == h, ql_ref[t], zero))
            lhs = two_part(jnp.concatenate(his, axis=0), jnp.concatenate(los, axis=0))
            both = mxu(lhs, pack_ref[i, :, 2 * p * LANES : 2 * (p + 1) * LANES], NT)
            hi, lo = split(both[: 2 * total] + both[2 * total :])
            at = slice(2 * p * total, 2 * (p + 1) * total)
            r_ref[i, at, :] = jnp.concatenate([hi, lo], axis=1)
        r_ref[i, slots * total :, :] = diagonal_term_ref[i]
    sign = jnp.where(lane_iota((total, (slots + 1) * total)) < slots * total, -1.0, 1.0)
    for i in range(rows):
        both = mxu(left_ref[i], r_ref[i], NT)
        s_ref[i, :total, :], s_ref[i, total:, :] = split((both[:total] + both[total:]) * sign)
    for i in range(rows):
        hot = [(even_ref if k % 2 == 0 else odd_ref)[tiles[i][k]] for k in range(slots)]
        both = mxu(s_ref[i], jnp.concatenate(hot + [even_ref[rows + i]], axis=0), NN)
        at = slice(i * total, (i + 1) * total)
        t_ref[at, :LANES], t_ref[at, LANES:] = split(both[:total] + both[total:])
    both = mxu(turned_ref[...], t_ref[...], NN)
    absolute = both[:, :LANES] + both[:, LANES:]
    relative = [
        pltpu.roll(absolute[n : n + 8], (BAND // 2 - 4 * rows + 1 + n) % LANES, 1, stride=1, stride_axis=0)
        for n in range(0, 3 * rows, 8)
    ]
    relative = jnp.concatenate(relative, axis=0)
    share = rows // ncol
    out_ref[...] = jnp.zeros_like(out_ref)
    for g in range(3):
        row = wrap(lax.axis_index("row") + (g - 1), nrow)
        for c in range(ncol):
            at = (3 - g) * rows - (c + 1) * share
            out_ref[row * ncol + c] = relative[at : at + share]


def sum_kernel(ncol, nrow, got_ref, out_ref):
    total = None
    for step in (-1, 0, 1):
        row = wrap(lax.axis_index("row") + step, nrow)
        for c in range(ncol):
            part = got_ref[row * ncol + c]
            total = part if total is None else total + part
    for n in range(total.shape[0]):
        out_ref[n : n + 1, :] = total[total.shape[0] - 1 - n : total.shape[0] - n]


HBM = pl.BlockSpec(memory_space=pltpu.HBM)
SMEM = pl.BlockSpec(memory_space=pltpu.SMEM)
VMEM = pl.BlockSpec(memory_space=pltpu.VMEM)
VMEM_LIMIT = 20 * 1024 * 1024
PACK_LIMIT = 51 * 1024 * 1024
CHUNKS = 6


def on_device(weights, block_cols, counts, near_null, prior_ridge):
    rows, slots, size, _ = weights.shape
    total = block_cols.shape[1]
    nrow, ncol = lax.axis_size("row"), lax.axis_size("col")
    all_rows = rows * nrow
    f32, bf16, i32 = jnp.float32, jnp.bfloat16, jnp.int32
    array = jax.ShapeDtypeStruct
    scratch = pltpu.VMEM

    def call(kernel, out_shape, specs, scratches, *operands, limit=VMEM_LIMIT):
        return pl.pallas_call(
            kernel, out_shape=out_shape, in_specs=specs,
            out_specs=jax.tree.map(lambda _: VMEM, out_shape), scratch_shapes=scratches,
            compiler_params=pltpu.CompilerParams(vmem_limit_bytes=limit),
        )(*operands)

    def send(x, to):
        pairs = []
        for r in range(nrow):
            for c in range(ncol):
                nr, nc = to(r, c)
                pairs.append((r * ncol + c, (nr % nrow) * ncol + nc))
        return lax.ppermute(x, ("row", "col"), pairs)

    def partner(x):
        return send(x, lambda r, c: (r, c ^ 1))

    def across(x):
        return send(x, lambda r, c: (r, c ^ 2))

    def outward(x, d=0):
        return send(x, lambda r, c: (r + (1 if c % 2 == 0 else -1), c ^ d))

    cols = block_cols.T
    null_mine = outward(near_null)
    cols_mine = outward(cols)
    packed = call(
        pack_kernel, array((rows, size, 2 * slots * size), bf16), [HBM],
        [scratch(weights.shape, f32), pltpu.SemaphoreType.DMA((CHUNKS if rows % CHUNKS == 0 else 1,))],
        weights, limit=PACK_LIMIT)
    targets = call(
        functools.partial(aim_kernel, all_rows), array((total, rows), i32), [VMEM] * 2, [],
        counts.reshape(1, rows), cols)
    null_other = partner(null_mine)
    cols_other = partner(cols_mine)
    count = (slots // 2) * rows + -(-rows // 16) * 8
    block, unit = call(
        functools.partial(unit_kernel, size),
        [array((count, LANES), f32), array((3 * rows + 8, LANES), f32)],
        [SMEM] + [VMEM] * 5, [scratch((8 * rows, size), f32)],
        targets, null_mine, null_other, near_null, prior_ridge, packed)
    hots = call(
        functools.partial(hot_kernel, slots, all_rows),
        [array((3 * rows + 1, total, LANES), bf16)] * 2 + [array((3 * rows, rows * total), bf16)],
        [VMEM] * 3,
        [scratch((3 * rows * total, LANES), f32)] * 2 + [scratch((rows * total, LANES), f32)],
        cols_mine, cols_other, cols)
    own = jnp.concatenate([block, partner(block)])
    diagonal = outward(own, 2)
    straight = outward(own)
    far = across(block)
    far_partner = partner(far)
    last = partner(jnp.concatenate([straight, diagonal]))
    ready = call(
        functools.partial(ready_kernel, size, slots),
        [array((2 * rows, total, LANES), bf16)] * 2
        + [array((rows, 2 * total, LANES), bf16), array((rows, total, LANES), bf16)],
        [VMEM] * 6, [scratch((rows * total, LANES), f32)],
        straight, diagonal, own, far, far_partner, unit)
    parts = call(
        functools.partial(coarse_kernel, size, ncol, nrow),
        array((nrow * ncol, rows // ncol, LANES), f32), [SMEM] + [VMEM] * 10,
        [
            scratch((rows * total // 2, LANES), f32),
            scratch((3 * rows + 1, total, LANES), bf16),
            scratch((3 * rows + 1, total, LANES), bf16),
            scratch((rows, (slots + 1) * total, LANES), bf16),
            scratch((rows, 2 * total, (slots + 1) * total), bf16),
            scratch((rows * total, 2 * LANES), bf16),
        ],
        targets, last, unit, *ready, *hots, packed)
    got = lax.all_to_all(parts, ("row", "col"), 0, 0)
    return call(
        functools.partial(sum_kernel, ncol, nrow), array((rows // ncol, LANES), f32), [VMEM], [], got)


def solution(mesh):
    placed = (P("row", "col", None, None), P("row", None), P("row"), P("row", None), P("row", None))

    return jax.shard_map(on_device, mesh=mesh, in_specs=placed, out_specs=P(("row", "col"), None), check_vma=False)
```

time: 46.2 us -> 47.7 us (1.032)
  waiting for transfers between devices: 19.4 us -> 22.4 us
  local copies, waits for them, and re-layouts: 1.37 us -> 0.02 us
  Pallas kernels: 8.23 us -> 7.37 us
  starting transfers between devices: 6.52 us -> 7.33 us
    ppermute x9 -> x10, waiting for transfers between devices: 19.4 us -> 22.4 us  [send(): return lax.ppermute(x, ('row', 'col'), pairs)]
    unnamed x9, local copies, waits for them, and re-layouts: 1.36 us -> 0.02 us
    pallas_call x5 -> x7, Pallas kernels: 8.23 us -> 7.37 us  [call(): pl.pallas_call(kernel, out_shape=out_shape, in_specs=specs, out_specs=jax...]
    ppermute x9 -> x10, starting transfers between devices: 6.52 us -> 7.33 us  [send(): return lax.ppermute(x, ('row', 'col'), pairs)]
  transfers between devices with their start and end apart: 9 -> 10, of which waited for: 7 -> 7; matrix products, arithmetic and copies ran while one was open for 0% -> 0% of each run, Pallas kernels for 6% -> 7%
where the time goes in v4:
time: 47.7 us; the launch traced here: 47.6 us
  waiting for transfers between devices  22.4 us (47%)
  blocking collectives  10.4 us (22%)
  Pallas kernels  7.37 us (15%)
  starting transfers between devices  7.33 us (15%)
    ppermute x10, waiting for transfers between devices, send(): return lax.ppermute(x, ('row', 'col'), pairs)  22.4 us
    all_to_all x1, blocking collectives, on_device(): got = lax.all_to_all(parts, ('row', 'col'), 0, 0)  10.4 us
    pallas_call x7, Pallas kernels, call(): pl.pallas_call(kernel, out_shape=out_shape, in_specs=specs, out_specs=jax...  7.37 us
    ppermute x10, starting transfers between devices, send(): return lax.ppermute(x, ('row', 'col'), pairs)  7.33 us
  transfers between devices with their start and end apart: 10, of which 7 were waited for; matrix products, arithmetic and copies ran while one was open for 0% of the time, Pallas kernels for 7%

profile of v4, /device:TPU:0, one launch (start us, length us, event | category | flops | bytes accessed | tf_op | source)
XLA Modules:
  0.0 47.6 jit_solution(8196794473230003369)
XLA Ops:
  0.0 0.0 copy-start.1
  0.0 0.0 copy-start
  0.0 0.0 copy-start.3
  0.0 0.0 copy-start.2
  0.0 3.1 %collective-permute-start = (f32[24,64]{1,0:T(8,128)}, f32[24,64]{1,0:T(8,128)S(1)}, u32[]{:S(2)}, u32[]{:S(2)}) collective-permute-start(f32[24,64]{1,0:T(8,128)} %own_ref.1), channel_id=1, source_target_pairs={{0,4},{1,29},{2,6},{3,31},{4,8},{5,1},{6,10},{7,3},{8,12},{9,5},{1... | collective-permute-start | bytes 18440 | tf_op jit(solution)/shard_map/ppermute | solution.py:318
  3.1 4.9 %collective-permute-done.mine_ref = f32[24,64]{1,0:T(8,128)S(1)} collective-permute-done((f32[24,64]{1,0:T(8,128)}, f32[24,64]{1,0:T(8,128)S(1)}, u32[]{:S(2)}, u32[]{:S(2)}) %collective-permute-start) | collective-permute-done | bytes 6176 | tf_op jit(solution)/shard_map/ppermute | solution.py:318
  8.0 0.0 collective-permute-start.1
  8.0 2.0 %shard_map.56.pack_ref = bf16[24,64,512]{2,1,0:T(8,128)(2,1)S(1)} custom-call(f32[24,4,64,64]{3,2,1,0:T(8,128)} %w_hbm.1), custom_call_target="tpu_custom_call" | custom-call | tf_op jit(solution)/shard_map/pallas_call | solution.py:306
  10.0 0.0 copy-done
  10.0 0.0 copy-done.3
  10.1 0.0 collective-permute-done.1.other_ref
  10.1 0.0 copy-done.1
  10.1 0.0 copy-done.2
  10.1 1.4 %shard_map.57 = (f32[64,128]{1,0:T(8,128)S(1)}, f32[80,128]{1,0:T(8,128)S(1)}) custom-call(s32[16,24]{1,0:T(8,128)S(1)} %shard_map.55.targets, f32[24,64]{1,0:T(8,128)S(1)} %collective-permute-done.mine_ref, f32[24,64]{1,0:T(8,128)S(1)} %collective-permute-done.1.other_ref, f32[24,64]{1,0:T(8,128)S(1)} %copy-done.1, f32[24,64]{1,0:T(8,128)S(1)} %copy-done.2, ...), custom_call_target="tpu_custom_call" | custom-call | tf_op jit(solution)/shard_map/pallas_call | solution.py:306
  11.5 0.5 %collective-permute-start.2 = (f32[64,128]{1,0:T(8,128)S(1)}, f32[64,128]{1,0:T(8,128)S(1)}, u32[]{:S(2)}, u32[]{:S(2)}) collective-permute-start(f32[64,128]{1,0:T(8,128)S(1)} %get-tuple-element.14), channel_id=1, source_target_pairs={{0,1},{1,0},{2,3},{3,2},{4,5},{5,4},{6,7},{7,6},{8,9},{9,8},{10,11... | collective-permute-start | bytes 98312 | tf_op jit(solution)/shard_map/ppermute | solution.py:318
  12.1 0.9 %collective-permute-done.2 = f32[64,128]{1,0:T(8,128)S(1)} collective-permute-done((f32[64,128]{1,0:T(8,128)S(1)}, f32[64,128]{1,0:T(8,128)S(1)}, u32[]{:S(2)}, u32[]{:S(2)}) %collective-permute-start.2) | collective-permute-done | bytes 32800 | tf_op jit(solution)/shard_map/ppermute | solution.py:318
  12.9 0.0 collective-permute-start.3
  12.9 2.3 %collective-permute-start.4 = (f32[128,128]{1,0:T(8,128)S(1)}, f32[128,128]{1,0:T(8,128)S(1)}, u32[]{:S(2)}, u32[]{:S(2)}) collective-permute-start(f32[128,128]{1,0:T(8,128)S(1)} %constant_dynamic-update-slice_fusion.own_ref), channel_id=1, source_target_pairs={{0,6},{1,31},{2,4},{3,29},{4,10},{5,3},{6,8},{7,1},{8,14},{9,7},{1... | collective-permute-start | bytes 196616 | tf_op jit(solution)/shard_map/ppermute | solution.py:318
  15.3 5.0 %collective-permute-done.3.straight_ref = f32[128,128]{1,0:T(8,128)S(1)} collective-permute-done((f32[128,128]{1,0:T(8,128)S(1)}, f32[128,128]{1,0:T(8,128)S(1)}, u32[]{:S(2)}, u32[]{:S(2)}) %collective-permute-start.3) | collective-permute-done | bytes 65568 | tf_op jit(solution)/shard_map/ppermute | solution.py:318
  20.2 1.4 %collective-permute-done.4.diagonal_ref = f32[128,128]{1,0:T(8,128)S(1)} collective-permute-done((f32[128,128]{1,0:T(8,128)S(1)}, f32[128,128]{1,0:T(8,128)S(1)}, u32[]{:S(2)}, u32[]{:S(2)}) %collective-permute-start.4) | collective-permute-done | bytes 65568 | tf_op jit(solution)/shard_map/ppermute | solution.py:318
  21.7 0.1 collective-permute-start.5
  21.8 1.3 %collective-permute-start.6 = (f32[64,128]{1,0:T(8,128)S(1)}, f32[64,128]{1,0:T(8,128)S(1)}, u32[]{:S(2)}, u32[]{:S(2)}) collective-permute-start(f32[64,128]{1,0:T(8,128)S(1)} %get-tuple-element.14), channel_id=1, source_target_pairs={{0,2},{1,3},{2,0},{3,1},{4,6},{5,7},{6,4},{7,5},{8,10},{9,11},{10,... | collective-permute-start | bytes 98312 | tf_op jit(solution)/shard_map/ppermute | solution.py:318
  23.1 2.6 %collective-permute-done.6.far_ref = f32[64,128]{1,0:T(8,128)S(1)} collective-permute-done((f32[64,128]{1,0:T(8,128)S(1)}, f32[64,128]{1,0:T(8,128)S(1)}, u32[]{:S(2)}, u32[]{:S(2)}) %collective-permute-start.6) | collective-permute-done | bytes 32800 | tf_op jit(solution)/shard_map/ppermute | solution.py:318
  25.8 0.0 collective-permute-start.7
  25.8 0.0 collective-permute-start.8
  25.8 6.3 %collective-permute-done.8.mine_ref = s32[16,24]{1,0:T(8,128)S(1)} collective-permute-done((s32[16,24]{1,0:T(8,128)S(1)}, s32[16,24]{1,0:T(8,128)S(1)}, u32[]{:S(2)}, u32[]{:S(2)}) %collective-permute-start.8) | collective-permute-done | bytes 1568 | tf_op jit(solution)/shard_map/ppermute | solution.py:318
  32.1 0.0 collective-permute-start.9
  32.1 1.2 %collective-permute-done.9.other_ref = s32[16,24]{1,0:T(8,128)S(1)} collective-permute-done((s32[16,24]{1,0:T(8,128)S(1)}, s32[16,24]{1,0:T(8,128)S(1)}, u32[]{:S(2)}, u32[]{:S(2)}) %collective-permute-start.9) | collective-permute-done | bytes 1568 | tf_op jit(solution)/shard_map/ppermute | solution.py:318
  33.3 0.9 %shard_map.59 = (bf16[73,16,128]{2,1,0:T(8,128)(2,1)S(1)}, bf16[73,16,128]{2,1,0:T(8,128)(2,1)S(1)}, bf16[72,384]{1,0:T(8,128)(2,1)S(1)}) custom-call(s32[16,24]{1,0:T(8,128)S(1)} %collective-permute-done.8.mine_ref, s32[16,24]{1,0:T(8,128)S(1)} %collective-permute-done.9.other_ref, s32[16,24]{1,0:T(8,128)S(1)} %bitcast.4), custom_call_target="tpu_custom_call" | custom-call | tf_op jit(solution)/shard_map/pallas_call | solution.py:306
  34.2 0.0 collective-permute-done.7.far_partner_ref
  34.2 0.3 shard_map.58
  34.5 0.0 collective-permute-done.5.last_ref
  34.5 2.1 %shard_map.60 = f32[32,6,128]{2,1,0:T(8,128)S(1)} custom-call(s32[16,24]{1,0:T(8,128)S(1)} %shard_map.55.targets, f32[256,128]{1,0:T(8,128)S(1)} %collective-permute-done.5.last_ref, f32[80,128]{1,0:T(8,128)S(1)} %get-tuple-element.15.unit_ref, bf16[48,16,128]{2,1,0:T(8,128)(2,1)S(1)} %get-tuple-element.16.ready_h_ref, ...), custom_call_target="tpu_custom_call" | custom-call | tf_op jit(solution)/shard_map/pallas_call | solution.py:306
  36.6 10.4 %all_to_all.5.got_ref = f32[32,6,128]{2,1,0:T(8,128)S(1)} all-to-all(f32[32,6,128]{2,1,0:T(8,128)S(1)} %shard_map.60), channel_id=1, replica_groups=mesh['row'=8,'col'=4] {'row','col'}, dimensions={0} | all-to-all | bytes 196608 | tf_op jit(solution)/shard_map/all_to_all | solution.py:377
  47.0 0.6 %shard_map.61 = f32[6,128]{1,0:T(8,128)} custom-call(f32[32,6,128]{2,1,0:T(8,128)S(1)} %all_to_all.5.got_ref), custom_call_target="tpu_custom_call" | custom-call | tf_op jit(solution)/shard_map/pallas_call | solution.py:306
  (4 shorter events, 0.0 us)
Async XLA Ops:
  0.0 10.1 %copy-start.1 = (f32[24,64]{1,0:T(8,128)S(1)}, f32[24,64]{1,0:T(8,128)}, u32[]{:S(2)}) copy-start(f32[24,64]{1,0:T(8,128)} %own_ref.1) | copy-start | bytes 18436
  0.0 10.0 %copy-start = (s32[24,16]{0,1:T(8,128)S(1)}, s32[24,16]{0,1:T(8,128)}, u32[]{:S(2)}) copy-start(s32[24,16]{0,1:T(8,128)} %param.6) | copy-start | bytes 4612
  0.0 10.0 %copy-start.3 = (s32[24]{0:T(128)S(1)}, s32[24]{0:T(128)}, u32[]{:S(2)}) copy-start(s32[24]{0:T(128)} %param.7) | copy-start | bytes 292
  0.0 10.1 %copy-start.2 = (f32[24,64]{1,0:T(8,128)S(1)}, f32[24,64]{1,0:T(8,128)}, u32[]{:S(2)}) copy-start(f32[24,64]{1,0:T(8,128)} %ridge_ref.1) | copy-start | bytes 18436
  0.0 8.0 %collective-permute-start = (f32[24,64]{1,0:T(8,128)}, f32[24,64]{1,0:T(8,128)S(1)}, u32[]{:S(2)}, u32[]{:S(2)}) collective-permute-start(f32[24,64]{1,0:T(8,128)} %own_ref.1), channel_id=1, source_target_pairs={{0,4},{1,29},{2,6},{3,31},{4,8},{5,1},{6,10},{7,3},{8,12},{9,5},{1... | collective-permute-start | bytes 18440 | tf_op jit(solution)/shard_map/ppermute | solution.py:318
  8.0 2.1 %collective-permute-start.1 = (f32[24,64]{1,0:T(8,128)S(1)}, f32[24,64]{1,0:T(8,128)S(1)}, u32[]{:S(2)}, u32[]{:S(2)}) collective-permute-start(f32[24,64]{1,0:T(8,128)S(1)} %collective-permute-done.mine_ref), channel_id=1, source_target_pairs={{0,1},{1,0},{2,3},{3,2},{4,5},{5,4},{6,7},{7,6},{8,9},{9,8},{10,11... | collective-permute-start | bytes 18440 | tf_op jit(solution)/shard_map/ppermute | solution.py:318
  11.5 1.4 %collective-permute-start.2 = (f32[64,128]{1,0:T(8,128)S(1)}, f32[64,128]{1,0:T(8,128)S(1)}, u32[]{:S(2)}, u32[]{:S(2)}) collective-permute-start(f32[64,128]{1,0:T(8,128)S(1)} %get-tuple-element.14), channel_id=1, source_target_pairs={{0,1},{1,0},{2,3},{3,2},{4,5},{5,4},{6,7},{7,6},{8,9},{9,8},{10,11... | collective-permute-start | bytes 98312 | tf_op jit(solution)/shard_map/ppermute | solution.py:318
  12.9 7.3 %collective-permute-start.3 = (f32[128,128]{1,0:T(8,128)S(1)}, f32[128,128]{1,0:T(8,128)S(1)}, u32[]{:S(2)}, u32[]{:S(2)}) collective-permute-start(f32[128,128]{1,0:T(8,128)S(1)} %constant_dynamic-update-slice_fusion.own_ref), channel_id=1, source_target_pairs={{0,4},{1,29},{2,6},{3,31},{4,8},{5,1},{6,10},{7,3},{8,12},{9,5},{1... | collective-permute-start | bytes 196616 | tf_op jit(solution)/shard_map/ppermute | solution.py:318
  12.9 8.7 %collective-permute-start.4 = (f32[128,128]{1,0:T(8,128)S(1)}, f32[128,128]{1,0:T(8,128)S(1)}, u32[]{:S(2)}, u32[]{:S(2)}) collective-permute-start(f32[128,128]{1,0:T(8,128)S(1)} %constant_dynamic-update-slice_fusion.own_ref), channel_id=1, source_target_pairs={{0,6},{1,31},{2,4},{3,29},{4,10},{5,3},{6,8},{7,1},{8,14},{9,7},{1... | collective-permute-start | bytes 196616 | tf_op jit(solution)/shard_map/ppermute | solution.py:318
  21.7 12.8 %collective-permute-start.5 = (f32[256,128]{1,0:T(8,128)S(1)}, f32[256,128]{1,0:T(8,128)S(1)}, u32[]{:S(2)}, u32[]{:S(2)}) collective-permute-start(f32[256,128]{1,0:T(8,128)S(1)} %pad_maximum_fusion), channel_id=1, source_target_pairs={{0,1},{1,0},{2,3},{3,2},{4,5},{5,4},{6,7},{7,6},{8,9},{9,8},{10,11... | collective-permute-start | bytes 393224 | tf_op jit(solution)/shard_map/ppermute | solution.py:318
  21.8 4.0 %collective-permute-start.6 = (f32[64,128]{1,0:T(8,128)S(1)}, f32[64,128]{1,0:T(8,128)S(1)}, u32[]{:S(2)}, u32[]{:S(2)}) collective-permute-start(f32[64,128]{1,0:T(8,128)S(1)} %get-tuple-element.14), channel_id=1, source_target_pairs={{0,2},{1,3},{2,0},{3,1},{4,6},{5,7},{6,4},{7,5},{8,10},{9,11},{10,... | collective-permute-start | bytes 98312 | tf_op jit(solution)/shard_map/ppermute | solution.py:318
  25.8 8.4 %collective-permute-start.7 = (f32[64,128]{1,0:T(8,128)S(1)}, f32[64,128]{1,0:T(8,128)S(1)}, u32[]{:S(2)}, u32[]{:S(2)}) collective-permute-start(f32[64,128]{1,0:T(8,128)S(1)} %collective-permute-done.6.far_ref), channel_id=1, source_target_pairs={{0,1},{1,0},{2,3},{3,2},{4,5},{5,4},{6,7},{7,6},{8,9},{9,8},{10,11... | collective-permute-start | bytes 98312 | tf_op jit(solution)/shard_map/ppermute | solution.py:318
  25.8 6.3 %collective-permute-start.8 = (s32[16,24]{1,0:T(8,128)S(1)}, s32[16,24]{1,0:T(8,128)S(1)}, u32[]{:S(2)}, u32[]{:S(2)}) collective-permute-start(s32[16,24]{1,0:T(8,128)S(1)} %bitcast.3), channel_id=1, source_target_pairs={{0,4},{1,29},{2,6},{3,31},{4,8},{5,1},{6,10},{7,3},{8,12},{9,5},{1... | collective-permute-start | bytes 4616 | tf_op jit(solution)/shard_map/ppermute | solution.py:318
  32.1 1.2 %collective-permute-start.9 = (s32[16,24]{1,0:T(8,128)S(1)}, s32[16,24]{1,0:T(8,128)S(1)}, u32[]{:S(2)}, u32[]{:S(2)}) collective-permute-start(s32[16,24]{1,0:T(8,128)S(1)} %collective-permute-done.8.mine_ref), channel_id=1, source_target_pairs={{0,1},{1,0},{2,3},{3,2},{4,5},{5,4},{6,7},{7,6},{8,9},{9,8},{10,11... | collective-permute-start | bytes 4616 | tf_op jit(solution)/shard_map/ppermute | solution.py:318

commit v5 on v4

--- a/solution.py
+++ b/solution.py
@@ -72,18 +72,18 @@
     return jnp.concatenate([top, jnp.concatenate([lo, jnp.zeros_like(lo)], axis=1)], axis=0)
 
 
-def aim_kernel(all_rows, counts_ref, cols_ref, target_ref):
-    total, rows = cols_ref.shape
+def aim(all_rows, counts, cols):
+    total, rows = cols.shape
     local = lane_iota((total, rows))
     first = lax.axis_index("row") * rows
-    at = wrap(cols_ref[...] - (first + local) + H, all_rows) + (rows - H) + local
+    at = wrap(cols - (first + local) + H, all_rows) + (rows - H) + local
     mirror = jnp.where(at < rows, at + 2 * rows, jnp.where(at >= 2 * rows, at - 2 * rows, at))
     at = jnp.where(lax.axis_index("col") % 2 == 0, at, mirror)
-    target_ref[...] = jnp.where(row_iota((total, rows)) < counts_ref[...], at, 3 * rows)
+    return jnp.where(row_iota((total, rows)) < counts[None, :], at, 3 * rows)
 
 
 def unit_kernel(size, targets, mine_ref, other_ref, own_ref, ridge_ref, pack_ref,
-                block_ref, unit_ref, acc_ref):
+                block_ref, unit_ref, acc_ref, one_ref):
     rows = own_ref.shape[0]
     slots = pack_ref.shape[2] // (2 * size)
     column = lax.axis_index("col")
@@ -92,6 +92,8 @@
         unit = x / jnp.sqrt(jnp.sum(x * x, axis=1, keepdims=True) + epsilon)
         unit_ref[g * rows : (g + 1) * rows, :] = jnp.concatenate([unit, unit], axis=1)
     unit_ref[3 * rows :, :] = jnp.zeros((8, LANES), jnp.float32)
+    one_ref[: 3 * rows, :] = jnp.ones((3 * rows, LANES), jnp.float32)
+    one_ref[3 * rows :, :] = jnp.zeros((8, LANES), jnp.float32)
     row8 = row_iota((8, LANES))
     half = lane_iota((8, LANES)) // size
     for i in range(rows):
@@ -102,7 +104,7 @@
                 k = 2 * p + h
                 t = targets[column * slots + k, i]
                 vec = jnp.broadcast_to(unit_ref[pl.ds(t, 1), :], (8, LANES))
-                one = jnp.where(t < 3 * rows, 1.0, 0.0)
+                one = jnp.broadcast_to(one_ref[pl.ds(t, 1), :], (8, LANES))
                 tile = jnp.where((row8 == k) & (half == h), vec, tile)
                 tile = jnp.where((row8 == slots) & (half == h), one, tile)
             term = mxu(two_part(*split(tile)), pack_ref[i, :, 2 * p * LANES : 2 * (p + 1) * LANES], NT)
@@ -298,7 +300,7 @@
     total = block_cols.shape[1]
     nrow, ncol = lax.axis_size("row"), lax.axis_size("col")
     all_rows = rows * nrow
-    f32, bf16, i32 = jnp.float32, jnp.bfloat16, jnp.int32
+    f32, bf16 = jnp.float32, jnp.bfloat16
     array = jax.ShapeDtypeStruct
     scratch = pltpu.VMEM
 
@@ -333,16 +335,14 @@
         pack_kernel, array((rows, size, 2 * slots * size), bf16), [HBM],
         [scratch(weights.shape, f32), pltpu.SemaphoreType.DMA((CHUNKS if rows % CHUNKS == 0 else 1,))],
         weights, limit=PACK_LIMIT)
-    targets = call(
-        functools.partial(aim_kernel, all_rows), array((total, rows), i32), [VMEM] * 2, [],
-        counts.reshape(1, rows), cols)
+    targets = aim(all_rows, counts, cols)
     null_other = partner(null_mine)
     cols_other = partner(cols_mine)
     count = (slots // 2) * rows + -(-rows // 16) * 8
     block, unit = call(
         functools.partial(unit_kernel, size),
         [array((count, LANES), f32), array((3 * rows + 8, LANES), f32)],
-        [SMEM] + [VMEM] * 5, [scratch((8 * rows, size), f32)],
+        [SMEM] + [VMEM] * 5, [scratch((8 * rows, size), f32), scratch((3 * rows + 8, LANES), f32)],
         targets, null_mine, null_other, near_null, prior_ridge, packed)
     hots = call(
         functools.partial(hot_kernel, slots, all_rows),

time: 47.7 us -> 48.5 us (1.017)
  other arithmetic: 0.01 us -> 0.74 us
    select_n x0 -> x1, other arithmetic: none -> 0.73 us  [aim(): return jnp.where(row_iota((total, rows)) < counts[None, :], at, 3 * rows)]
    pallas_call x7 -> x6, Pallas kernels: 7.37 us -> 7.37 us  [call(): pl.pallas_call(kernel, out_shape=out_shape, in_specs=specs, out_specs=jax...]
  transfers between devices with their start and end apart: 10 -> 10, of which waited for: 7 -> 7; matrix products, arithmetic and copies ran while one was open for 0% -> 2% of each run, Pallas kernels for 7% -> 7%
where the time goes in v5:
time: 48.5 us; the launch traced here: 48.2 us
  waiting for transfers between devices  22.4 us (46%)
  blocking collectives  10.4 us (21%)
  Pallas kernels  7.37 us (15%)
  starting transfers between devices  7.21 us (15%)
  other arithmetic  0.74 us (2%)
    ppermute x10, waiting for transfers between devices, send(): return lax.ppermute(x, ('row', 'col'), pairs)  22.4 us
    all_to_all x1, blocking collectives, on_device(): got = lax.all_to_all(parts, ('row', 'col'), 0, 0)  10.4 us
    pallas_call x6, Pallas kernels, call(): pl.pallas_call(kernel, out_shape=out_shape, in_specs=specs, out_specs=jax...  7.37 us
    ppermute x10, starting transfers between devices, send(): return lax.ppermute(x, ('row', 'col'), pairs)  7.21 us
  transfers between devices with their start and end apart: 10, of which 7 were waited for; matrix products, arithmetic and copies ran while one was open for 2% of the time, Pallas kernels for 7%

profile of v5, /device:TPU:0, one launch (start us, length us, event | category | flops | bytes accessed | tf_op | source)
XLA Modules:
  0.0 48.2 jit_solution(8924608944181795441)
XLA Ops:
  0.0 0.0 copy-start.1
  0.0 0.0 copy-start.2
  0.0 3.0 %collective-permute-start = (f32[24,64]{1,0:T(8,128)}, f32[24,64]{1,0:T(8,128)S(1)}, u32[]{:S(2)}, u32[]{:S(2)}) collective-permute-start(f32[24,64]{1,0:T(8,128)} %own_ref.1), channel_id=1, source_target_pairs={{0,4},{1,29},{2,6},{3,31},{4,8},{5,1},{6,10},{7,3},{8,12},{9,5},{1... | collective-permute-start | bytes 18440 | tf_op jit(solution)/shard_map/ppermute | solution.py:320
  3.0 5.0 %collective-permute-done.mine_ref = f32[24,64]{1,0:T(8,128)S(1)} collective-permute-done((f32[24,64]{1,0:T(8,128)}, f32[24,64]{1,0:T(8,128)S(1)}, u32[]{:S(2)}, u32[]{:S(2)}) %collective-permute-start) | collective-permute-done | bytes 6176 | tf_op jit(solution)/shard_map/ppermute | solution.py:320
  8.0 0.0 collective-permute-start.1
  8.0 0.7 %fusion.4.targets = s32[16,24]{1,0:T(8,128)S(1)} fusion(s32[24]{0:T(128)S(1)} %iota_add_fusion, s32[24]{0:T(128)} %param.7, pred[]{:T(512)S(6)} %eq.5, s32[24,16]{0,1:T(8,128)} %param.6), kind=kLoop, calls=%fused_computation.8 | loop fusion | flops 7296 | bytes 3265 | tf_op jit(solution)/shard_map/jit(_where)/select_n | solution.py:82
  8.7 0.0 copy-start
  8.7 2.0 %shard_map.55.pack_ref = bf16[24,64,512]{2,1,0:T(8,128)(2,1)S(1)} custom-call(f32[24,4,64,64]{3,2,1,0:T(8,128)} %w_hbm.1), custom_call_target="tpu_custom_call" | custom-call | tf_op jit(solution)/shard_map/pallas_call | solution.py:308
  10.8 0.0 collective-permute-done.1.other_ref
  10.8 0.0 copy-done.1
  10.8 0.0 copy-done.2
  10.8 1.4 %shard_map.56 = (f32[64,128]{1,0:T(8,128)S(1)}, f32[80,128]{1,0:T(8,128)S(1)}) custom-call(s32[16,24]{1,0:T(8,128)S(1)} %fusion.4.targets, f32[24,64]{1,0:T(8,128)S(1)} %collective-permute-done.mine_ref, f32[24,64]{1,0:T(8,128)S(1)} %collective-permute-done.1.other_ref, f32[24,64]{1,0:T(8,128)S(1)} %copy-done.1, f32[24,64]{1,0:T(8,128)S(1)} %copy-done.2, ...), custom_call_target="tpu_custom_call" | custom-call | tf_op jit(solution)/shard_map/pallas_call | solution.py:308
  12.2 0.5 %collective-permute-start.2 = (f32[64,128]{1,0:T(8,128)S(1)}, f32[64,128]{1,0:T(8,128)S(1)}, u32[]{:S(2)}, u32[]{:S(2)}) collective-permute-start(f32[64,128]{1,0:T(8,128)S(1)} %get-tuple-element.14), channel_id=1, source_target_pairs={{0,1},{1,0},{2,3},{3,2},{4,5},{5,4},{6,7},{7,6},{8,9},{9,8},{10,11... | collective-permute-start | bytes 98312 | tf_op jit(solution)/shard_map/ppermute | solution.py:320
  12.8 0.9 %collective-permute-done.2 = f32[64,128]{1,0:T(8,128)S(1)} collective-permute-done((f32[64,128]{1,0:T(8,128)S(1)}, f32[64,128]{1,0:T(8,128)S(1)}, u32[]{:S(2)}, u32[]{:S(2)}) %collective-permute-start.2) | collective-permute-done | bytes 32800 | tf_op jit(solution)/shard_map/ppermute | solution.py:320
  13.6 0.0 collective-permute-start.3
  13.7 2.3 %collective-permute-start.4 = (f32[128,128]{1,0:T(8,128)S(1)}, f32[128,128]{1,0:T(8,128)S(1)}, u32[]{:S(2)}, u32[]{:S(2)}) collective-permute-start(f32[128,128]{1,0:T(8,128)S(1)} %constant_dynamic-update-slice_fusion.own_ref), channel_id=1, source_target_pairs={{0,6},{1,31},{2,4},{3,29},{4,10},{5,3},{6,8},{7,1},{8,14},{9,7},{1... | collective-permute-start | bytes 196616 | tf_op jit(solution)/shard_map/ppermute | solution.py:320
  15.9 5.1 %collective-permute-done.3.straight_ref = f32[128,128]{1,0:T(8,128)S(1)} collective-permute-done((f32[128,128]{1,0:T(8,128)S(1)}, f32[128,128]{1,0:T(8,128)S(1)}, u32[]{:S(2)}, u32[]{:S(2)}) %collective-permute-start.3) | collective-permute-done | bytes 65568 | tf_op jit(solution)/shard_map/ppermute | solution.py:320
  21.0 1.3 %collective-permute-done.4.diagonal_ref = f32[128,128]{1,0:T(8,128)S(1)} collective-permute-done((f32[128,128]{1,0:T(8,128)S(1)}, f32[128,128]{1,0:T(8,128)S(1)}, u32[]{:S(2)}, u32[]{:S(2)}) %collective-permute-start.4) | collective-permute-done | bytes 65568 | tf_op jit(solution)/shard_map/ppermute | solution.py:320
  22.3 0.1 collective-permute-start.5
  22.4 1.3 %collective-permute-start.6 = (f32[64,128]{1,0:T(8,128)S(1)}, f32[64,128]{1,0:T(8,128)S(1)}, u32[]{:S(2)}, u32[]{:S(2)}) collective-permute-start(f32[64,128]{1,0:T(8,128)S(1)} %get-tuple-element.14), channel_id=1, source_target_pairs={{0,2},{1,3},{2,0},{3,1},{4,6},{5,7},{6,4},{7,5},{8,10},{9,11},{10,... | collective-permute-start | bytes 98312 | tf_op jit(solution)/shard_map/ppermute | solution.py:320
  23.8 2.6 %collective-permute-done.6.far_ref = f32[64,128]{1,0:T(8,128)S(1)} collective-permute-done((f32[64,128]{1,0:T(8,128)S(1)}, f32[64,128]{1,0:T(8,128)S(1)}, u32[]{:S(2)}, u32[]{:S(2)}) %collective-permute-start.6) | collective-permute-done | bytes 32800 | tf_op jit(solution)/shard_map/ppermute | solution.py:320
  26.4 0.0 collective-permute-start.7
  26.4 0.0 copy-done
  26.4 0.0 collective-permute-start.8
  26.4 6.3 %collective-permute-done.8.mine_ref = s32[16,24]{1,0:T(8,128)S(1)} collective-permute-done((s32[16,24]{1,0:T(8,128)S(1)}, s32[16,24]{1,0:T(8,128)S(1)}, u32[]{:S(2)}, u32[]{:S(2)}) %collective-permute-start.8) | collective-permute-done | bytes 1568 | tf_op jit(solution)/shard_map/ppermute | solution.py:320
  32.8 0.0 collective-permute-start.9
  32.8 1.2 %collective-permute-done.9.other_ref = s32[16,24]{1,0:T(8,128)S(1)} collective-permute-done((s32[16,24]{1,0:T(8,128)S(1)}, s32[16,24]{1,0:T(8,128)S(1)}, u32[]{:S(2)}, u32[]{:S(2)}) %collective-permute-start.9) | collective-permute-done | bytes 1568 | tf_op jit(solution)/shard_map/ppermute | solution.py:320
  33.9 0.9 %shard_map.58 = (bf16[73,16,128]{2,1,0:T(8,128)(2,1)S(1)}, bf16[73,16,128]{2,1,0:T(8,128)(2,1)S(1)}, bf16[72,384]{1,0:T(8,128)(2,1)S(1)}) custom-call(s32[16,24]{1,0:T(8,128)S(1)} %collective-permute-done.8.mine_ref, s32[16,24]{1,0:T(8,128)S(1)} %collective-permute-done.9.other_ref, s32[16,24]{1,0:T(8,128)S(1)} %bitcast.3), custom_call_target="tpu_custom_call" | custom-call | tf_op jit(solution)/shard_map/pallas_call | solution.py:308
  34.8 0.0 collective-permute-done.7.far_partner_ref
  34.8 0.3 shard_map.57
  35.2 0.0 collective-permute-done.5.last_ref
  35.2 2.1 %shard_map.59 = f32[32,6,128]{2,1,0:T(8,128)S(1)} custom-call(s32[16,24]{1,0:T(8,128)S(1)} %fusion.4.targets, f32[256,128]{1,0:T(8,128)S(1)} %collective-permute-done.5.last_ref, f32[80,128]{1,0:T(8,128)S(1)} %get-tuple-element.15.unit_ref, bf16[48,16,128]{2,1,0:T(8,128)(2,1)S(1)} %get-tuple-element.16.ready_h_ref, ...), custom_call_target="tpu_custom_call" | custom-call | tf_op jit(solution)/shard_map/pallas_call | solution.py:308
  37.3 10.4 %all_to_all.5.got_ref = f32[32,6,128]{2,1,0:T(8,128)S(1)} all-to-all(f32[32,6,128]{2,1,0:T(8,128)S(1)} %shard_map.59), channel_id=1, replica_groups=mesh['row'=8,'col'=4] {'row','col'}, dimensions={0} | all-to-all | bytes 196608 | tf_op jit(solution)/shard_map/all_to_all | solution.py:377
  47.6 0.6 %shard_map.60 = f32[6,128]{1,0:T(8,128)} custom-call(f32[32,6,128]{2,1,0:T(8,128)S(1)} %all_to_all.5.got_ref), custom_call_target="tpu_custom_call" | custom-call | tf_op jit(solution)/shard_map/pallas_call | solution.py:308
  (4 shorter events, 0.0 us)
Async XLA Ops:
  0.0 10.8 %copy-start.1 = (f32[24,64]{1,0:T(8,128)S(1)}, f32[24,64]{1,0:T(8,128)}, u32[]{:S(2)}) copy-start(f32[24,64]{1,0:T(8,128)} %own_ref.1) | copy-start | bytes 18436
  0.0 10.8 %copy-start.2 = (f32[24,64]{1,0:T(8,128)S(1)}, f32[24,64]{1,0:T(8,128)}, u32[]{:S(2)}) copy-start(f32[24,64]{1,0:T(8,128)} %ridge_ref.1) | copy-start | bytes 18436
  0.0 8.0 %collective-permute-start = (f32[24,64]{1,0:T(8,128)}, f32[24,64]{1,0:T(8,128)S(1)}, u32[]{:S(2)}, u32[]{:S(2)}) collective-permute-start(f32[24,64]{1,0:T(8,128)} %own_ref.1), channel_id=1, source_target_pairs={{0,4},{1,29},{2,6},{3,31},{4,8},{5,1},{6,10},{7,3},{8,12},{9,5},{1... | collective-permute-start | bytes 18440 | tf_op jit(solution)/shard_map/ppermute | solution.py:320
  8.0 2.8 %collective-permute-start.1 = (f32[24,64]{1,0:T(8,128)S(1)}, f32[24,64]{1,0:T(8,128)S(1)}, u32[]{:S(2)}, u32[]{:S(2)}) collective-permute-start(f32[24,64]{1,0:T(8,128)S(1)} %collective-permute-done.mine_ref), channel_id=1, source_target_pairs={{0,1},{1,0},{2,3},{3,2},{4,5},{5,4},{6,7},{7,6},{8,9},{9,8},{10,11... | collective-permute-start | bytes 18440 | tf_op jit(solution)/shard_map/ppermute | solution.py:320
  8.7 17.7 %copy-start = (s32[24,16]{0,1:T(8,128)S(1)}, s32[24,16]{0,1:T(8,128)}, u32[]{:S(2)}) copy-start(s32[24,16]{0,1:T(8,128)} %param.6) | copy-start | bytes 4612
  12.2 1.4 %collective-permute-start.2 = (f32[64,128]{1,0:T(8,128)S(1)}, f32[64,128]{1,0:T(8,128)S(1)}, u32[]{:S(2)}, u32[]{:S(2)}) collective-permute-start(f32[64,128]{1,0:T(8,128)S(1)} %get-tuple-element.14), channel_id=1, source_target_pairs={{0,1},{1,0},{2,3},{3,2},{4,5},{5,4},{6,7},{7,6},{8,9},{9,8},{10,11... | collective-permute-start | bytes 98312 | tf_op jit(solution)/shard_map/ppermute | solution.py:320
  13.6 7.4 %collective-permute-start.3 = (f32[128,128]{1,0:T(8,128)S(1)}, f32[128,128]{1,0:T(8,128)S(1)}, u32[]{:S(2)}, u32[]{:S(2)}) collective-permute-start(f32[128,128]{1,0:T(8,128)S(1)} %constant_dynamic-update-slice_fusion.own_ref), channel_id=1, source_target_pairs={{0,4},{1,29},{2,6},{3,31},{4,8},{5,1},{6,10},{7,3},{8,12},{9,5},{1... | collective-permute-start | bytes 196616 | tf_op jit(solution)/shard_map/ppermute | solution.py:320
  13.7 8.7 %collective-permute-start.4 = (f32[128,128]{1,0:T(8,128)S(1)}, f32[128,128]{1,0:T(8,128)S(1)}, u32[]{:S(2)}, u32[]{:S(2)}) collective-permute-start(f32[128,128]{1,0:T(8,128)S(1)} %constant_dynamic-update-slice_fusion.own_ref), channel_id=1, source_target_pairs={{0,6},{1,31},{2,4},{3,29},{4,10},{5,3},{6,8},{7,1},{8,14},{9,7},{1... | collective-permute-start | bytes 196616 | tf_op jit(solution)/shard_map/ppermute | solution.py:320
  22.3 12.8 %collective-permute-start.5 = (f32[256,128]{1,0:T(8,128)S(1)}, f32[256,128]{1,0:T(8,128)S(1)}, u32[]{:S(2)}, u32[]{:S(2)}) collective-permute-start(f32[256,128]{1,0:T(8,128)S(1)} %pad_maximum_fusion), channel_id=1, source_target_pairs={{0,1},{1,0},{2,3},{3,2},{4,5},{5,4},{6,7},{7,6},{8,9},{9,8},{10,11... | collective-permute-start | bytes 393224 | tf_op jit(solution)/shard_map/ppermute | solution.py:320
  22.4 4.0 %collective-permute-start.6 = (f32[64,128]{1,0:T(8,128)S(1)}, f32[64,128]{1,0:T(8,128)S(1)}, u32[]{:S(2)}, u32[]{:S(2)}) collective-permute-start(f32[64,128]{1,0:T(8,128)S(1)} %get-tuple-element.14), channel_id=1, source_target_pairs={{0,2},{1,3},{2,0},{3,1},{4,6},{5,7},{6,4},{7,5},{8,10},{9,11},{10,... | collective-permute-start | bytes 98312 | tf_op jit(solution)/shard_map/ppermute | solution.py:320
  26.4 8.4 %collective-permute-start.7 = (f32[64,128]{1,0:T(8,128)S(1)}, f32[64,128]{1,0:T(8,128)S(1)}, u32[]{:S(2)}, u32[]{:S(2)}) collective-permute-start(f32[64,128]{1,0:T(8,128)S(1)} %collective-permute-done.6.far_ref), channel_id=1, source_target_pairs={{0,1},{1,0},{2,3},{3,2},{4,5},{5,4},{6,7},{7,6},{8,9},{9,8},{10,11... | collective-permute-start | bytes 98312 | tf_op jit(solution)/shard_map/ppermute | solution.py:320
  26.4 6.3 %collective-permute-start.8 = (s32[16,24]{1,0:T(8,128)S(1)}, s32[16,24]{1,0:T(8,128)S(1)}, u32[]{:S(2)}, u32[]{:S(2)}) collective-permute-start(s32[16,24]{1,0:T(8,128)S(1)} %bitcast.2), channel_id=1, source_target_pairs={{0,4},{1,29},{2,6},{3,31},{4,8},{5,1},{6,10},{7,3},{8,12},{9,5},{1... | collective-permute-start | bytes 4616 | tf_op jit(solution)/shard_map/ppermute | solution.py:320
  32.8 1.2 %collective-permute-start.9 = (s32[16,24]{1,0:T(8,128)S(1)}, s32[16,24]{1,0:T(8,128)S(1)}, u32[]{:S(2)}, u32[]{:S(2)}) collective-permute-start(s32[16,24]{1,0:T(8,128)S(1)} %collective-permute-done.8.mine_ref), channel_id=1, source_target_pairs={{0,1},{1,0},{2,3},{3,2},{4,5},{5,4},{6,7},{7,6},{8,9},{9,8},{10,11... | collective-permute-start | bytes 4616 | tf_op jit(solution)/shard_map/ppermute | solution.py:320

commit v6 on v5

--- a/solution.py
+++ b/solution.py
@@ -188,41 +188,54 @@
     return rows_of
 
 
-def ready_kernel(size, slots, straight_ref, diagonal_ref, own_ref, far_ref, far_partner_ref, unit_ref,
-                 qh_ref, ql_ref, left_ref, diagonal_term_ref, p_ref):
+def own_kernel(size, own_ref, far_ref, far_partner_ref, unit_ref, pack_ref,
+               qh_ref, ql_ref, v_ref, diagonal_ref, p_ref):
+    rows, total, _ = qh_ref.shape
+    slots = pack_ref.shape[2] // (2 * size)
     count = far_ref.shape[0]
-    rows, total, _ = diagonal_term_ref.shape
-    column = lax.axis_index("col")
     degree = own_ref[(slots // 2) * rows : count, :]
     degree = jnp.concatenate([degree, roll(degree, size)[: rows - degree.shape[0]]], axis=0)
     low_half = lane_iota((total, LANES)) < size
-    groups = (
-        [(straight_ref, 0), (straight_ref, 1), (diagonal_ref, 0), (diagonal_ref, 1)],
-        [(own_ref, 0), (own_ref, 1), (far_ref, 0), (far_partner_ref, 0)],
-    )
+    kept = []
+
+    def store(i, q):
+        hi, lo = split(q)
+        qh_ref[i], ql_ref[i] = hi, lo
+        term = q[:, :size] * degree[i : i + 1, :size]
+        kept.append((jnp.concatenate([hi[:, :size], lo[:, :size]], axis=0),
+                     jnp.where(low_half, q, roll(q, size)), jnp.concatenate(split(term), axis=1)))
+
+    group = [(own_ref, 0), (own_ref, 1), (far_ref, 0), (far_partner_ref, 0)]
+    blocks = [block_of(ref, index, count) for ref, index in group]
+    prolong_rows(blocks, unit_ref[rows : 2 * rows, :], lax.axis_index("col"), slots, size, p_ref, 0, store)
+    for i, (left, _, _) in enumerate(kept):
+        both = mxu(left, pack_ref[i], NN)
+        for p in range(slots // 2):
+            at = 2 * p * LANES
+            hi_lanes, lo_lanes = slice(at, at + LANES), slice(at + LANES, at + 2 * LANES)
+            v = both[:total, hi_lanes] + both[:total, lo_lanes] + both[total:, hi_lanes]
+            v_ref[i, :, at : at + 2 * LANES] = two_part(*split(-v))
+    for i, (_, doubled, term) in enumerate(kept):
+        hi, lo = split(doubled)
+        both = mxu(jnp.concatenate([hi, jnp.where(low_half, lo, jnp.zeros_like(lo))], axis=0), term, NT)
+        diagonal_ref[i] = jnp.concatenate(split(both[:total] + both[total:]), axis=0)
+
+
+def ready_kernel(size, slots, straight_ref, diagonal_ref, unit_ref, qh_ref, ql_ref, p_ref):
+    rows = qh_ref.shape[0]
+    count = straight_ref.shape[0] // 2
 
     def store(j, q):
         qh_ref[j], ql_ref[j] = split(q)
-        if j >= rows:
-            i = j - rows
-            hi, lo = split(jnp.where(low_half, q, roll(q, size)))
-            left_ref[i, :total, :] = hi
-            left_ref[i, total:, :] = jnp.where(low_half, lo, jnp.zeros_like(lo))
-            term = q[:, :size] * degree[i : i + 1, :size]
-            diagonal_term_ref[i] = jnp.concatenate(split(term), axis=1)
-
-    for g, group in enumerate(groups):
-        blocks = [block_of(ref, index, count) for ref, index in group]
-        unit = unit_ref[g * rows : (g + 1) * rows, :]
-        prolong_rows(blocks, unit, column, slots, size, p_ref, g * rows, store)
-
-
-def coarse_kernel(size, ncol, nrow, targets, last_ref, unit_ref, ready_h_ref, ready_l_ref, left_ref,
-                  diagonal_term_ref, even_ref, odd_ref, turned_ref, pack_ref, out_ref,
-                  p_ref, qh_ref, ql_ref, r_ref, s_ref, t_ref):
-    rows = pack_ref.shape[0]
-    slots = pack_ref.shape[2] // (2 * size)
-    total = slots * ncol
+
+    blocks = [block_of(ref, index, count) for ref in (straight_ref, diagonal_ref) for index in range(2)]
+    prolong_rows(blocks, unit_ref[:rows, :], lax.axis_index("col"), slots, size, p_ref, 0, store)
+
+
+def coarse_kernel(size, slots, ncol, nrow, targets, last_ref, unit_ref, own_h_ref, own_l_ref, v_ref,
+                  diagonal_ref, mine_h_ref, mine_l_ref, even_ref, odd_ref, turned_ref, out_ref,
+                  p_ref, qh_ref, ql_ref, s_ref, t_ref):
+    rows, total, _ = own_h_ref.shape
     pairs = slots // 2
     column = lax.axis_index("col")
     count = last_ref.shape[0] // ncol
@@ -232,29 +245,24 @@
 
     blocks = [block_of(last_ref, d ^ 1, count) for d in range(ncol)]
     prolong_rows(blocks, unit_ref[2 * rows : 3 * rows, :], column, slots, size, p_ref, 0, store)
-    for table, ready in ((qh_ref, ready_h_ref), (ql_ref, ready_l_ref)):
-        table[: 2 * rows] = ready[...]
+    for table, mine, own in ((qh_ref, mine_h_ref, own_h_ref), (ql_ref, mine_l_ref, own_l_ref)):
+        table[:rows] = mine[...]
+        table[rows : 2 * rows] = own[...]
         table[3 * rows] = jnp.zeros((total, LANES), jnp.bfloat16)
     tile_half = lane_iota((total, LANES)) // size
     zero = jnp.zeros((total, LANES), jnp.bfloat16)
     tiles = [[targets[column * slots + k, i] for k in range(slots)] for i in range(rows)]
     for i in range(rows):
         for p in range(pairs):
-            his, los = [], []
+            right = []
             for h in range(2):
                 t = tiles[i][2 * p + h]
-                his.append(jnp.where(tile_half == h, qh_ref[t], zero))
-                los.append(jnp.where(tile_half == h, ql_ref[t], zero))
-            lhs = two_part(jnp.concatenate(his, axis=0), jnp.concatenate(los, axis=0))
-            both = mxu(lhs, pack_ref[i, :, 2 * p * LANES : 2 * (p + 1) * LANES], NT)
-            hi, lo = split(both[: 2 * total] + both[2 * total :])
+                parts = [jnp.where(tile_half == h, table[t], zero) for table in (qh_ref, ql_ref)]
+                right.append(jnp.concatenate(parts, axis=1))
+            both = mxu(v_ref[i, :, 2 * p * LANES : 2 * (p + 1) * LANES], jnp.concatenate(right, axis=0), NT)
             at = slice(2 * p * total, 2 * (p + 1) * total)
-            r_ref[i, at, :] = jnp.concatenate([hi, lo], axis=1)
-        r_ref[i, slots * total :, :] = diagonal_term_ref[i]
-    sign = jnp.where(lane_iota((total, (slots + 1) * total)) < slots * total, -1.0, 1.0)
-    for i in range(rows):
-        both = mxu(left_ref[i], r_ref[i], NT)
-        s_ref[i, :total, :], s_ref[i, total:, :] = split((both[:total] + both[total:]) * sign)
+            s_ref[i, :total, at], s_ref[i, total:, at] = split(both[:total] + both[total:])
+        s_ref[i, :, slots * total :] = diagonal_ref[i]
     for i in range(rows):
         hot = [(even_ref if k % 2 == 0 else odd_ref)[tiles[i][k]] for k in range(slots)]
         both = mxu(s_ref[i], jnp.concatenate(hot + [even_ref[rows + i]], axis=0), NN)
@@ -356,24 +364,27 @@
     far = across(block)
     far_partner = partner(far)
     last = partner(jnp.concatenate([straight, diagonal]))
+    own_parts = call(
+        functools.partial(own_kernel, size),
+        [array((rows, total, LANES), bf16)] * 2
+        + [array((rows, 2 * total, 2 * slots * size), bf16), array((rows, 2 * total, total), bf16)],
+        [VMEM] * 5, [scratch((rows * total // 2, LANES), f32)],
+        own, far, far_partner, unit, packed)
     ready = call(
-        functools.partial(ready_kernel, size, slots),
-        [array((2 * rows, total, LANES), bf16)] * 2
-        + [array((rows, 2 * total, LANES), bf16), array((rows, total, LANES), bf16)],
-        [VMEM] * 6, [scratch((rows * total, LANES), f32)],
-        straight, diagonal, own, far, far_partner, unit)
+        functools.partial(ready_kernel, size, slots), [array((rows, total, LANES), bf16)] * 2,
+        [VMEM] * 3, [scratch((rows * total // 2, LANES), f32)],
+        straight, diagonal, unit)
     parts = call(
-        functools.partial(coarse_kernel, size, ncol, nrow),
-        array((nrow * ncol, rows // ncol, LANES), f32), [SMEM] + [VMEM] * 10,
+        functools.partial(coarse_kernel, size, slots, ncol, nrow),
+        array((nrow * ncol, rows // ncol, LANES), f32), [SMEM] + [VMEM] * 11,
         [
             scratch((rows * total // 2, LANES), f32),
             scratch((3 * rows + 1, total, LANES), bf16),
             scratch((3 * rows + 1, total, LANES), bf16),
-            scratch((rows, (slots + 1) * total, LANES), bf16),
             scratch((rows, 2 * total, (slots + 1) * total), bf16),
             scratch((rows * total, 2 * LANES), bf16),
         ],
-        targets, last, unit, *ready, *hots, packed)
+        targets, last, unit, *own_parts, *ready, *hots)
     got = lax.all_to_all(parts, ("row", "col"), 0, 0)
     return call(
         functools.partial(sum_kernel, ncol, nrow), array((rows // ncol, LANES), f32), [VMEM], [], got)

time: 48.5 us -> 48.4 us (level)
    pallas_call x6 -> x7, Pallas kernels: 7.37 us -> 7.53 us  [call(): pl.pallas_call(kernel, out_shape=out_shape, in_specs=specs, out_specs=jax...]
  transfers between devices with their start and end apart: 10 -> 10, of which waited for: 7 -> 7; matrix products, arithmetic and copies ran while one was open for 2% -> 2% of each run, Pallas kernels for 7% -> 8%
where the time goes in v6:
time: 48.4 us; the launch traced here: 48.2 us
  waiting for transfers between devices  22.5 us (46%)
  blocking collectives  10.1 us (21%)
  Pallas kernels  7.53 us (16%)
  starting transfers between devices  7.09 us (15%)
  other arithmetic  0.74 us (2%)
    ppermute x10, waiting for transfers between devices, send(): return lax.ppermute(x, ('row', 'col'), pairs)  22.5 us
    all_to_all x1, blocking collectives, on_device(): got = lax.all_to_all(parts, ('row', 'col'), 0, 0)  10.1 us
    pallas_call x7, Pallas kernels, call(): pl.pallas_call(kernel, out_shape=out_shape, in_specs=specs, out_specs=jax...  7.53 us
    ppermute x10, starting transfers between devices, send(): return lax.ppermute(x, ('row', 'col'), pairs)  7.09 us
  transfers between devices with their start and end apart: 10, of which 7 were waited for; matrix products, arithmetic and copies ran while one was open for 2% of the time, Pallas kernels for 8%

profile of v6, /device:TPU:0, one launch (start us, length us, event | category | flops | bytes accessed | tf_op | source)
XLA Modules:
  0.0 48.2 jit_solution(16417406057375867174)
XLA Ops:
  0.0 0.0 copy-start.1
  0.0 0.0 copy-start.2
  0.0 3.0 %collective-permute-start = (f32[24,64]{1,0:T(8,128)}, f32[24,64]{1,0:T(8,128)S(1)}, u32[]{:S(2)}, u32[]{:S(2)}) collective-permute-start(f32[24,64]{1,0:T(8,128)} %own_ref.1), channel_id=1, source_target_pairs={{0,4},{1,29},{2,6},{3,31},{4,8},{5,1},{6,10},{7,3},{8,12},{9,5},{1... | collective-permute-start | bytes 18440 | tf_op jit(solution)/shard_map/ppermute | solution.py:328
  3.0 5.0 %collective-permute-done.mine_ref = f32[24,64]{1,0:T(8,128)S(1)} collective-permute-done((f32[24,64]{1,0:T(8,128)}, f32[24,64]{1,0:T(8,128)S(1)}, u32[]{:S(2)}, u32[]{:S(2)}) %collective-permute-start) | collective-permute-done | bytes 6176 | tf_op jit(solution)/shard_map/ppermute | solution.py:328
  8.0 0.0 collective-permute-start.1
  8.0 0.7 %fusion.4.targets = s32[16,24]{1,0:T(8,128)S(1)} fusion(s32[24]{0:T(128)S(1)} %iota_add_fusion, s32[24]{0:T(128)} %param.7, pred[]{:T(512)S(6)} %eq.5, s32[24,16]{0,1:T(8,128)} %param.6), kind=kLoop, calls=%fused_computation.8 | loop fusion | flops 7296 | bytes 3265 | tf_op jit(solution)/shard_map/jit(_where)/select_n | solution.py:82
  8.7 0.0 copy-start
  8.7 2.0 %shard_map.55.pack_ref = bf16[24,64,512]{2,1,0:T(8,128)(2,1)S(1)} custom-call(f32[24,4,64,64]{3,2,1,0:T(8,128)} %w_hbm.1), custom_call_target="tpu_custom_call" | custom-call | tf_op jit(solution)/shard_map/pallas_call | solution.py:316
  10.8 0.0 collective-permute-done.1.other_ref
  10.8 0.0 copy-done.1
  10.8 0.0 copy-done.2
  10.8 1.4 %shard_map.56 = (f32[64,128]{1,0:T(8,128)S(1)}, f32[80,128]{1,0:T(8,128)S(1)}) custom-call(s32[16,24]{1,0:T(8,128)S(1)} %fusion.4.targets, f32[24,64]{1,0:T(8,128)S(1)} %collective-permute-done.mine_ref, f32[24,64]{1,0:T(8,128)S(1)} %collective-permute-done.1.other_ref, f32[24,64]{1,0:T(8,128)S(1)} %copy-done.1, f32[24,64]{1,0:T(8,128)S(1)} %copy-done.2, ...), custom_call_target="tpu_custom_call" | custom-call | tf_op jit(solution)/shard_map/pallas_call | solution.py:316
  12.2 0.5 %collective-permute-start.2 = (f32[64,128]{1,0:T(8,128)S(1)}, f32[64,128]{1,0:T(8,128)S(1)}, u32[]{:S(2)}, u32[]{:S(2)}) collective-permute-start(f32[64,128]{1,0:T(8,128)S(1)} %get-tuple-element.16), channel_id=1, source_target_pairs={{0,1},{1,0},{2,3},{3,2},{4,5},{5,4},{6,7},{7,6},{8,9},{9,8},{10,11... | collective-permute-start | bytes 98312 | tf_op jit(solution)/shard_map/ppermute | solution.py:328
  12.8 0.9 %collective-permute-done.2 = f32[64,128]{1,0:T(8,128)S(1)} collective-permute-done((f32[64,128]{1,0:T(8,128)S(1)}, f32[64,128]{1,0:T(8,128)S(1)}, u32[]{:S(2)}, u32[]{:S(2)}) %collective-permute-start.2) | collective-permute-done | bytes 32800 | tf_op jit(solution)/shard_map/ppermute | solution.py:328
  13.6 0.0 collective-permute-start.4
  13.7 2.3 %collective-permute-start.3 = (f32[128,128]{1,0:T(8,128)S(1)}, f32[128,128]{1,0:T(8,128)S(1)}, u32[]{:S(2)}, u32[]{:S(2)}) collective-permute-start(f32[128,128]{1,0:T(8,128)S(1)} %constant_dynamic-update-slice_fusion.own_ref), channel_id=1, source_target_pairs={{0,4},{1,29},{2,6},{3,31},{4,8},{5,1},{6,10},{7,3},{8,12},{9,5},{1... | collective-permute-start | bytes 196616 | tf_op jit(solution)/shard_map/ppermute | solution.py:328
  15.9 5.7 %collective-permute-done.4.diagonal_ref = f32[128,128]{1,0:T(8,128)S(1)} collective-permute-done((f32[128,128]{1,0:T(8,128)S(1)}, f32[128,128]{1,0:T(8,128)S(1)}, u32[]{:S(2)}, u32[]{:S(2)}) %collective-permute-start.4) | collective-permute-done | bytes 65568 | tf_op jit(solution)/shard_map/ppermute | solution.py:328
  21.6 0.7 %collective-permute-done.3.straight_ref = f32[128,128]{1,0:T(8,128)S(1)} collective-permute-done((f32[128,128]{1,0:T(8,128)S(1)}, f32[128,128]{1,0:T(8,128)S(1)}, u32[]{:S(2)}, u32[]{:S(2)}) %collective-permute-start.3) | collective-permute-done | bytes 65568 | tf_op jit(solution)/shard_map/ppermute | solution.py:328
  22.3 0.1 collective-permute-start.5
  22.4 1.2 %collective-permute-start.6 = (f32[64,128]{1,0:T(8,128)S(1)}, f32[64,128]{1,0:T(8,128)S(1)}, u32[]{:S(2)}, u32[]{:S(2)}) collective-permute-start(f32[64,128]{1,0:T(8,128)S(1)} %get-tuple-element.16), channel_id=1, source_target_pairs={{0,2},{1,3},{2,0},{3,1},{4,6},{5,7},{6,4},{7,5},{8,10},{9,11},{10,... | collective-permute-start | bytes 98312 | tf_op jit(solution)/shard_map/ppermute | solution.py:328
  23.6 2.8 %collective-permute-done.6.far_ref = f32[64,128]{1,0:T(8,128)S(1)} collective-permute-done((f32[64,128]{1,0:T(8,128)S(1)}, f32[64,128]{1,0:T(8,128)S(1)}, u32[]{:S(2)}, u32[]{:S(2)}) %collective-permute-start.6) | collective-permute-done | bytes 32800 | tf_op jit(solution)/shard_map/ppermute | solution.py:328
  26.4 0.0 collective-permute-start.7
  26.4 0.0 copy-done
  26.4 0.0 collective-permute-start.8
  26.4 6.3 %collective-permute-done.8.mine_ref = s32[16,24]{1,0:T(8,128)S(1)} collective-permute-done((s32[16,24]{1,0:T(8,128)S(1)}, s32[16,24]{1,0:T(8,128)S(1)}, u32[]{:S(2)}, u32[]{:S(2)}) %collective-permute-start.8) | collective-permute-done | bytes 1568 | tf_op jit(solution)/shard_map/ppermute | solution.py:328
  32.8 0.0 collective-permute-start.9
  32.8 1.2 %collective-permute-done.9.other_ref = s32[16,24]{1,0:T(8,128)S(1)} collective-permute-done((s32[16,24]{1,0:T(8,128)S(1)}, s32[16,24]{1,0:T(8,128)S(1)}, u32[]{:S(2)}, u32[]{:S(2)}) %collective-permute-start.9) | collective-permute-done | bytes 1568 | tf_op jit(solution)/shard_map/ppermute | solution.py:328
  33.9 0.9 %shard_map.59 = (bf16[73,16,128]{2,1,0:T(8,128)(2,1)S(1)}, bf16[73,16,128]{2,1,0:T(8,128)(2,1)S(1)}, bf16[72,384]{1,0:T(8,128)(2,1)S(1)}) custom-call(s32[16,24]{1,0:T(8,128)S(1)} %collective-permute-done.8.mine_ref, s32[16,24]{1,0:T(8,128)S(1)} %collective-permute-done.9.other_ref, s32[16,24]{1,0:T(8,128)S(1)} %bitcast.3), custom_call_target="tpu_custom_call" | custom-call | tf_op jit(solution)/shard_map/pallas_call | solution.py:316
  34.8 0.0 collective-permute-done.7.far_partner_ref
  34.8 0.6 %shard_map.57 = (bf16[24,16,128]{2,1,0:T(8,128)(2,1)S(1)}, bf16[24,16,128]{2,1,0:T(8,128)(2,1)S(1)}, bf16[24,32,512]{2,1,0:T(8,128)(2,1)S(1)}, bf16[24,32,16]{2,1,0:T(8,128)(2,1)S(1)}) custom-call(f32[128,128]{1,0:T(8,128)S(1)} %constant_dynamic-update-slice_fusion.own_ref, f32[64,128]{1,0:T(8,128)S(1)} %collective-permute-done.6.far_ref, ...), custom_call_target="tpu_custom_call" | custom-call | tf_op jit(solution)/shard_map/pallas_call | solution.py:316
  35.4 0.2 shard_map.58
  35.7 0.0 collective-permute-done.5.last_ref
  35.7 1.7 %shard_map.60 = f32[32,6,128]{2,1,0:T(8,128)S(1)} custom-call(s32[16,24]{1,0:T(8,128)S(1)} %fusion.4.targets, f32[256,128]{1,0:T(8,128)S(1)} %collective-permute-done.5.last_ref, f32[80,128]{1,0:T(8,128)S(1)} %get-tuple-element.17.unit_ref, bf16[24,16,128]{2,1,0:T(8,128)(2,1)S(1)} %get-tuple-element.18.own_h_ref, ...), custom_call_target="tpu_custom_call" | custom-call | tf_op jit(solution)/shard_map/pallas_call | solution.py:316
  37.4 10.1 %all_to_all.5.got_ref = f32[32,6,128]{2,1,0:T(8,128)S(1)} all-to-all(f32[32,6,128]{2,1,0:T(8,128)S(1)} %shard_map.60), channel_id=1, replica_groups=mesh['row'=8,'col'=4] {'row','col'}, dimensions={0} | all-to-all | bytes 196608 | tf_op jit(solution)/shard_map/all_to_all | solution.py:388
  47.6 0.6 %shard_map.61 = f32[6,128]{1,0:T(8,128)} custom-call(f32[32,6,128]{2,1,0:T(8,128)S(1)} %all_to_all.5.got_ref), custom_call_target="tpu_custom_call" | custom-call | tf_op jit(solution)/shard_map/pallas_call | solution.py:316
  (4 shorter events, 0.0 us)
Async XLA Ops:
  0.0 10.8 %copy-start.1 = (f32[24,64]{1,0:T(8,128)S(1)}, f32[24,64]{1,0:T(8,128)}, u32[]{:S(2)}) copy-start(f32[24,64]{1,0:T(8,128)} %own_ref.1) | copy-start | bytes 18436
  0.0 10.8 %copy-start.2 = (f32[24,64]{1,0:T(8,128)S(1)}, f32[24,64]{1,0:T(8,128)}, u32[]{:S(2)}) copy-start(f32[24,64]{1,0:T(8,128)} %ridge_ref.1) | copy-start | bytes 18436
  0.0 8.0 %collective-permute-start = (f32[24,64]{1,0:T(8,128)}, f32[24,64]{1,0:T(8,128)S(1)}, u32[]{:S(2)}, u32[]{:S(2)}) collective-permute-start(f32[24,64]{1,0:T(8,128)} %own_ref.1), channel_id=1, source_target_pairs={{0,4},{1,29},{2,6},{3,31},{4,8},{5,1},{6,10},{7,3},{8,12},{9,5},{1... | collective-permute-start | bytes 18440 | tf_op jit(solution)/shard_map/ppermute | solution.py:328
  8.0 2.8 %collective-permute-start.1 = (f32[24,64]{1,0:T(8,128)S(1)}, f32[24,64]{1,0:T(8,128)S(1)}, u32[]{:S(2)}, u32[]{:S(2)}) collective-permute-start(f32[24,64]{1,0:T(8,128)S(1)} %collective-permute-done.mine_ref), channel_id=1, source_target_pairs={{0,1},{1,0},{2,3},{3,2},{4,5},{5,4},{6,7},{7,6},{8,9},{9,8},{10,11... | collective-permute-start | bytes 18440 | tf_op jit(solution)/shard_map/ppermute | solution.py:328
  8.7 17.7 %copy-start = (s32[24,16]{0,1:T(8,128)S(1)}, s32[24,16]{0,1:T(8,128)}, u32[]{:S(2)}) copy-start(s32[24,16]{0,1:T(8,128)} %param.6) | copy-start | bytes 4612
  12.2 1.4 %collective-permute-start.2 = (f32[64,128]{1,0:T(8,128)S(1)}, f32[64,128]{1,0:T(8,128)S(1)}, u32[]{:S(2)}, u32[]{:S(2)}) collective-permute-start(f32[64,128]{1,0:T(8,128)S(1)} %get-tuple-element.16), channel_id=1, source_target_pairs={{0,1},{1,0},{2,3},{3,2},{4,5},{5,4},{6,7},{7,6},{8,9},{9,8},{10,11... | collective-permute-start | bytes 98312 | tf_op jit(solution)/shard_map/ppermute | solution.py:328
  13.6 8.0 %collective-permute-start.4 = (f32[128,128]{1,0:T(8,128)S(1)}, f32[128,128]{1,0:T(8,128)S(1)}, u32[]{:S(2)}, u32[]{:S(2)}) collective-permute-start(f32[128,128]{1,0:T(8,128)S(1)} %constant_dynamic-update-slice_fusion.own_ref), channel_id=1, source_target_pairs={{0,6},{1,31},{2,4},{3,29},{4,10},{5,3},{6,8},{7,1},{8,14},{9,7},{1... | collective-permute-start | bytes 196616 | tf_op jit(solution)/shard_map/ppermute | solution.py:328
  13.7 8.7 %collective-permute-start.3 = (f32[128,128]{1,0:T(8,128)S(1)}, f32[128,128]{1,0:T(8,128)S(1)}, u32[]{:S(2)}, u32[]{:S(2)}) collective-permute-start(f32[128,128]{1,0:T(8,128)S(1)} %constant_dynamic-update-slice_fusion.own_ref), channel_id=1, source_target_pairs={{0,4},{1,29},{2,6},{3,31},{4,8},{5,1},{6,10},{7,3},{8,12},{9,5},{1... | collective-permute-start | bytes 196616 | tf_op jit(solution)/shard_map/ppermute | solution.py:328
  22.3 13.3 %collective-permute-start.5 = (f32[256,128]{1,0:T(8,128)S(1)}, f32[256,128]{1,0:T(8,128)S(1)}, u32[]{:S(2)}, u32[]{:S(2)}) collective-permute-start(f32[256,128]{1,0:T(8,128)S(1)} %pad_maximum_fusion), channel_id=1, source_target_pairs={{0,1},{1,0},{2,3},{3,2},{4,5},{5,4},{6,7},{7,6},{8,9},{9,8},{10,11... | collective-permute-start | bytes 393224 | tf_op jit(solution)/shard_map/ppermute | solution.py:328
  22.4 4.0 %collective-permute-start.6 = (f32[64,128]{1,0:T(8,128)S(1)}, f32[64,128]{1,0:T(8,128)S(1)}, u32[]{:S(2)}, u32[]{:S(2)}) collective-permute-start(f32[64,128]{1,0:T(8,128)S(1)} %get-tuple-element.16), channel_id=1, source_target_pairs={{0,2},{1,3},{2,0},{3,1},{4,6},{5,7},{6,4},{7,5},{8,10},{9,11},{10,... | collective-permute-start | bytes 98312 | tf_op jit(solution)/shard_map/ppermute | solution.py:328
  26.4 8.4 %collective-permute-start.7 = (f32[64,128]{1,0:T(8,128)S(1)}, f32[64,128]{1,0:T(8,128)S(1)}, u32[]{:S(2)}, u32[]{:S(2)}) collective-permute-start(f32[64,128]{1,0:T(8,128)S(1)} %collective-permute-done.6.far_ref), channel_id=1, source_target_pairs={{0,1},{1,0},{2,3},{3,2},{4,5},{5,4},{6,7},{7,6},{8,9},{9,8},{10,11... | collective-permute-start | bytes 98312 | tf_op jit(solution)/shard_map/ppermute | solution.py:328
  26.4 6.3 %collective-permute-start.8 = (s32[16,24]{1,0:T(8,128)S(1)}, s32[16,24]{1,0:T(8,128)S(1)}, u32[]{:S(2)}, u32[]{:S(2)}) collective-permute-start(s32[16,24]{1,0:T(8,128)S(1)} %bitcast.2), channel_id=1, source_target_pairs={{0,4},{1,29},{2,6},{3,31},{4,8},{5,1},{6,10},{7,3},{8,12},{9,5},{1... | collective-permute-start | bytes 4616 | tf_op jit(solution)/shard_map/ppermute | solution.py:328
  32.8 1.2 %collective-permute-start.9 = (s32[16,24]{1,0:T(8,128)S(1)}, s32[16,24]{1,0:T(8,128)S(1)}, u32[]{:S(2)}, u32[]{:S(2)}) collective-permute-start(s32[16,24]{1,0:T(8,128)S(1)} %collective-permute-done.8.mine_ref), channel_id=1, source_target_pairs={{0,1},{1,0},{2,3},{3,2},{4,5},{5,4},{6,7},{7,6},{8,9},{9,8},{10,11... | collective-permute-start | bytes 4616 | tf_op jit(solution)/shard_map/ppermute | solution.py:328

commit v7 on v6

--- a/solution.py
+++ b/solution.py
@@ -72,14 +72,14 @@
     return jnp.concatenate([top, jnp.concatenate([lo, jnp.zeros_like(lo)], axis=1)], axis=0)
 
 
-def aim(all_rows, counts, cols):
-    total, rows = cols.shape
-    local = lane_iota((total, rows))
+def aim(all_rows, start, counts, cols):
+    slots, rows = cols.shape
+    local = lane_iota((slots, rows))
     first = lax.axis_index("row") * rows
     at = wrap(cols - (first + local) + H, all_rows) + (rows - H) + local
     mirror = jnp.where(at < rows, at + 2 * rows, jnp.where(at >= 2 * rows, at - 2 * rows, at))
     at = jnp.where(lax.axis_index("col") % 2 == 0, at, mirror)
-    return jnp.where(row_iota((total, rows)) < counts[None, :], at, 3 * rows)
+    return jnp.where(row_iota((slots, rows)) + start < counts[None, :], at, 3 * rows)
 
 
 def unit_kernel(size, targets, mine_ref, other_ref, own_ref, ridge_ref, pack_ref,
@@ -102,7 +102,7 @@
             tile = jnp.zeros((8, LANES), jnp.float32)
             for h in range(2):
                 k = 2 * p + h
-                t = targets[column * slots + k, i]
+                t = targets[k, i]
                 vec = jnp.broadcast_to(unit_ref[pl.ds(t, 1), :], (8, LANES))
                 one = jnp.broadcast_to(one_ref[pl.ds(t, 1), :], (8, LANES))
                 tile = jnp.where((row8 == k) & (half == h), vec, tile)
@@ -232,18 +232,20 @@
     prolong_rows(blocks, unit_ref[:rows, :], lax.axis_index("col"), slots, size, p_ref, 0, store)
 
 
-def coarse_kernel(size, slots, ncol, nrow, targets, last_ref, unit_ref, own_h_ref, own_l_ref, v_ref,
+def coarse_kernel(size, slots, ncol, nrow, targets, last_ref, diagonal_partner_ref, unit_ref, own_h_ref, own_l_ref, v_ref,
                   diagonal_ref, mine_h_ref, mine_l_ref, even_ref, odd_ref, turned_ref, out_ref,
                   p_ref, qh_ref, ql_ref, s_ref, t_ref):
     rows, total, _ = own_h_ref.shape
     pairs = slots // 2
     column = lax.axis_index("col")
-    count = last_ref.shape[0] // ncol
+    count = last_ref.shape[0] // 2
 
     def store(j, q):
         qh_ref[2 * rows + j], ql_ref[2 * rows + j] = split(q)
 
-    blocks = [block_of(last_ref, d ^ 1, count) for d in range(ncol)]
+    blocks = [
+        block_of(ref, index, count) for ref in (last_ref, diagonal_partner_ref) for index in (1, 0)
+    ]
     prolong_rows(blocks, unit_ref[2 * rows : 3 * rows, :], column, slots, size, p_ref, 0, store)
     for table, mine, own in ((qh_ref, mine_h_ref, own_h_ref), (ql_ref, mine_l_ref, own_l_ref)):
         table[:rows] = mine[...]
@@ -251,7 +253,7 @@
         table[3 * rows] = jnp.zeros((total, LANES), jnp.bfloat16)
     tile_half = lane_iota((total, LANES)) // size
     zero = jnp.zeros((total, LANES), jnp.bfloat16)
-    tiles = [[targets[column * slots + k, i] for k in range(slots)] for i in range(rows)]
+    tiles = [[targets[k, i] for k in range(slots)] for i in range(rows)]
     for i in range(rows):
         for p in range(pairs):
             right = []
@@ -343,48 +345,50 @@
         pack_kernel, array((rows, size, 2 * slots * size), bf16), [HBM],
         [scratch(weights.shape, f32), pltpu.SemaphoreType.DMA((CHUNKS if rows % CHUNKS == 0 else 1,))],
         weights, limit=PACK_LIMIT)
-    targets = aim(all_rows, counts, cols)
+    start = lax.axis_index("col") * slots
+    targets = aim(all_rows, start, counts, lax.dynamic_slice_in_dim(cols, start, slots, 0))
     null_other = partner(null_mine)
     cols_other = partner(cols_mine)
     count = (slots // 2) * rows + -(-rows // 16) * 8
     block, unit = call(
         functools.partial(unit_kernel, size),
         [array((count, LANES), f32), array((3 * rows + 8, LANES), f32)],
-        [SMEM] + [VMEM] * 5, [scratch((8 * rows, size), f32), scratch((3 * rows + 8, LANES), f32)],
+        [SMEM] + [VMEM] * 5, [scratch((8 * rows + 8, size), f32), scratch((3 * rows + 8, LANES), f32)],
         targets, null_mine, null_other, near_null, prior_ridge, packed)
     hots = call(
         functools.partial(hot_kernel, slots, all_rows),
         [array((3 * rows + 1, total, LANES), bf16)] * 2 + [array((3 * rows, rows * total), bf16)],
         [VMEM] * 3,
-        [scratch((3 * rows * total, LANES), f32)] * 2 + [scratch((rows * total, LANES), f32)],
+        [scratch((3 * rows * total + total, LANES), f32)] * 2 + [scratch((rows * total + total, LANES), f32)],
         cols_mine, cols_other, cols)
     own = jnp.concatenate([block, partner(block)])
     diagonal = outward(own, 2)
     straight = outward(own)
     far = across(block)
     far_partner = partner(far)
-    last = partner(jnp.concatenate([straight, diagonal]))
+    diagonal_partner = partner(diagonal)
+    last = partner(straight)
     own_parts = call(
         functools.partial(own_kernel, size),
         [array((rows, total, LANES), bf16)] * 2
         + [array((rows, 2 * total, 2 * slots * size), bf16), array((rows, 2 * total, total), bf16)],
-        [VMEM] * 5, [scratch((rows * total // 2, LANES), f32)],
+        [VMEM] * 5, [scratch((rows * total // 2 + total, LANES), f32)],
         own, far, far_partner, unit, packed)
     ready = call(
         functools.partial(ready_kernel, size, slots), [array((rows, total, LANES), bf16)] * 2,
-        [VMEM] * 3, [scratch((rows * total // 2, LANES), f32)],
+        [VMEM] * 3, [scratch((rows * total // 2 + total, LANES), f32)],
         straight, diagonal, unit)
     parts = call(
         functools.partial(coarse_kernel, size, slots, ncol, nrow),
-        array((nrow * ncol, rows // ncol, LANES), f32), [SMEM] + [VMEM] * 11,
+        array((nrow * ncol, rows // ncol, LANES), f32), [SMEM] + [VMEM] * 12,
         [
-            scratch((rows * total // 2, LANES), f32),
+            scratch((rows * total // 2 + total, LANES), f32),
             scratch((3 * rows + 1, total, LANES), bf16),
             scratch((3 * rows + 1, total, LANES), bf16),
             scratch((rows, 2 * total, (slots + 1) * total), bf16),
             scratch((rows * total, 2 * LANES), bf16),
         ],
-        targets, last, unit, *own_parts, *ready, *hots)
+        targets, last, diagonal_partner, unit, *own_parts, *ready, *hots)
     got = lax.all_to_all(parts, ("row", "col"), 0, 0)
     return call(
         functools.partial(sum_kernel, ncol, nrow), array((rows // ncol, LANES), f32), [VMEM], [], got)

time: 48.4 us -> 44.5 us (0.919)
  waiting for transfers between devices: 22.5 us -> 19.3 us
    ppermute x10 -> x11, waiting for transfers between devices: 22.5 us -> 19.3 us  [send(): return lax.ppermute(x, ('row', 'col'), pairs)]
    ppermute x10 -> x11, starting transfers between devices: 7.09 us -> 6.85 us  [send(): return lax.ppermute(x, ('row', 'col'), pairs)]
  transfers between devices with their start and end apart: 10 -> 11, of which waited for: 7 -> 6; matrix products, arithmetic and copies ran while one was open for 2% -> 2% of each run, Pallas kernels for 8% -> 8%
where the time goes in v7:
time: 44.5 us; the launch traced here: 44.3 us
  waiting for transfers between devices  19.3 us (43%)
  blocking collectives  9.91 us (22%)
  Pallas kernels  7.34 us (16%)
  starting transfers between devices  6.85 us (15%)
  other arithmetic  0.77 us (2%)
    ppermute x11, waiting for transfers between devices, send(): return lax.ppermute(x, ('row', 'col'), pairs)  19.3 us
    all_to_all x1, blocking collectives, on_device(): got = lax.all_to_all(parts, ('row', 'col'), 0, 0)  9.91 us
    pallas_call x7, Pallas kernels, call(): pl.pallas_call(kernel, out_shape=out_shape, in_specs=specs, out_specs=jax...  7.34 us
    ppermute x11, starting transfers between devices, send(): return lax.ppermute(x, ('row', 'col'), pairs)  6.85 us
  transfers between devices with their start and end apart: 11, of which 6 were waited for; matrix products, arithmetic and copies ran while one was open for 2% of the time, Pallas kernels for 8%

profile of v7, /device:TPU:0, one launch (start us, length us, event | category | flops | bytes accessed | tf_op | source)
XLA Modules:
  0.0 44.3 jit_solution(11609434011831306986)
XLA Ops:
  0.0 0.0 copy-start.1
  0.0 0.0 copy-start.2
  0.0 3.0 %collective-permute-start = (f32[24,64]{1,0:T(8,128)}, f32[24,64]{1,0:T(8,128)S(1)}, u32[]{:S(2)}, u32[]{:S(2)}) collective-permute-start(f32[24,64]{1,0:T(8,128)} %own_ref.1), channel_id=1, source_target_pairs={{0,4},{1,29},{2,6},{3,31},{4,8},{5,1},{6,10},{7,3},{8,12},{9,5},{1... | collective-permute-start | bytes 18440 | tf_op jit(solution)/shard_map/ppermute | solution.py:330
  3.0 5.0 %collective-permute-done.mine_ref = f32[24,64]{1,0:T(8,128)S(1)} collective-permute-done((f32[24,64]{1,0:T(8,128)}, f32[24,64]{1,0:T(8,128)S(1)}, u32[]{:S(2)}, u32[]{:S(2)}) %collective-permute-start) | collective-permute-done | bytes 6176 | tf_op jit(solution)/shard_map/ppermute | solution.py:330
  8.0 0.0 collective-permute-start.1
  8.0 0.8 %fusion.4.targets = s32[4,24]{1,0:T(4,128)S(1)} fusion(s32[24,16]{0,1:T(8,128)} %param.6, s32[]{:T(128)S(6)} %select_n.37, s32[24]{0:T(128)S(1)} %iota_add_fusion, s32[24]{0:T(128)} %param.7, pred[]{:T(512)S(6)} %eq.5, s32[4]{0:T(128)S(1)} %iota_add_fusion.1), kind=kLoop, calls=%fused_computation.9 | loop fusion | flops 1824 | bytes 981 | tf_op jit(solution)/shard_map/jit(_where)/select_n | solution.py:82
  8.8 0.0 copy-start
  8.8 2.0 %shard_map.55.pack_ref = bf16[24,64,512]{2,1,0:T(8,128)(2,1)S(1)} custom-call(f32[24,4,64,64]{3,2,1,0:T(8,128)} %w_hbm.1), custom_call_target="tpu_custom_call" | custom-call | tf_op jit(solution)/shard_map/pallas_call | solution.py:318
  10.8 0.0 collective-permute-done.1.other_ref
  10.8 0.0 copy-done.1
  10.8 0.0 copy-done.2
  10.8 1.4 %shard_map.56 = (f32[64,128]{1,0:T(8,128)S(1)}, f32[80,128]{1,0:T(8,128)S(1)}) custom-call(s32[4,24]{1,0:T(4,128)S(1)} %fusion.4.targets, f32[24,64]{1,0:T(8,128)S(1)} %collective-permute-done.mine_ref, f32[24,64]{1,0:T(8,128)S(1)} %collective-permute-done.1.other_ref, f32[24,64]{1,0:T(8,128)S(1)} %copy-done.1, f32[24,64]{1,0:T(8,128)S(1)} %copy-done.2, ...), custom_call_target="tpu_custom_call" | custom-call | tf_op jit(solution)/shard_map/pallas_call | solution.py:318
  12.2 0.5 %collective-permute-start.2 = (f32[64,128]{1,0:T(8,128)S(1)}, f32[64,128]{1,0:T(8,128)S(1)}, u32[]{:S(2)}, u32[]{:S(2)}) collective-permute-start(f32[64,128]{1,0:T(8,128)S(1)} %get-tuple-element.16), channel_id=1, source_target_pairs={{0,1},{1,0},{2,3},{3,2},{4,5},{5,4},{6,7},{7,6},{8,9},{9,8},{10,11... | collective-permute-start | bytes 98312 | tf_op jit(solution)/shard_map/ppermute | solution.py:330
  12.7 0.9 %collective-permute-done.2 = f32[64,128]{1,0:T(8,128)S(1)} collective-permute-done((f32[64,128]{1,0:T(8,128)S(1)}, f32[64,128]{1,0:T(8,128)S(1)}, u32[]{:S(2)}, u32[]{:S(2)}) %collective-permute-start.2) | collective-permute-done | bytes 32800 | tf_op jit(solution)/shard_map/ppermute | solution.py:330
  13.6 0.0 collective-permute-start.3
  13.6 2.3 %collective-permute-start.5 = (f32[128,128]{1,0:T(8,128)S(1)}, f32[128,128]{1,0:T(8,128)S(1)}, u32[]{:S(2)}, u32[]{:S(2)}) collective-permute-start(f32[128,128]{1,0:T(8,128)S(1)} %constant_dynamic-update-slice_fusion.own_ref), channel_id=1, source_target_pairs={{0,6},{1,31},{2,4},{3,29},{4,10},{5,3},{6,8},{7,1},{8,14},{9,7},{1... | collective-permute-start | bytes 196616 | tf_op jit(solution)/shard_map/ppermute | solution.py:330
  15.8 0.5 %collective-permute-start.7 = (f32[64,128]{1,0:T(8,128)S(1)}, f32[64,128]{1,0:T(8,128)S(1)}, u32[]{:S(2)}, u32[]{:S(2)}) collective-permute-start(f32[64,128]{1,0:T(8,128)S(1)} %get-tuple-element.16), channel_id=1, source_target_pairs={{0,2},{1,3},{2,0},{3,1},{4,6},{5,7},{6,4},{7,5},{8,10},{9,11},{10,... | collective-permute-start | bytes 98312 | tf_op jit(solution)/shard_map/ppermute | solution.py:330
  16.4 4.6 %collective-permute-done.3.straight_ref = f32[128,128]{1,0:T(8,128)S(1)} collective-permute-done((f32[128,128]{1,0:T(8,128)S(1)}, f32[128,128]{1,0:T(8,128)S(1)}, u32[]{:S(2)}, u32[]{:S(2)}) %collective-permute-start.3) | collective-permute-done | bytes 65568 | tf_op jit(solution)/shard_map/ppermute | solution.py:330
  21.0 0.0 collective-permute-start.4
  21.0 1.4 %collective-permute-done.5.diagonal_ref = f32[128,128]{1,0:T(8,128)S(1)} collective-permute-done((f32[128,128]{1,0:T(8,128)S(1)}, f32[128,128]{1,0:T(8,128)S(1)}, u32[]{:S(2)}, u32[]{:S(2)}) %collective-permute-start.5) | collective-permute-done | bytes 65568 | tf_op jit(solution)/shard_map/ppermute | solution.py:330
  22.4 0.0 collective-permute-start.6
  22.4 0.0 collective-permute-done.7.far_ref
  22.4 0.5 %collective-permute-start.8 = (f32[64,128]{1,0:T(8,128)S(1)}, f32[64,128]{1,0:T(8,128)S(1)}, u32[]{:S(2)}, u32[]{:S(2)}) collective-permute-start(f32[64,128]{1,0:T(8,128)S(1)} %collective-permute-done.7.far_ref), channel_id=1, source_target_pairs={{0,1},{1,0},{2,3},{3,2},{4,5},{5,4},{6,7},{7,6},{8,9},{9,8},{10,11... | collective-permute-start | bytes 98312 | tf_op jit(solution)/shard_map/ppermute | solution.py:330
  22.9 0.0 copy-done
  22.9 0.0 collective-permute-start.9
  22.9 6.3 %collective-permute-done.9.mine_ref = s32[16,24]{1,0:T(8,128)S(1)} collective-permute-done((s32[16,24]{1,0:T(8,128)S(1)}, s32[16,24]{1,0:T(8,128)S(1)}, u32[]{:S(2)}, u32[]{:S(2)}) %collective-permute-start.9) | collective-permute-done | bytes 1568 | tf_op jit(solution)/shard_map/ppermute | solution.py:330
  29.2 0.0 collective-permute-start.10
  29.2 1.2 %collective-permute-done.10.other_ref = s32[16,24]{1,0:T(8,128)S(1)} collective-permute-done((s32[16,24]{1,0:T(8,128)S(1)}, s32[16,24]{1,0:T(8,128)S(1)}, u32[]{:S(2)}, u32[]{:S(2)}) %collective-permute-start.10) | collective-permute-done | bytes 1568 | tf_op jit(solution)/shard_map/ppermute | solution.py:330
  30.4 0.9 %shard_map.59 = (bf16[73,16,128]{2,1,0:T(8,128)(2,1)S(1)}, bf16[73,16,128]{2,1,0:T(8,128)(2,1)S(1)}, bf16[72,384]{1,0:T(8,128)(2,1)S(1)}) custom-call(s32[16,24]{1,0:T(8,128)S(1)} %collective-permute-done.9.mine_ref, s32[16,24]{1,0:T(8,128)S(1)} %collective-permute-done.10.other_ref, s32[16,24]{1,0:T(8,128)S(1)} %bitcast.10), custom_call_target="tpu_custom_call" | custom-call | tf_op jit(solution)/shard_map/pallas_call | solution.py:318
  31.3 0.0 collective-permute-done.8.far_partner_ref
  31.3 0.6 %shard_map.57 = (bf16[24,16,128]{2,1,0:T(8,128)(2,1)S(1)}, bf16[24,16,128]{2,1,0:T(8,128)(2,1)S(1)}, bf16[24,32,512]{2,1,0:T(8,128)(2,1)S(1)}, bf16[24,32,16]{2,1,0:T(8,128)(2,1)S(1)}) custom-call(f32[128,128]{1,0:T(8,128)S(1)} %constant_dynamic-update-slice_fusion.own_ref, f32[64,128]{1,0:T(8,128)S(1)} %collective-permute-done.7.far_ref, ...), custom_call_target="tpu_custom_call" | custom-call | tf_op jit(solution)/shard_map/pallas_call | solution.py:318
  31.9 0.2 shard_map.58
  32.1 0.0 collective-permute-done.4.last_ref
  32.2 0.0 collective-permute-done.6.diagonal_partner_ref
  32.2 1.6 %shard_map.60 = f32[32,6,128]{2,1,0:T(8,128)S(1)} custom-call(s32[4,24]{1,0:T(4,128)S(1)} %fusion.4.targets, f32[128,128]{1,0:T(8,128)S(1)} %collective-permute-done.4.last_ref, f32[128,128]{1,0:T(8,128)S(1)} %collective-permute-done.6.diagonal_partner_ref, f32[80,128]{1,0:T(8,128)S(1)} %get-tuple-element.17.unit_ref, ...), custom_call_target="tpu_custom_call" | custom-call | tf_op jit(solution)/shard_map/pallas_call | solution.py:318
  33.8 9.9 %all_to_all.5.got_ref = f32[32,6,128]{2,1,0:T(8,128)S(1)} all-to-all(f32[32,6,128]{2,1,0:T(8,128)S(1)} %shard_map.60), channel_id=1, replica_groups=mesh['row'=8,'col'=4] {'row','col'}, dimensions={0} | all-to-all | bytes 196608 | tf_op jit(solution)/shard_map/all_to_all | solution.py:392
  43.7 0.6 %shard_map.61 = f32[6,128]{1,0:T(8,128)} custom-call(f32[32,6,128]{2,1,0:T(8,128)S(1)} %all_to_all.5.got_ref), custom_call_target="tpu_custom_call" | custom-call | tf_op jit(solution)/shard_map/pallas_call | solution.py:318
  (4 shorter events, 0.0 us)
Async XLA Ops:
  0.0 10.8 %copy-start.1 = (f32[24,64]{1,0:T(8,128)S(1)}, f32[24,64]{1,0:T(8,128)}, u32[]{:S(2)}) copy-start(f32[24,64]{1,0:T(8,128)} %own_ref.1) | copy-start | bytes 18436
  0.0 10.8 %copy-start.2 = (f32[24,64]{1,0:T(8,128)S(1)}, f32[24,64]{1,0:T(8,128)}, u32[]{:S(2)}) copy-start(f32[24,64]{1,0:T(8,128)} %ridge_ref.1) | copy-start | bytes 18436
  0.0 8.0 %collective-permute-start = (f32[24,64]{1,0:T(8,128)}, f32[24,64]{1,0:T(8,128)S(1)}, u32[]{:S(2)}, u32[]{:S(2)}) collective-permute-start(f32[24,64]{1,0:T(8,128)} %own_ref.1), channel_id=1, source_target_pairs={{0,4},{1,29},{2,6},{3,31},{4,8},{5,1},{6,10},{7,3},{8,12},{9,5},{1... | collective-permute-start | bytes 18440 | tf_op jit(solution)/shard_map/ppermute | solution.py:330
  8.0 2.8 %collective-permute-start.1 = (f32[24,64]{1,0:T(8,128)S(1)}, f32[24,64]{1,0:T(8,128)S(1)}, u32[]{:S(2)}, u32[]{:S(2)}) collective-permute-start(f32[24,64]{1,0:T(8,128)S(1)} %collective-permute-done.mine_ref), channel_id=1, source_target_pairs={{0,1},{1,0},{2,3},{3,2},{4,5},{5,4},{6,7},{7,6},{8,9},{9,8},{10,11... | collective-permute-start | bytes 18440 | tf_op jit(solution)/shard_map/ppermute | solution.py:330
  8.8 14.1 %copy-start = (s32[24,16]{0,1:T(8,128)S(1)}, s32[24,16]{0,1:T(8,128)}, u32[]{:S(2)}) copy-start(s32[24,16]{0,1:T(8,128)} %param.6) | copy-start | bytes 4612
  12.2 1.4 %collective-permute-start.2 = (f32[64,128]{1,0:T(8,128)S(1)}, f32[64,128]{1,0:T(8,128)S(1)}, u32[]{:S(2)}, u32[]{:S(2)}) collective-permute-start(f32[64,128]{1,0:T(8,128)S(1)} %get-tuple-element.16), channel_id=1, source_target_pairs={{0,1},{1,0},{2,3},{3,2},{4,5},{5,4},{6,7},{7,6},{8,9},{9,8},{10,11... | collective-permute-start | bytes 98312 | tf_op jit(solution)/shard_map/ppermute | solution.py:330
  13.6 7.4 %collective-permute-start.3 = (f32[128,128]{1,0:T(8,128)S(1)}, f32[128,128]{1,0:T(8,128)S(1)}, u32[]{:S(2)}, u32[]{:S(2)}) collective-permute-start(f32[128,128]{1,0:T(8,128)S(1)} %constant_dynamic-update-slice_fusion.own_ref), channel_id=1, source_target_pairs={{0,4},{1,29},{2,6},{3,31},{4,8},{5,1},{6,10},{7,3},{8,12},{9,5},{1... | collective-permute-start | bytes 196616 | tf_op jit(solution)/shard_map/ppermute | solution.py:330
  13.6 8.8 %collective-permute-start.5 = (f32[128,128]{1,0:T(8,128)S(1)}, f32[128,128]{1,0:T(8,128)S(1)}, u32[]{:S(2)}, u32[]{:S(2)}) collective-permute-start(f32[128,128]{1,0:T(8,128)S(1)} %constant_dynamic-update-slice_fusion.own_ref), channel_id=1, source_target_pairs={{0,6},{1,31},{2,4},{3,29},{4,10},{5,3},{6,8},{7,1},{8,14},{9,7},{1... | collective-permute-start | bytes 196616 | tf_op jit(solution)/shard_map/ppermute | solution.py:330
  15.8 6.5 %collective-permute-start.7 = (f32[64,128]{1,0:T(8,128)S(1)}, f32[64,128]{1,0:T(8,128)S(1)}, u32[]{:S(2)}, u32[]{:S(2)}) collective-permute-start(f32[64,128]{1,0:T(8,128)S(1)} %get-tuple-element.16), channel_id=1, source_target_pairs={{0,2},{1,3},{2,0},{3,1},{4,6},{5,7},{6,4},{7,5},{8,10},{9,11},{10,... | collective-permute-start | bytes 98312 | tf_op jit(solution)/shard_map/ppermute | solution.py:330
  21.0 11.2 %collective-permute-start.4 = (f32[128,128]{1,0:T(8,128)S(1)}, f32[128,128]{1,0:T(8,128)S(1)}, u32[]{:S(2)}, u32[]{:S(2)}) collective-permute-start(f32[128,128]{1,0:T(8,128)S(1)} %collective-permute-done.3.straight_ref), channel_id=1, source_target_pairs={{0,1},{1,0},{2,3},{3,2},{4,5},{5,4},{6,7},{7,6},{8,9},{9,8},{10,11... | collective-permute-start | bytes 196616 | tf_op jit(solution)/shard_map/ppermute | solution.py:330
  22.4 9.8 %collective-permute-start.6 = (f32[128,128]{1,0:T(8,128)S(1)}, f32[128,128]{1,0:T(8,128)S(1)}, u32[]{:S(2)}, u32[]{:S(2)}) collective-permute-start(f32[128,128]{1,0:T(8,128)S(1)} %collective-permute-done.5.diagonal_ref), channel_id=1, source_target_pairs={{0,1},{1,0},{2,3},{3,2},{4,5},{5,4},{6,7},{7,6},{8,9},{9,8},{10,11... | collective-permute-start | bytes 196616 | tf_op jit(solution)/shard_map/ppermute | solution.py:330
  22.4 8.9 %collective-permute-start.8 = (f32[64,128]{1,0:T(8,128)S(1)}, f32[64,128]{1,0:T(8,128)S(1)}, u32[]{:S(2)}, u32[]{:S(2)}) collective-permute-start(f32[64,128]{1,0:T(8,128)S(1)} %collective-permute-done.7.far_ref), channel_id=1, source_target_pairs={{0,1},{1,0},{2,3},{3,2},{4,5},{5,4},{6,7},{7,6},{8,9},{9,8},{10,11... | collective-permute-start | bytes 98312 | tf_op jit(solution)/shard_map/ppermute | solution.py:330
  22.9 6.3 %collective-permute-start.9 = (s32[16,24]{1,0:T(8,128)S(1)}, s32[16,24]{1,0:T(8,128)S(1)}, u32[]{:S(2)}, u32[]{:S(2)}) collective-permute-start(s32[16,24]{1,0:T(8,128)S(1)} %bitcast.9), channel_id=1, source_target_pairs={{0,4},{1,29},{2,6},{3,31},{4,8},{5,1},{6,10},{7,3},{8,12},{9,5},{1... | collective-permute-start | bytes 4616 | tf_op jit(solution)/shard_map/ppermute | solution.py:330
  29.2 1.2 %collective-permute-start.10 = (s32[16,24]{1,0:T(8,128)S(1)}, s32[16,24]{1,0:T(8,128)S(1)}, u32[]{:S(2)}, u32[]{:S(2)}) collective-permute-start(s32[16,24]{1,0:T(8,128)S(1)} %collective-permute-done.9.mine_ref), channel_id=1, source_target_pairs={{0,1},{1,0},{2,3},{3,2},{4,5},{5,4},{6,7},{7,6},{8,9},{9,8},{10,11... | collective-permute-start | bytes 4616 | tf_op jit(solution)/shard_map/ppermute | solution.py:330

commit v8 on v7

--- a/solution.py
+++ b/solution.py
@@ -283,18 +283,22 @@
         row = wrap(lax.axis_index("row") + (g - 1), nrow)
         for c in range(ncol):
             at = (3 - g) * rows - (c + 1) * share
-            out_ref[row * ncol + c] = relative[at : at + share]
+            for n in range(share // 2):
+                out_ref[(row * ncol + c) * (share // 2) + n] = relative[at + 2 * n : at + 2 * n + 2]
 
 
 def sum_kernel(ncol, nrow, got_ref, out_ref):
-    total = None
-    for step in (-1, 0, 1):
-        row = wrap(lax.axis_index("row") + step, nrow)
-        for c in range(ncol):
-            part = got_ref[row * ncol + c]
-            total = part if total is None else total + part
-    for n in range(total.shape[0]):
-        out_ref[n : n + 1, :] = total[total.shape[0] - 1 - n : total.shape[0] - n]
+    share = out_ref.shape[0]
+    for n in range(share // 2):
+        total = None
+        for step in (-1, 0, 1):
+            row = wrap(lax.axis_index("row") + step, nrow)
+            for c in range(ncol):
+                part = got_ref[(row * ncol + c) * (share // 2) + n]
+                total = part if total is None else total + part
+        for m in range(2):
+            at = share - 1 - 2 * n - m
+            out_ref[at : at + 1, :] = total[m : m + 1]
 
 
 HBM = pl.BlockSpec(memory_space=pltpu.HBM)
@@ -380,7 +384,7 @@
         straight, diagonal, unit)
     parts = call(
         functools.partial(coarse_kernel, size, slots, ncol, nrow),
-        array((nrow * ncol, rows // ncol, LANES), f32), [SMEM] + [VMEM] * 12,
+        array((nrow * rows // 2, 2, LANES), f32), [SMEM] + [VMEM] * 12,
         [
             scratch((rows * total // 2 + total, LANES), f32),
             scratch((3 * rows + 1, total, LANES), bf16),
@@ -389,7 +393,7 @@
             scratch((rows * total, 2 * LANES), bf16),
         ],
         targets, last, diagonal_partner, unit, *own_parts, *ready, *hots)
-    got = lax.all_to_all(parts, ("row", "col"), 0, 0)
+    got = lax.all_to_all(parts, ("row", "col"), 0, 0, tiled=True)
     return call(
         functools.partial(sum_kernel, ncol, nrow), array((rows // ncol, LANES), f32), [VMEM], [], got)
 

time: 44.5 us -> 44.1 us (level)
  transfers between devices with their start and end apart: 11 -> 11, of which waited for: 6 -> 6; matrix products, arithmetic and copies ran while one was open for 2% -> 2% of each run, Pallas kernels for 8% -> 9%
where the time goes in v8:
time: 44.1 us; the launch traced here: 43.9 us
  waiting for transfers between devices  19.3 us (44%)
  blocking collectives  9.48 us (21%)
  Pallas kernels  7.37 us (17%)
  starting transfers between devices  6.85 us (16%)
  other arithmetic  0.77 us (2%)
    ppermute x11, waiting for transfers between devices, send(): return lax.ppermute(x, ('row', 'col'), pairs)  19.3 us
    all_to_all x1, blocking collectives, on_device(): got = lax.all_to_all(parts, ('row', 'col'), 0, 0, tiled=True)  9.48 us
    pallas_call x7, Pallas kernels, call(): pl.pallas_call(kernel, out_shape=out_shape, in_specs=specs, out_specs=jax...  7.37 us
    ppermute x11, starting transfers between devices, send(): return lax.ppermute(x, ('row', 'col'), pairs)  6.85 us
  transfers between devices with their start and end apart: 11, of which 6 were waited for; matrix products, arithmetic and copies ran while one was open for 2% of the time, Pallas kernels for 9%

profile of v8, /device:TPU:0, one launch (start us, length us, event | category | flops | bytes accessed | tf_op | source)
XLA Modules:
  0.0 43.9 jit_solution(1691513120172914994)
XLA Ops:
  0.0 0.0 copy-start.1
  0.0 0.0 copy-start.2
  0.0 3.0 %collective-permute-start = (f32[24,64]{1,0:T(8,128)}, f32[24,64]{1,0:T(8,128)S(1)}, u32[]{:S(2)}, u32[]{:S(2)}) collective-permute-start(f32[24,64]{1,0:T(8,128)} %own_ref.1), channel_id=1, source_target_pairs={{0,4},{1,29},{2,6},{3,31},{4,8},{5,1},{6,10},{7,3},{8,12},{9,5},{1... | collective-permute-start | bytes 18440 | tf_op jit(solution)/shard_map/ppermute | solution.py:334
  3.0 5.0 %collective-permute-done.mine_ref = f32[24,64]{1,0:T(8,128)S(1)} collective-permute-done((f32[24,64]{1,0:T(8,128)}, f32[24,64]{1,0:T(8,128)S(1)}, u32[]{:S(2)}, u32[]{:S(2)}) %collective-permute-start) | collective-permute-done | bytes 6176 | tf_op jit(solution)/shard_map/ppermute | solution.py:334
  8.0 0.0 collective-permute-start.1
  8.0 0.8 %fusion.4.targets = s32[4,24]{1,0:T(4,128)S(1)} fusion(s32[24,16]{0,1:T(8,128)} %param.6, s32[]{:T(128)S(6)} %select_n.37, s32[24]{0:T(128)S(1)} %iota_add_fusion, s32[24]{0:T(128)} %param.7, pred[]{:T(512)S(6)} %eq.5, s32[4]{0:T(128)S(1)} %iota_add_fusion.1), kind=kLoop, calls=%fused_computation.9 | loop fusion | flops 1824 | bytes 981 | tf_op jit(solution)/shard_map/jit(_where)/select_n | solution.py:82
  8.8 0.0 copy-start
  8.8 2.0 %shard_map.55.pack_ref = bf16[24,64,512]{2,1,0:T(8,128)(2,1)S(1)} custom-call(f32[24,4,64,64]{3,2,1,0:T(8,128)} %w_hbm.1), custom_call_target="tpu_custom_call" | custom-call | tf_op jit(solution)/shard_map/pallas_call | solution.py:322
  10.8 0.0 collective-permute-done.1.other_ref
  10.8 0.0 copy-done.1
  10.8 0.0 copy-done.2
  10.8 1.4 %shard_map.56 = (f32[64,128]{1,0:T(8,128)S(1)}, f32[80,128]{1,0:T(8,128)S(1)}) custom-call(s32[4,24]{1,0:T(4,128)S(1)} %fusion.4.targets, f32[24,64]{1,0:T(8,128)S(1)} %collective-permute-done.mine_ref, f32[24,64]{1,0:T(8,128)S(1)} %collective-permute-done.1.other_ref, f32[24,64]{1,0:T(8,128)S(1)} %copy-done.1, f32[24,64]{1,0:T(8,128)S(1)} %copy-done.2, ...), custom_call_target="tpu_custom_call" | custom-call | tf_op jit(solution)/shard_map/pallas_call | solution.py:322
  12.2 0.5 %collective-permute-start.2 = (f32[64,128]{1,0:T(8,128)S(1)}, f32[64,128]{1,0:T(8,128)S(1)}, u32[]{:S(2)}, u32[]{:S(2)}) collective-permute-start(f32[64,128]{1,0:T(8,128)S(1)} %get-tuple-element.16), channel_id=1, source_target_pairs={{0,1},{1,0},{2,3},{3,2},{4,5},{5,4},{6,7},{7,6},{8,9},{9,8},{10,11... | collective-permute-start | bytes 98312 | tf_op jit(solution)/shard_map/ppermute | solution.py:334
  12.7 0.9 %collective-permute-done.2 = f32[64,128]{1,0:T(8,128)S(1)} collective-permute-done((f32[64,128]{1,0:T(8,128)S(1)}, f32[64,128]{1,0:T(8,128)S(1)}, u32[]{:S(2)}, u32[]{:S(2)}) %collective-permute-start.2) | collective-permute-done | bytes 32800 | tf_op jit(solution)/shard_map/ppermute | solution.py:334
  13.6 0.0 collective-permute-start.3
  13.6 2.3 %collective-permute-start.5 = (f32[128,128]{1,0:T(8,128)S(1)}, f32[128,128]{1,0:T(8,128)S(1)}, u32[]{:S(2)}, u32[]{:S(2)}) collective-permute-start(f32[128,128]{1,0:T(8,128)S(1)} %constant_dynamic-update-slice_fusion.own_ref), channel_id=1, source_target_pairs={{0,6},{1,31},{2,4},{3,29},{4,10},{5,3},{6,8},{7,1},{8,14},{9,7},{1... | collective-permute-start | bytes 196616 | tf_op jit(solution)/shard_map/ppermute | solution.py:334
  15.8 0.5 %collective-permute-start.7 = (f32[64,128]{1,0:T(8,128)S(1)}, f32[64,128]{1,0:T(8,128)S(1)}, u32[]{:S(2)}, u32[]{:S(2)}) collective-permute-start(f32[64,128]{1,0:T(8,128)S(1)} %get-tuple-element.16), channel_id=1, source_target_pairs={{0,2},{1,3},{2,0},{3,1},{4,6},{5,7},{6,4},{7,5},{8,10},{9,11},{10,... | collective-permute-start | bytes 98312 | tf_op jit(solution)/shard_map/ppermute | solution.py:334
  16.4 4.6 %collective-permute-done.3.straight_ref = f32[128,128]{1,0:T(8,128)S(1)} collective-permute-done((f32[128,128]{1,0:T(8,128)S(1)}, f32[128,128]{1,0:T(8,128)S(1)}, u32[]{:S(2)}, u32[]{:S(2)}) %collective-permute-start.3) | collective-permute-done | bytes 65568 | tf_op jit(solution)/shard_map/ppermute | solution.py:334
  21.0 0.0 collective-permute-start.4
  21.0 1.4 %collective-permute-done.5.diagonal_ref = f32[128,128]{1,0:T(8,128)S(1)} collective-permute-done((f32[128,128]{1,0:T(8,128)S(1)}, f32[128,128]{1,0:T(8,128)S(1)}, u32[]{:S(2)}, u32[]{:S(2)}) %collective-permute-start.5) | collective-permute-done | bytes 65568 | tf_op jit(solution)/shard_map/ppermute | solution.py:334
  22.4 0.0 collective-permute-start.6
  22.4 0.0 collective-permute-done.7.far_ref
  22.4 0.5 %collective-permute-start.8 = (f32[64,128]{1,0:T(8,128)S(1)}, f32[64,128]{1,0:T(8,128)S(1)}, u32[]{:S(2)}, u32[]{:S(2)}) collective-permute-start(f32[64,128]{1,0:T(8,128)S(1)} %collective-permute-done.7.far_ref), channel_id=1, source_target_pairs={{0,1},{1,0},{2,3},{3,2},{4,5},{5,4},{6,7},{7,6},{8,9},{9,8},{10,11... | collective-permute-start | bytes 98312 | tf_op jit(solution)/shard_map/ppermute | solution.py:334
  22.9 0.0 copy-done
  22.9 0.0 collective-permute-start.9
  22.9 6.3 %collective-permute-done.9.mine_ref = s32[16,24]{1,0:T(8,128)S(1)} collective-permute-done((s32[16,24]{1,0:T(8,128)S(1)}, s32[16,24]{1,0:T(8,128)S(1)}, u32[]{:S(2)}, u32[]{:S(2)}) %collective-permute-start.9) | collective-permute-done | bytes 1568 | tf_op jit(solution)/shard_map/ppermute | solution.py:334
  29.2 0.0 collective-permute-start.10
  29.2 1.2 %collective-permute-done.10.other_ref = s32[16,24]{1,0:T(8,128)S(1)} collective-permute-done((s32[16,24]{1,0:T(8,128)S(1)}, s32[16,24]{1,0:T(8,128)S(1)}, u32[]{:S(2)}, u32[]{:S(2)}) %collective-permute-start.10) | collective-permute-done | bytes 1568 | tf_op jit(solution)/shard_map/ppermute | solution.py:334
  30.4 0.9 %shard_map.59 = (bf16[73,16,128]{2,1,0:T(8,128)(2,1)S(1)}, bf16[73,16,128]{2,1,0:T(8,128)(2,1)S(1)}, bf16[72,384]{1,0:T(8,128)(2,1)S(1)}) custom-call(s32[16,24]{1,0:T(8,128)S(1)} %collective-permute-done.9.mine_ref, s32[16,24]{1,0:T(8,128)S(1)} %collective-permute-done.10.other_ref, s32[16,24]{1,0:T(8,128)S(1)} %bitcast.10), custom_call_target="tpu_custom_call" | custom-call | tf_op jit(solution)/shard_map/pallas_call | solution.py:322
  31.3 0.0 collective-permute-done.8.far_partner_ref
  31.3 0.6 %shard_map.57 = (bf16[24,16,128]{2,1,0:T(8,128)(2,1)S(1)}, bf16[24,16,128]{2,1,0:T(8,128)(2,1)S(1)}, bf16[24,32,512]{2,1,0:T(8,128)(2,1)S(1)}, bf16[24,32,16]{2,1,0:T(8,128)(2,1)S(1)}) custom-call(f32[128,128]{1,0:T(8,128)S(1)} %constant_dynamic-update-slice_fusion.own_ref, f32[64,128]{1,0:T(8,128)S(1)} %collective-permute-done.7.far_ref, ...), custom_call_target="tpu_custom_call" | custom-call | tf_op jit(solution)/shard_map/pallas_call | solution.py:322
  31.9 0.2 shard_map.58
  32.1 0.0 collective-permute-done.4.last_ref
  32.2 0.0 collective-permute-done.6.diagonal_partner_ref
  32.2 1.7 %shard_map.60 = f32[96,2,128]{2,1,0:T(2,128)S(1)} custom-call(s32[4,24]{1,0:T(4,128)S(1)} %fusion.4.targets, f32[128,128]{1,0:T(8,128)S(1)} %collective-permute-done.4.last_ref, f32[128,128]{1,0:T(8,128)S(1)} %collective-permute-done.6.diagonal_partner_ref, f32[80,128]{1,0:T(8,128)S(1)} %get-tuple-element.17.unit_ref, ...), custom_call_target="tpu_custom_call" | custom-call | tf_op jit(solution)/shard_map/pallas_call | solution.py:322
  33.8 9.5 %all_to_all.5.got_ref = f32[96,2,128]{2,1,0:T(2,128)S(1)} all-to-all(f32[96,2,128]{2,1,0:T(2,128)S(1)} %shard_map.60), channel_id=1, replica_groups=mesh['row'=8,'col'=4] {'row','col'}, dimensions={0} | all-to-all | bytes 196608 | tf_op jit(solution)/shard_map/all_to_all | solution.py:396
  43.3 0.6 %shard_map.61 = f32[6,128]{1,0:T(8,128)} custom-call(f32[96,2,128]{2,1,0:T(2,128)S(1)} %all_to_all.5.got_ref), custom_call_target="tpu_custom_call" | custom-call | tf_op jit(solution)/shard_map/pallas_call | solution.py:322
  (4 shorter events, 0.0 us)
Async XLA Ops:
  0.0 10.8 %copy-start.1 = (f32[24,64]{1,0:T(8,128)S(1)}, f32[24,64]{1,0:T(8,128)}, u32[]{:S(2)}) copy-start(f32[24,64]{1,0:T(8,128)} %own_ref.1) | copy-start | bytes 18436
  0.0 10.8 %copy-start.2 = (f32[24,64]{1,0:T(8,128)S(1)}, f32[24,64]{1,0:T(8,128)}, u32[]{:S(2)}) copy-start(f32[24,64]{1,0:T(8,128)} %ridge_ref.1) | copy-start | bytes 18436
  0.0 8.0 %collective-permute-start = (f32[24,64]{1,0:T(8,128)}, f32[24,64]{1,0:T(8,128)S(1)}, u32[]{:S(2)}, u32[]{:S(2)}) collective-permute-start(f32[24,64]{1,0:T(8,128)} %own_ref.1), channel_id=1, source_target_pairs={{0,4},{1,29},{2,6},{3,31},{4,8},{5,1},{6,10},{7,3},{8,12},{9,5},{1... | collective-permute-start | bytes 18440 | tf_op jit(solution)/shard_map/ppermute | solution.py:334
  8.0 2.8 %collective-permute-start.1 = (f32[24,64]{1,0:T(8,128)S(1)}, f32[24,64]{1,0:T(8,128)S(1)}, u32[]{:S(2)}, u32[]{:S(2)}) collective-permute-start(f32[24,64]{1,0:T(8,128)S(1)} %collective-permute-done.mine_ref), channel_id=1, source_target_pairs={{0,1},{1,0},{2,3},{3,2},{4,5},{5,4},{6,7},{7,6},{8,9},{9,8},{10,11... | collective-permute-start | bytes 18440 | tf_op jit(solution)/shard_map/ppermute | solution.py:334
  8.8 14.1 %copy-start = (s32[24,16]{0,1:T(8,128)S(1)}, s32[24,16]{0,1:T(8,128)}, u32[]{:S(2)}) copy-start(s32[24,16]{0,1:T(8,128)} %param.6) | copy-start | bytes 4612
  12.2 1.4 %collective-permute-start.2 = (f32[64,128]{1,0:T(8,128)S(1)}, f32[64,128]{1,0:T(8,128)S(1)}, u32[]{:S(2)}, u32[]{:S(2)}) collective-permute-start(f32[64,128]{1,0:T(8,128)S(1)} %get-tuple-element.16), channel_id=1, source_target_pairs={{0,1},{1,0},{2,3},{3,2},{4,5},{5,4},{6,7},{7,6},{8,9},{9,8},{10,11... | collective-permute-start | bytes 98312 | tf_op jit(solution)/shard_map/ppermute | solution.py:334
  13.6 7.4 %collective-permute-start.3 = (f32[128,128]{1,0:T(8,128)S(1)}, f32[128,128]{1,0:T(8,128)S(1)}, u32[]{:S(2)}, u32[]{:S(2)}) collective-permute-start(f32[128,128]{1,0:T(8,128)S(1)} %constant_dynamic-update-slice_fusion.own_ref), channel_id=1, source_target_pairs={{0,4},{1,29},{2,6},{3,31},{4,8},{5,1},{6,10},{7,3},{8,12},{9,5},{1... | collective-permute-start | bytes 196616 | tf_op jit(solution)/shard_map/ppermute | solution.py:334
  13.6 8.8 %collective-permute-start.5 = (f32[128,128]{1,0:T(8,128)S(1)}, f32[128,128]{1,0:T(8,128)S(1)}, u32[]{:S(2)}, u32[]{:S(2)}) collective-permute-start(f32[128,128]{1,0:T(8,128)S(1)} %constant_dynamic-update-slice_fusion.own_ref), channel_id=1, source_target_pairs={{0,6},{1,31},{2,4},{3,29},{4,10},{5,3},{6,8},{7,1},{8,14},{9,7},{1... | collective-permute-start | bytes 196616 | tf_op jit(solution)/shard_map/ppermute | solution.py:334
  15.8 6.5 %collective-permute-start.7 = (f32[64,128]{1,0:T(8,128)S(1)}, f32[64,128]{1,0:T(8,128)S(1)}, u32[]{:S(2)}, u32[]{:S(2)}) collective-permute-start(f32[64,128]{1,0:T(8,128)S(1)} %get-tuple-element.16), channel_id=1, source_target_pairs={{0,2},{1,3},{2,0},{3,1},{4,6},{5,7},{6,4},{7,5},{8,10},{9,11},{10,... | collective-permute-start | bytes 98312 | tf_op jit(solution)/shard_map/ppermute | solution.py:334
  21.0 11.2 %collective-permute-start.4 = (f32[128,128]{1,0:T(8,128)S(1)}, f32[128,128]{1,0:T(8,128)S(1)}, u32[]{:S(2)}, u32[]{:S(2)}) collective-permute-start(f32[128,128]{1,0:T(8,128)S(1)} %collective-permute-done.3.straight_ref), channel_id=1, source_target_pairs={{0,1},{1,0},{2,3},{3,2},{4,5},{5,4},{6,7},{7,6},{8,9},{9,8},{10,11... | collective-permute-start | bytes 196616 | tf_op jit(solution)/shard_map/ppermute | solution.py:334
  22.4 9.8 %collective-permute-start.6 = (f32[128,128]{1,0:T(8,128)S(1)}, f32[128,128]{1,0:T(8,128)S(1)}, u32[]{:S(2)}, u32[]{:S(2)}) collective-permute-start(f32[128,128]{1,0:T(8,128)S(1)} %collective-permute-done.5.diagonal_ref), channel_id=1, source_target_pairs={{0,1},{1,0},{2,3},{3,2},{4,5},{5,4},{6,7},{7,6},{8,9},{9,8},{10,11... | collective-permute-start | bytes 196616 | tf_op jit(solution)/shard_map/ppermute | solution.py:334
  22.4 8.9 %collective-permute-start.8 = (f32[64,128]{1,0:T(8,128)S(1)}, f32[64,128]{1,0:T(8,128)S(1)}, u32[]{:S(2)}, u32[]{:S(2)}) collective-permute-start(f32[64,128]{1,0:T(8,128)S(1)} %collective-permute-done.7.far_ref), channel_id=1, source_target_pairs={{0,1},{1,0},{2,3},{3,2},{4,5},{5,4},{6,7},{7,6},{8,9},{9,8},{10,11... | collective-permute-start | bytes 98312 | tf_op jit(solution)/shard_map/ppermute | solution.py:334
  22.9 6.3 %collective-permute-start.9 = (s32[16,24]{1,0:T(8,128)S(1)}, s32[16,24]{1,0:T(8,128)S(1)}, u32[]{:S(2)}, u32[]{:S(2)}) collective-permute-start(s32[16,24]{1,0:T(8,128)S(1)} %bitcast.9), channel_id=1, source_target_pairs={{0,4},{1,29},{2,6},{3,31},{4,8},{5,1},{6,10},{7,3},{8,12},{9,5},{1... | collective-permute-start | bytes 4616 | tf_op jit(solution)/shard_map/ppermute | solution.py:334
  29.2 1.2 %collective-permute-start.10 = (s32[16,24]{1,0:T(8,128)S(1)}, s32[16,24]{1,0:T(8,128)S(1)}, u32[]{:S(2)}, u32[]{:S(2)}) collective-permute-start(s32[16,24]{1,0:T(8,128)S(1)} %collective-permute-done.9.mine_ref), channel_id=1, source_target_pairs={{0,1},{1,0},{2,3},{3,2},{4,5},{5,4},{6,7},{7,6},{8,9},{9,8},{10,11... | collective-permute-start | bytes 4616 | tf_op jit(solution)/shard_map/ppermute | solution.py:334

commit v9 on v8

--- a/solution.py
+++ b/solution.py
@@ -230,6 +230,13 @@
 
     blocks = [block_of(ref, index, count) for ref in (straight_ref, diagonal_ref) for index in range(2)]
     prolong_rows(blocks, unit_ref[:rows, :], lax.axis_index("col"), slots, size, p_ref, 0, store)
+
+
+def rows_kernel(size, slots, straight_ref, diagonal_ref, own_ref, far_ref, far_partner_ref, unit_ref, pack_ref,
+                qh_ref, ql_ref, v_ref, term_ref, mine_h_ref, mine_l_ref, p_ref, mine_p_ref):
+    ready_kernel(size, slots, straight_ref, diagonal_ref, unit_ref, mine_h_ref, mine_l_ref, mine_p_ref)
+    own_kernel(size, own_ref, far_ref, far_partner_ref, unit_ref, pack_ref,
+               qh_ref, ql_ref, v_ref, term_ref, p_ref)
 
 
 def coarse_kernel(size, slots, ncol, nrow, targets, last_ref, diagonal_partner_ref, unit_ref, own_h_ref, own_l_ref, v_ref,
@@ -372,16 +379,13 @@
     far_partner = partner(far)
     diagonal_partner = partner(diagonal)
     last = partner(straight)
-    own_parts = call(
-        functools.partial(own_kernel, size),
+    made = call(
+        functools.partial(rows_kernel, size, slots),
         [array((rows, total, LANES), bf16)] * 2
-        + [array((rows, 2 * total, 2 * slots * size), bf16), array((rows, 2 * total, total), bf16)],
-        [VMEM] * 5, [scratch((rows * total // 2 + total, LANES), f32)],
-        own, far, far_partner, unit, packed)
-    ready = call(
-        functools.partial(ready_kernel, size, slots), [array((rows, total, LANES), bf16)] * 2,
-        [VMEM] * 3, [scratch((rows * total // 2 + total, LANES), f32)],
-        straight, diagonal, unit)
+        + [array((rows, 2 * total, 2 * slots * size), bf16), array((rows, 2 * total, total), bf16)]
+        + [array((rows, total, LANES), bf16)] * 2,
+        [VMEM] * 7, [scratch((rows * total // 2 + total, LANES), f32)] * 2,
+        straight, diagonal, own, far, far_partner, unit, packed)
     parts = call(
         functools.partial(coarse_kernel, size, slots, ncol, nrow),
         array((nrow * rows // 2, 2, LANES), f32), [SMEM] + [VMEM] * 12,
@@ -392,7 +396,7 @@
             scratch((rows, 2 * total, (slots + 1) * total), bf16),
             scratch((rows * total, 2 * LANES), bf16),
         ],
-        targets, last, diagonal_partner, unit, *own_parts, *ready, *hots)
+        targets, last, diagonal_partner, unit, *made, *hots)
     got = lax.all_to_all(parts, ("row", "col"), 0, 0, tiled=True)
     return call(
         functools.partial(sum_kernel, ncol, nrow), array((rows // ncol, LANES), f32), [VMEM], [], got)

time: 44.1 us -> 43.9 us (level)
    pallas_call x7 -> x6, Pallas kernels: 7.37 us -> 7.15 us  [call(): pl.pallas_call(kernel, out_shape=out_shape, in_specs=specs, out_specs=jax...]
  transfers between devices with their start and end apart: 11 -> 11, of which waited for: 6 -> 6; matrix products, arithmetic and copies ran while one was open for 2% -> 2% of each run, Pallas kernels for 9% -> 8%
where the time goes in v9:
time: 43.9 us; the launch traced here: 43.7 us
  waiting for transfers between devices  19.3 us (44%)
  blocking collectives  9.48 us (22%)
  Pallas kernels  7.15 us (16%)
  starting transfers between devices  6.85 us (16%)
  other arithmetic  0.77 us (2%)
    ppermute x11, waiting for transfers between devices, send(): return lax.ppermute(x, ('row', 'col'), pairs)  19.3 us
    all_to_all x1, blocking collectives, on_device(): got = lax.all_to_all(parts, ('row', 'col'), 0, 0, tiled=True)  9.48 us
    pallas_call x6, Pallas kernels, call(): pl.pallas_call(kernel, out_shape=out_shape, in_specs=specs, out_specs=jax...  7.15 us
    ppermute x11, starting transfers between devices, send(): return lax.ppermute(x, ('row', 'col'), pairs)  6.85 us
  transfers between devices with their start and end apart: 11, of which 6 were waited for; matrix products, arithmetic and copies ran while one was open for 2% of the time, Pallas kernels for 8%

profile of v9, /device:TPU:0, one launch (start us, length us, event | category | flops | bytes accessed | tf_op | source)
XLA Modules:
  0.0 43.7 jit_solution(3220977894674134163)
XLA Ops:
  0.0 0.0 copy-start.1
  0.0 0.0 copy-start.2
  0.0 3.0 %collective-permute-start = (f32[24,64]{1,0:T(8,128)}, f32[24,64]{1,0:T(8,128)S(1)}, u32[]{:S(2)}, u32[]{:S(2)}) collective-permute-start(f32[24,64]{1,0:T(8,128)} %own_ref.1), channel_id=1, source_target_pairs={{0,4},{1,29},{2,6},{3,31},{4,8},{5,1},{6,10},{7,3},{8,12},{9,5},{1... | collective-permute-start | bytes 18440 | tf_op jit(solution)/shard_map/ppermute | solution.py:341
  3.0 5.0 %collective-permute-done.mine_ref = f32[24,64]{1,0:T(8,128)S(1)} collective-permute-done((f32[24,64]{1,0:T(8,128)}, f32[24,64]{1,0:T(8,128)S(1)}, u32[]{:S(2)}, u32[]{:S(2)}) %collective-permute-start) | collective-permute-done | bytes 6176 | tf_op jit(solution)/shard_map/ppermute | solution.py:341
  8.0 0.0 collective-permute-start.1
  8.0 0.8 %fusion.4.targets = s32[4,24]{1,0:T(4,128)S(1)} fusion(s32[24,16]{0,1:T(8,128)} %param.6, s32[]{:T(128)S(6)} %select_n.37, s32[24]{0:T(128)S(1)} %iota_add_fusion, s32[24]{0:T(128)} %param.7, pred[]{:T(512)S(6)} %eq.5, s32[4]{0:T(128)S(1)} %iota_add_fusion.1), kind=kLoop, calls=%fused_computation.9 | loop fusion | flops 1824 | bytes 981 | tf_op jit(solution)/shard_map/jit(_where)/select_n | solution.py:82
  8.8 0.0 copy-start
  8.8 2.0 %shard_map.55.pack_ref = bf16[24,64,512]{2,1,0:T(8,128)(2,1)S(1)} custom-call(f32[24,4,64,64]{3,2,1,0:T(8,128)} %w_hbm.1), custom_call_target="tpu_custom_call" | custom-call | tf_op jit(solution)/shard_map/pallas_call | solution.py:329
  10.8 0.0 collective-permute-done.1.other_ref
  10.8 0.0 copy-done.1
  10.8 0.0 copy-done.2
  10.8 1.3 %shard_map.56 = (f32[64,128]{1,0:T(8,128)S(1)}, f32[80,128]{1,0:T(8,128)S(1)}) custom-call(s32[4,24]{1,0:T(4,128)S(1)} %fusion.4.targets, f32[24,64]{1,0:T(8,128)S(1)} %collective-permute-done.mine_ref, f32[24,64]{1,0:T(8,128)S(1)} %collective-permute-done.1.other_ref, f32[24,64]{1,0:T(8,128)S(1)} %copy-done.1, f32[24,64]{1,0:T(8,128)S(1)} %copy-done.2, ...), custom_call_target="tpu_custom_call" | custom-call | tf_op jit(solution)/shard_map/pallas_call | solution.py:329
  12.2 0.5 %collective-permute-start.2 = (f32[64,128]{1,0:T(8,128)S(1)}, f32[64,128]{1,0:T(8,128)S(1)}, u32[]{:S(2)}, u32[]{:S(2)}) collective-permute-start(f32[64,128]{1,0:T(8,128)S(1)} %get-tuple-element.16), channel_id=1, source_target_pairs={{0,1},{1,0},{2,3},{3,2},{4,5},{5,4},{6,7},{7,6},{8,9},{9,8},{10,11... | collective-permute-start | bytes 98312 | tf_op jit(solution)/shard_map/ppermute | solution.py:341
  12.7 0.9 %collective-permute-done.2 = f32[64,128]{1,0:T(8,128)S(1)} collective-permute-done((f32[64,128]{1,0:T(8,128)S(1)}, f32[64,128]{1,0:T(8,128)S(1)}, u32[]{:S(2)}, u32[]{:S(2)}) %collective-permute-start.2) | collective-permute-done | bytes 32800 | tf_op jit(solution)/shard_map/ppermute | solution.py:341
  13.6 0.0 collective-permute-start.3
  13.6 2.3 %collective-permute-start.5 = (f32[128,128]{1,0:T(8,128)S(1)}, f32[128,128]{1,0:T(8,128)S(1)}, u32[]{:S(2)}, u32[]{:S(2)}) collective-permute-start(f32[128,128]{1,0:T(8,128)S(1)} %constant_dynamic-update-slice_fusion.own_ref), channel_id=1, source_target_pairs={{0,6},{1,31},{2,4},{3,29},{4,10},{5,3},{6,8},{7,1},{8,14},{9,7},{1... | collective-permute-start | bytes 196616 | tf_op jit(solution)/shard_map/ppermute | solution.py:341
  15.8 0.5 %collective-permute-start.7 = (f32[64,128]{1,0:T(8,128)S(1)}, f32[64,128]{1,0:T(8,128)S(1)}, u32[]{:S(2)}, u32[]{:S(2)}) collective-permute-start(f32[64,128]{1,0:T(8,128)S(1)} %get-tuple-element.16), channel_id=1, source_target_pairs={{0,2},{1,3},{2,0},{3,1},{4,6},{5,7},{6,4},{7,5},{8,10},{9,11},{10,... | collective-permute-start | bytes 98312 | tf_op jit(solution)/shard_map/ppermute | solution.py:341
  16.4 4.6 %collective-permute-done.3.straight_ref = f32[128,128]{1,0:T(8,128)S(1)} collective-permute-done((f32[128,128]{1,0:T(8,128)S(1)}, f32[128,128]{1,0:T(8,128)S(1)}, u32[]{:S(2)}, u32[]{:S(2)}) %collective-permute-start.3) | collective-permute-done | bytes 65568 | tf_op jit(solution)/shard_map/ppermute | solution.py:341
  20.9 0.0 collective-permute-start.4
  20.9 1.4 %collective-permute-done.5.diagonal_ref = f32[128,128]{1,0:T(8,128)S(1)} collective-permute-done((f32[128,128]{1,0:T(8,128)S(1)}, f32[128,128]{1,0:T(8,128)S(1)}, u32[]{:S(2)}, u32[]{:S(2)}) %collective-permute-start.5) | collective-permute-done | bytes 65568 | tf_op jit(solution)/shard_map/ppermute | solution.py:341
  22.4 0.0 collective-permute-start.6
  22.4 0.0 collective-permute-done.7.far_ref
  22.4 0.5 %collective-permute-start.8 = (f32[64,128]{1,0:T(8,128)S(1)}, f32[64,128]{1,0:T(8,128)S(1)}, u32[]{:S(2)}, u32[]{:S(2)}) collective-permute-start(f32[64,128]{1,0:T(8,128)S(1)} %collective-permute-done.7.far_ref), channel_id=1, source_target_pairs={{0,1},{1,0},{2,3},{3,2},{4,5},{5,4},{6,7},{7,6},{8,9},{9,8},{10,11... | collective-permute-start | bytes 98312 | tf_op jit(solution)/shard_map/ppermute | solution.py:341
  22.9 0.0 copy-done
  22.9 0.0 collective-permute-start.9
  22.9 6.3 %collective-permute-done.9.mine_ref = s32[16,24]{1,0:T(8,128)S(1)} collective-permute-done((s32[16,24]{1,0:T(8,128)S(1)}, s32[16,24]{1,0:T(8,128)S(1)}, u32[]{:S(2)}, u32[]{:S(2)}) %collective-permute-start.9) | collective-permute-done | bytes 1568 | tf_op jit(solution)/shard_map/ppermute | solution.py:341
  29.2 0.0 collective-permute-start.10
  29.2 1.2 %collective-permute-done.10.other_ref = s32[16,24]{1,0:T(8,128)S(1)} collective-permute-done((s32[16,24]{1,0:T(8,128)S(1)}, s32[16,24]{1,0:T(8,128)S(1)}, u32[]{:S(2)}, u32[]{:S(2)}) %collective-permute-start.10) | collective-permute-done | bytes 1568 | tf_op jit(solution)/shard_map/ppermute | solution.py:341
  30.4 0.9 %shard_map.58 = (bf16[73,16,128]{2,1,0:T(8,128)(2,1)S(1)}, bf16[73,16,128]{2,1,0:T(8,128)(2,1)S(1)}, bf16[72,384]{1,0:T(8,128)(2,1)S(1)}) custom-call(s32[16,24]{1,0:T(8,128)S(1)} %collective-permute-done.9.mine_ref, s32[16,24]{1,0:T(8,128)S(1)} %collective-permute-done.10.other_ref, s32[16,24]{1,0:T(8,128)S(1)} %bitcast.10), custom_call_target="tpu_custom_call" | custom-call | tf_op jit(solution)/shard_map/pallas_call | solution.py:329
  31.3 0.0 collective-permute-done.8.far_partner_ref
  31.3 0.6 %shard_map.57 = (bf16[24,16,128]{2,1,0:T(8,128)(2,1)S(1)}, bf16[24,16,128]{2,1,0:T(8,128)(2,1)S(1)}, bf16[24,32,512]{2,1,0:T(8,128)(2,1)S(1)}, bf16[24,32,16]{2,...) custom-call(f32[128,128]{1,0:T(8,128)S(1)} %collective-permute-done.3.straight_ref, ...), custom_call_target="tpu_custom_call" | custom-call | tf_op jit(solution)/shard_map/pallas_call | solution.py:329
  31.9 0.0 collective-permute-done.4.last_ref
  31.9 0.0 collective-permute-done.6.diagonal_partner_ref
  32.0 1.7 %shard_map.59 = f32[96,2,128]{2,1,0:T(2,128)S(1)} custom-call(s32[4,24]{1,0:T(4,128)S(1)} %fusion.4.targets, f32[128,128]{1,0:T(8,128)S(1)} %collective-permute-done.4.last_ref, f32[128,128]{1,0:T(8,128)S(1)} %collective-permute-done.6.diagonal_partner_ref, f32[80,128]{1,0:T(8,128)S(1)} %get-tuple-element.17.unit_ref, ...), custom_call_target="tpu_custom_call" | custom-call | tf_op jit(solution)/shard_map/pallas_call | solution.py:329
  33.6 9.5 %all_to_all.5.got_ref = f32[96,2,128]{2,1,0:T(2,128)S(1)} all-to-all(f32[96,2,128]{2,1,0:T(2,128)S(1)} %shard_map.59), channel_id=1, replica_groups=mesh['row'=8,'col'=4] {'row','col'}, dimensions={0} | all-to-all | bytes 196608 | tf_op jit(solution)/shard_map/all_to_all | solution.py:400
  43.1 0.6 %shard_map.60 = f32[6,128]{1,0:T(8,128)} custom-call(f32[96,2,128]{2,1,0:T(2,128)S(1)} %all_to_all.5.got_ref), custom_call_target="tpu_custom_call" | custom-call | tf_op jit(solution)/shard_map/pallas_call | solution.py:329
  (4 shorter events, 0.0 us)
Async XLA Ops:
  0.0 10.8 %copy-start.1 = (f32[24,64]{1,0:T(8,128)S(1)}, f32[24,64]{1,0:T(8,128)}, u32[]{:S(2)}) copy-start(f32[24,64]{1,0:T(8,128)} %own_ref.1) | copy-start | bytes 18436
  0.0 10.8 %copy-start.2 = (f32[24,64]{1,0:T(8,128)S(1)}, f32[24,64]{1,0:T(8,128)}, u32[]{:S(2)}) copy-start(f32[24,64]{1,0:T(8,128)} %ridge_ref.1) | copy-start | bytes 18436
  0.0 8.0 %collective-permute-start = (f32[24,64]{1,0:T(8,128)}, f32[24,64]{1,0:T(8,128)S(1)}, u32[]{:S(2)}, u32[]{:S(2)}) collective-permute-start(f32[24,64]{1,0:T(8,128)} %own_ref.1), channel_id=1, source_target_pairs={{0,4},{1,29},{2,6},{3,31},{4,8},{5,1},{6,10},{7,3},{8,12},{9,5},{1... | collective-permute-start | bytes 18440 | tf_op jit(solution)/shard_map/ppermute | solution.py:341
  8.0 2.8 %collective-permute-start.1 = (f32[24,64]{1,0:T(8,128)S(1)}, f32[24,64]{1,0:T(8,128)S(1)}, u32[]{:S(2)}, u32[]{:S(2)}) collective-permute-start(f32[24,64]{1,0:T(8,128)S(1)} %collective-permute-done.mine_ref), channel_id=1, source_target_pairs={{0,1},{1,0},{2,3},{3,2},{4,5},{5,4},{6,7},{7,6},{8,9},{9,8},{10,11... | collective-permute-start | bytes 18440 | tf_op jit(solution)/shard_map/ppermute | solution.py:341
  8.8 14.1 %copy-start = (s32[24,16]{0,1:T(8,128)S(1)}, s32[24,16]{0,1:T(8,128)}, u32[]{:S(2)}) copy-start(s32[24,16]{0,1:T(8,128)} %param.6) | copy-start | bytes 4612
  12.2 1.4 %collective-permute-start.2 = (f32[64,128]{1,0:T(8,128)S(1)}, f32[64,128]{1,0:T(8,128)S(1)}, u32[]{:S(2)}, u32[]{:S(2)}) collective-permute-start(f32[64,128]{1,0:T(8,128)S(1)} %get-tuple-element.16), channel_id=1, source_target_pairs={{0,1},{1,0},{2,3},{3,2},{4,5},{5,4},{6,7},{7,6},{8,9},{9,8},{10,11... | collective-permute-start | bytes 98312 | tf_op jit(solution)/shard_map/ppermute | solution.py:341
  13.6 7.4 %collective-permute-start.3 = (f32[128,128]{1,0:T(8,128)S(1)}, f32[128,128]{1,0:T(8,128)S(1)}, u32[]{:S(2)}, u32[]{:S(2)}) collective-permute-start(f32[128,128]{1,0:T(8,128)S(1)} %constant_dynamic-update-slice_fusion.own_ref), channel_id=1, source_target_pairs={{0,4},{1,29},{2,6},{3,31},{4,8},{5,1},{6,10},{7,3},{8,12},{9,5},{1... | collective-permute-start | bytes 196616 | tf_op jit(solution)/shard_map/ppermute | solution.py:341
  13.6 8.8 %collective-permute-start.5 = (f32[128,128]{1,0:T(8,128)S(1)}, f32[128,128]{1,0:T(8,128)S(1)}, u32[]{:S(2)}, u32[]{:S(2)}) collective-permute-start(f32[128,128]{1,0:T(8,128)S(1)} %constant_dynamic-update-slice_fusion.own_ref), channel_id=1, source_target_pairs={{0,6},{1,31},{2,4},{3,29},{4,10},{5,3},{6,8},{7,1},{8,14},{9,7},{1... | collective-permute-start | bytes 196616 | tf_op jit(solution)/shard_map/ppermute | solution.py:341
  15.8 6.5 %collective-permute-start.7 = (f32[64,128]{1,0:T(8,128)S(1)}, f32[64,128]{1,0:T(8,128)S(1)}, u32[]{:S(2)}, u32[]{:S(2)}) collective-permute-start(f32[64,128]{1,0:T(8,128)S(1)} %get-tuple-element.16), channel_id=1, source_target_pairs={{0,2},{1,3},{2,0},{3,1},{4,6},{5,7},{6,4},{7,5},{8,10},{9,11},{10,... | collective-permute-start | bytes 98312 | tf_op jit(solution)/shard_map/ppermute | solution.py:341
  20.9 11.0 %collective-permute-start.4 = (f32[128,128]{1,0:T(8,128)S(1)}, f32[128,128]{1,0:T(8,128)S(1)}, u32[]{:S(2)}, u32[]{:S(2)}) collective-permute-start(f32[128,128]{1,0:T(8,128)S(1)} %collective-permute-done.3.straight_ref), channel_id=1, source_target_pairs={{0,1},{1,0},{2,3},{3,2},{4,5},{5,4},{6,7},{7,6},{8,9},{9,8},{10,11... | collective-permute-start | bytes 196616 | tf_op jit(solution)/shard_map/ppermute | solution.py:341
  22.4 9.6 %collective-permute-start.6 = (f32[128,128]{1,0:T(8,128)S(1)}, f32[128,128]{1,0:T(8,128)S(1)}, u32[]{:S(2)}, u32[]{:S(2)}) collective-permute-start(f32[128,128]{1,0:T(8,128)S(1)} %collective-permute-done.5.diagonal_ref), channel_id=1, source_target_pairs={{0,1},{1,0},{2,3},{3,2},{4,5},{5,4},{6,7},{7,6},{8,9},{9,8},{10,11... | collective-permute-start | bytes 196616 | tf_op jit(solution)/shard_map/ppermute | solution.py:341
  22.4 8.9 %collective-permute-start.8 = (f32[64,128]{1,0:T(8,128)S(1)}, f32[64,128]{1,0:T(8,128)S(1)}, u32[]{:S(2)}, u32[]{:S(2)}) collective-permute-start(f32[64,128]{1,0:T(8,128)S(1)} %collective-permute-done.7.far_ref), channel_id=1, source_target_pairs={{0,1},{1,0},{2,3},{3,2},{4,5},{5,4},{6,7},{7,6},{8,9},{9,8},{10,11... | collective-permute-start | bytes 98312 | tf_op jit(solution)/shard_map/ppermute | solution.py:341
  22.9 6.3 %collective-permute-start.9 = (s32[16,24]{1,0:T(8,128)S(1)}, s32[16,24]{1,0:T(8,128)S(1)}, u32[]{:S(2)}, u32[]{:S(2)}) collective-permute-start(s32[16,24]{1,0:T(8,128)S(1)} %bitcast.9), channel_id=1, source_target_pairs={{0,4},{1,29},{2,6},{3,31},{4,8},{5,1},{6,10},{7,3},{8,12},{9,5},{1... | collective-permute-start | bytes 4616 | tf_op jit(solution)/shard_map/ppermute | solution.py:341
  29.2 1.2 %collective-permute-start.10 = (s32[16,24]{1,0:T(8,128)S(1)}, s32[16,24]{1,0:T(8,128)S(1)}, u32[]{:S(2)}, u32[]{:S(2)}) collective-permute-start(s32[16,24]{1,0:T(8,128)S(1)} %collective-permute-done.9.mine_ref), channel_id=1, source_target_pairs={{0,1},{1,0},{2,3},{3,2},{4,5},{5,4},{6,7},{7,6},{8,9},{9,8},{10,11... | collective-permute-start | bytes 4616 | tf_op jit(solution)/shard_map/ppermute | solution.py:341
